TPU v7x, 32 devices: a whole 2x2x4 slice. The times are simulated.
32 devices in a mesh: row: 8 (over y, x, core), col: 4 (over z).
Axes of the slice: x: 2, y: 2, z: 4, core: 2. Of those that a mesh axis runs over, the one named last changes fastest.
Arguments:
- vector_panel: bfloat16 [8192, 256], P(('row', 'col')), may hold values from -6 to 6
- block_tiles: bfloat16 [3072, 128, 128], P(('row', 'col')), may hold values from -0.0625 to 0.0625
- tile_rows: int32 [3072], P(('row', 'col')), may hold values from 0 to 63, as said below
- tile_cols: int32 [3072], P(('row', 'col')), may hold values from 0 to 63, as said below
- owner_counts: int32 [32], P(('row', 'col')), may hold values from 1 to 96, as said below
Outputs:
- filtered: bfloat16 [8192, 256], P(('row', 'col'))
Inputs may be any that keep to these rules, and one draw needn't show every extreme that they name: The live slots of owner (row index p, col index q) hold distinct pairs (tile_rows, tile_cols) with tile_rows <= tile_cols, tile_rows in p * 2 * 4 to (p + 1) * 2 * 4 - 1 and tile_cols // 2 % 4 = q; slots past the owner's count repeat its first pair and are ignored. `tile_cols`: see tile_rows. `owner_counts`: some owner fills all 96 slots.
All inputs are finite; a program needn't handle non-finite values.
Results may differ from a plain program's by a relative error of at most 0.022.
Values may be sent and summed in bfloat16 or wider, within the bound.
No kernel may reach another device: no remote copies, remote signals or barrier semaphores. Data moves between devices by JAX's collectives and lax.ppermute only.
A program may use at most 128 MiB of HBM per device.

v0:
```python
import functools

import jax
import jax.numpy as jnp
from jax import lax
from jax.experimental import pallas as pl
from jax.experimental.pallas import tpu as pltpu
from jax.sharding import PartitionSpec as P


BS = 128
MIB = 2**20


center_shift = 0.25
half_width = 1.25


def power_of_two(n):
    return n & (n - 1) == 0


def densify_kernel(
    n_rows, n_cols, panel_blocks, rows_ref, cols_ref, count_ref, tiles_ref, a_ref, at_ref, table
):
    slots = tiles_ref.shape[0]
    range_blocks = panel_blocks * n_cols
    set_blocks = panel_blocks * n_rows
    p = lax.axis_index("row")
    q = lax.axis_index("col")

    def clear(i, carry):
        table[i] = slots
        return carry

    lax.fori_loop(0, range_blocks * set_blocks, clear, 0)

    def place(s, carry):
        row = rows_ref[s] - p * range_blocks
        row_at = ((row // panel_blocks) ^ q) * panel_blocks + row % panel_blocks
        col = cols_ref[s]
        relative = (col // (panel_blocks * n_cols)) ^ p
        unit = (relative % 2) * (n_rows // 2) + relative // 2
        col_at = unit * panel_blocks + col % panel_blocks
        table[row_at * set_blocks + col_at] = s
        return carry

    lax.fori_loop(0, jnp.minimum(count_ref[0], slots), place, 0)

    def fill(r, carry):
        for c in range(set_blocks):
            s = table[r * set_blocks + c]
            tile = tiles_ref[jnp.minimum(s, slots - 1)]
            tile = jnp.where(s < slots, tile, jnp.zeros_like(tile))
            a_ref[pl.ds(pl.multiple_of(r * BS, BS), BS), c * BS : (c + 1) * BS] = tile
            at_ref[c * BS : (c + 1) * BS, pl.ds(pl.multiple_of(r * BS, BS), BS)] = tile.T
        return carry

    lax.fori_loop(0, range_blocks, fill, 0)


def densify(n_rows, n_cols, panel_blocks, tile_rows, tile_cols, owner_counts, block_tiles):
    height = panel_blocks * n_cols * BS
    breadth = panel_blocks * n_rows * BS
    smem = pl.BlockSpec(memory_space=pltpu.SMEM)
    vmem = pl.BlockSpec(memory_space=pltpu.VMEM)
    return pl.pallas_call(
        functools.partial(densify_kernel, n_rows, n_cols, panel_blocks),
        out_shape=(
            jax.ShapeDtypeStruct((height, breadth), block_tiles.dtype),
            jax.ShapeDtypeStruct((breadth, height), block_tiles.dtype),
        ),
        in_specs=[smem, smem, smem, vmem],
        out_specs=(vmem, vmem),
        scratch_shapes=[pltpu.SMEM((height // BS * (breadth // BS),), jnp.int32)],
        compiler_params=pltpu.CompilerParams(vmem_limit_bytes=16 * MIB),
        cost_estimate=pl.CostEstimate(
            flops=0, transcendentals=0, bytes_accessed=2 * block_tiles.size + 4 * height * breadth
        ),
        name="densify",
    )(tile_rows, tile_cols, owner_counts, block_tiles)


def product_kernel(n_in, m_ref, *refs):
    panels, outs = refs[:n_in], refs[n_in:]
    done = 0
    for out in outs:
        for top in range(0, out.shape[0], 256):
            total = None
            at = 0
            for panel in panels:
                rows = panel.shape[0]
                term = jnp.dot(
                    m_ref[done : done + 256, at : at + rows],
                    panel[...],
                    preferred_element_type=jnp.float32,
                )
                total = term if total is None else total + term
                at += rows
            out[top : top + 256, :] = total.astype(out.dtype)
            done += 256


def product(matrix, panels, out_rows):
    width = panels[0].shape[1]
    vmem = pl.BlockSpec(memory_space=pltpu.VMEM)
    return pl.pallas_call(
        functools.partial(product_kernel, len(panels)),
        out_shape=tuple(jax.ShapeDtypeStruct((rows, width), jnp.bfloat16) for rows in out_rows),
        in_specs=[vmem] * (1 + len(panels)),
        out_specs=tuple(vmem for _ in out_rows),
        compiler_params=pltpu.CompilerParams(vmem_limit_bytes=16 * MIB),
        cost_estimate=pl.CostEstimate(
            flops=2 * matrix.size * width,
            transcendentals=0,
            bytes_accessed=2 * (matrix.size + sum(matrix.shape) * width),
        ),
    )(matrix, *panels)


def swap(x, axis, j):
    return lax.ppermute(x, axis, [(i, i ^ j) for i in range(lax.axis_size(axis))])


def apply_dense(panel, matrix, matrix_t):
    n_rows = lax.axis_size("row")
    n_cols = lax.axis_size("col")
    rows, width = panel.shape
    half = n_rows // 2
    range_panels = [panel] + [swap(panel, "col", j) for j in range(1, n_cols)]
    near = [panel] + [swap(panel, "row", 2 * k) for k in range(1, half)]
    far = swap(jnp.concatenate(near), "row", 1)
    upper = product(matrix, near + [far], [rows] * n_cols)
    own = upper[0].astype(jnp.float32)
    for j in range(1, n_cols):
        own += swap(upper[j], "col", j).astype(jnp.float32)
    keep, give = product(matrix_t, range_panels, [half * rows] * 2)
    paired = keep.astype(jnp.float32) + swap(give, "row", 1).astype(jnp.float32)
    paired = paired.reshape(half, rows, width)
    own += paired[0]
    for k in range(1, half):
        share = paired[k].astype(jnp.bfloat16)
        own += swap(share, "row", 2 * k).astype(jnp.float32)
    return own


def apply_slots(
    panel, block_tiles, row_slot, set_slot, row_select, set_select, range_blocks, set_blocks
):
    width = panel.shape[1]
    gathered_set = lax.all_gather(panel, "row", axis=0, tiled=True).reshape(set_blocks, BS, width)
    picked_set = jnp.take(gathered_set, set_slot, axis=0)
    upper = jnp.einsum("sij,sjw->siw", block_tiles, picked_set, preferred_element_type=jnp.float32)
    upper_sum = jnp.einsum(
        "as,siw->aiw", row_select, upper, precision=lax.Precision.HIGHEST
    ).astype(jnp.bfloat16)
    own_upper = lax.psum_scatter(
        upper_sum.reshape(range_blocks * BS, width), "col", scatter_dimension=0, tiled=True
    ).astype(jnp.float32)
    gathered_range = lax.all_gather(panel, "col", axis=0, tiled=True).reshape(
        range_blocks, BS, width
    )
    picked_range = jnp.take(gathered_range, row_slot, axis=0)
    lower = jnp.einsum(
        "sji,sjw->siw", block_tiles, picked_range, preferred_element_type=jnp.float32
    )
    lower_sum = jnp.einsum(
        "bs,siw->biw", set_select, lower, precision=lax.Precision.HIGHEST
    ).astype(jnp.bfloat16)
    own_lower = lax.psum_scatter(
        lower_sum.reshape(set_blocks * BS, width), "row", scatter_dimension=0, tiled=True
    ).astype(jnp.float32)
    return own_upper + own_lower


def slot_operator(panel_blocks, block_tiles, tile_rows, tile_cols, owner_counts):
    n_rows = lax.axis_size("row")
    n_cols = lax.axis_size("col")
    row_index = lax.axis_index("row")
    slots = block_tiles.shape[0]
    range_blocks = panel_blocks * n_cols
    set_blocks = panel_blocks * n_rows
    row_slot = tile_rows - row_index * range_blocks
    shard_of = tile_cols // panel_blocks
    set_slot = shard_of // n_cols * panel_blocks + tile_cols % panel_blocks
    live_slots = jnp.arange(slots, dtype=jnp.int32) < owner_counts[0]
    row_select = (
        (row_slot[None, :] == jnp.arange(range_blocks, dtype=jnp.int32)[:, None])
        & live_slots[None, :]
    ).astype(jnp.float32)
    set_select = (
        (set_slot[None, :] == jnp.arange(set_blocks, dtype=jnp.int32)[:, None])
        & live_slots[None, :]
    ).astype(jnp.float32)

    def operate(panel):
        return apply_slots(
            panel, block_tiles, row_slot, set_slot, row_select, set_select, range_blocks, set_blocks
        )

    return operate


def is_dense(n_rows, n_cols, panel_blocks, slots):
    return (
        power_of_two(n_rows)
        and power_of_two(n_cols)
        and n_rows >= 4
        and n_cols >= 2
        and panel_blocks % 2 == 0
        and panel_blocks * n_cols * panel_blocks * n_rows <= 2 * slots
    )


def per_device(vector_panel, block_tiles, tile_rows, tile_cols, owner_counts):
    n_rows = lax.axis_size("row")
    n_cols = lax.axis_size("col")
    panel_blocks = vector_panel.shape[0] // BS
    if is_dense(n_rows, n_cols, panel_blocks, block_tiles.shape[0]):
        matrix, matrix_t = densify(
            n_rows, n_cols, panel_blocks, tile_rows, tile_cols, owner_counts, block_tiles
        )
        operate = functools.partial(apply_dense, matrix=matrix, matrix_t=matrix_t)
    else:
        operate = slot_operator(panel_blocks, block_tiles, tile_rows, tile_cols, owner_counts)

    start_f = vector_panel.astype(jnp.float32)
    hx = operate(vector_panel)
    first_step = ((hx - center_shift * start_f) / half_width).astype(jnp.bfloat16)
    first_f = first_step.astype(jnp.float32)
    hfirst = operate(first_step)
    filtered = 2.0 * (hfirst - center_shift * first_f) / half_width - start_f
    return filtered.astype(jnp.bfloat16)


def solution(mesh):
    in_specs = (
        P(("row", "col"), None),
        P(("row", "col"), None, None),
        P(("row", "col")),
        P(("row", "col")),
        P(("row", "col")),
    )
    out_specs = P(("row", "col"), None)
    step = jax.shard_map(
        per_device, mesh=mesh, in_specs=in_specs, out_specs=out_specs, check_vma=False
    )

    def run(vector_panel, block_tiles, tile_rows, tile_cols, owner_counts):
        args = (vector_panel, block_tiles, tile_rows, tile_cols, owner_counts)
        return step(*args)

    return run
```

profile of v0, /device:TPU:0, one launch (start us, length us, event | category | flops | bytes accessed | tf_op | source)
XLA Modules:
  0.0 93.8 jit_solution(8064687786339046759)
XLA Ops:
  0.0 3.1 %collective-permute-start.7 = (bf16[256,256]{1,0:T(8,128)(2,1)}, bf16[256,256]{1,0:T(8,128)(2,1)S(1)}, u32[]{:S(2)}, u32[]{:S(2)}) collective-permute-start(bf16[256,256]{1,0:T(8,128)(2,1)} %refs_0_.3), channel_id=1, source_target_pairs={{0,1},{1,0},{2,3},{3,2},{4,5},{5,4},{6,7},{7,6},{8,9},{9,8},{10,11... | collective-permute-start | bytes 393224 | tf_op jit(solution)/shard_map/ppermute | solution.py:122
  3.1 2.6 %collective-permute-start.8 = (bf16[256,256]{1,0:T(8,128)(2,1)}, bf16[256,256]{1,0:T(8,128)(2,1)S(1)}, u32[]{:S(2)}, u32[]{:S(2)}) collective-permute-start(bf16[256,256]{1,0:T(8,128)(2,1)} %refs_0_.3), channel_id=1, source_target_pairs={{0,2},{1,3},{2,0},{3,1},{4,6},{5,7},{6,4},{7,5},{8,10},{9,11},{10,... | collective-permute-start | bytes 393224 | tf_op jit(solution)/shard_map/ppermute | solution.py:122
  6.3 1.9 %copy-done.1 = bf16[96,128,128]{2,1,0:T(8,128)(2,1)S(1)} copy-done((bf16[96,128,128]{2,1,0:T(8,128)(2,1)S(1)}, bf16[96,128,128]{2,1,0:T(8,128)(2,1)}, u32[]{:S(2)}) %copy-start.1) | copy-done | bytes 3145752
  8.2 0.7 copy-done.2
  8.8 0.7 copy-done.3
  9.5 6.1 %densify.1 = (bf16[1024,2048]{1,0:T(8,128)(2,1)S(1)}, bf16[2048,1024]{1,0:T(8,128)(2,1)S(1)}) custom-call(s32[96]{0:T(128)S(1)} %copy-done.2, s32[96]{0:T(128)S(1)} %copy-done.3, s32[1]{0:T(128)S(6)} %copy.6.count_ref, bf16[96,128,128]{2,1,0:T(8,128)(2,1)S(1)} %copy-done.1), custom_call_target="tpu_custom_call" | custom-call | bytes 11534336 | tf_op jit(solution)/shard_map/densify/pallas_call | solution.py:67
  15.6 0.0 collective-permute-done.7.refs_1_
  15.6 0.5 collective-permute-done.8.refs_2_
  16.2 0.9 copy-done
  17.1 1.3 %shard_map.56 = (bf16[1024,256]{1,0:T(8,128)(2,1)S(1)}, bf16[1024,256]{1,0:T(8,128)(2,1)S(1)}) custom-call(bf16[2048,1024]{1,0:T(8,128)(2,1)S(1)} %get-tuple-element.24.m_ref, bf16[256,256]{1,0:T(8,128)(2,1)S(1)} %copy-done, bf16[256,256]{1,0:T(8,128)(2,1)S(1)} %collective-permute-done.7.refs_1_, bf16[256,256]{1,0:T(8,128)(2,1)S(1)} %collective-permute-done.8.refs_2_, ...), custom_call_target="tpu_custom_call" | custom-call | flops 1073741824 | bytes 5767168 | tf_op jit(solution)/shard_map/pallas_call | solution.py:107
  18.3 0.1 collective-permute-start.10
  18.4 1.6 %collective-permute-start = (bf16[256,256]{1,0:T(8,128)(2,1)S(1)}, bf16[256,256]{1,0:T(8,128)(2,1)S(1)}, u32[]{:S(2)}, u32[]{:S(2)}) collective-permute-start(bf16[256,256]{1,0:T(8,128)(2,1)S(1)} %copy-done), channel_id=1, source_target_pairs={{0,8},{4,12},{8,0},{12,4},{16,24},{20,28},{24,16},{28,20},{1,9},{5... | collective-permute-start | bytes 393224 | tf_op jit(solution)/shard_map/ppermute | solution.py:122
  20.0 1.5 %collective-permute-start.1 = (bf16[256,256]{1,0:T(8,128)(2,1)S(1)}, bf16[256,256]{1,0:T(8,128)(2,1)S(1)}, u32[]{:S(2)}, u32[]{:S(2)}) collective-permute-start(bf16[256,256]{1,0:T(8,128)(2,1)S(1)} %copy-done), channel_id=1, source_target_pairs={{0,16},{4,20},{8,24},{12,28},{16,0},{20,4},{24,8},{28,12},{1,17},{... | collective-permute-start | bytes 393224 | tf_op jit(solution)/shard_map/ppermute | solution.py:122
  21.5 0.5 collective-permute-start.2
  22.0 2.8 %collective-permute-done.refs_1_ = bf16[256,256]{1,0:T(8,128)(2,1)S(1)} collective-permute-done((bf16[256,256]{1,0:T(8,128)(2,1)S(1)}, bf16[256,256]{1,0:T(8,128)(2,1)S(1)}, u32[]{:S(2)}, u32[]{:S(2)}) %collective-permute-start) | collective-permute-done | bytes 131104 | tf_op jit(solution)/shard_map/ppermute | solution.py:122
  24.7 3.6 %collective-permute-done.1.refs_2_ = bf16[256,256]{1,0:T(8,128)(2,1)S(1)} collective-permute-done((bf16[256,256]{1,0:T(8,128)(2,1)S(1)}, bf16[256,256]{1,0:T(8,128)(2,1)S(1)}, u32[]{:S(2)}, u32[]{:S(2)}) %collective-permute-start.1) | collective-permute-done | bytes 131104 | tf_op jit(solution)/shard_map/ppermute | solution.py:122
  28.3 0.0 collective-permute-done.2.refs_3_
  28.4 0.1 collective-permute-start.3
  28.5 0.1 fusion.12
  28.6 1.6 %collective-permute-start.13 = (bf16[256,256]{1,0:T(8,128)(2,1)S(1)}, bf16[256,256]{1,0:T(8,128)(2,1)S(1)}, u32[]{:S(2)}, u32[]{:S(2)}) collective-permute-start(bf16[256,256]{1,0:T(8,128)(2,1)S(1)} %get-tuple-element.41), channel_id=1, source_target_pairs={{0,24},{4,28},{8,16},{12,20},{16,8},{20,12},{24,0},{28,4},{1,25},{... | collective-permute-start | bytes 393224 | tf_op jit(solution)/shard_map/ppermute | solution.py:122
  30.2 1.2 %collective-permute-start.12 = (bf16[256,256]{1,0:T(8,128)(2,1)S(1)}, bf16[256,256]{1,0:T(8,128)(2,1)S(1)}, u32[]{:S(2)}, u32[]{:S(2)}) collective-permute-start(bf16[256,256]{1,0:T(8,128)(2,1)S(1)} %get-tuple-element.42), channel_id=1, source_target_pairs={{0,16},{4,20},{8,24},{12,28},{16,0},{20,4},{24,8},{28,12},{1,17},{... | collective-permute-start | bytes 393224 | tf_op jit(solution)/shard_map/ppermute | solution.py:122
  31.4 0.8 collective-permute-start.11
  32.2 1.3 %shard_map.55 = (bf16[256,256]{1,0:T(8,128)(2,1)S(1)}, bf16[256,256]{1,0:T(8,128)(2,1)S(1)}, bf16[256,256]{1,0:T(8,128)(2,1)S(1)}, bf16[256,256]{1,0:T(8,128)(2,1)S(1)}) custom-call(bf16[1024,2048]{1,0:T(8,128)(2,1)S(1)} %get-tuple-element.19.m_ref, bf16[256,256]{1,0:T(8,128)(2,1)S(1)} %copy-done, bf16[256,256]{1,0:T(8,128)(2,1)S(1)} %collective-permute-done.refs_1_, ...), custom_call_target="tpu_custom_call" | custom-call | flops 1073741824 | bytes 5767168 | tf_op jit(solution)/shard_map/pallas_call | solution.py:107
  33.5 2.5 %collective-permute-start.6 = (bf16[256,256]{1,0:T(8,128)(2,1)S(1)}, bf16[256,256]{1,0:T(8,128)(2,1)S(1)}, u32[]{:S(2)}, u32[]{:S(2)}) collective-permute-start(bf16[256,256]{1,0:T(8,128)(2,1)S(1)} %get-tuple-element.23), channel_id=1, source_target_pairs={{0,3},{1,2},{2,1},{3,0},{4,7},{5,6},{6,5},{7,4},{8,11},{9,10},{10,... | collective-permute-start | bytes 393224 | tf_op jit(solution)/shard_map/ppermute | solution.py:122
  36.0 1.0 %collective-permute-start.5 = (bf16[256,256]{1,0:T(8,128)(2,1)S(1)}, bf16[256,256]{1,0:T(8,128)(2,1)S(1)}, u32[]{:S(2)}, u32[]{:S(2)}) collective-permute-start(bf16[256,256]{1,0:T(8,128)(2,1)S(1)} %get-tuple-element.22), channel_id=1, source_target_pairs={{0,2},{1,3},{2,0},{3,1},{4,6},{5,7},{6,4},{7,5},{8,10},{9,11},{10,... | collective-permute-start | bytes 393224 | tf_op jit(solution)/shard_map/ppermute | solution.py:122
  37.0 0.0 collective-permute-done.13
  37.0 1.0 %collective-permute-start.4 = (bf16[256,256]{1,0:T(8,128)(2,1)S(1)}, bf16[256,256]{1,0:T(8,128)(2,1)S(1)}, u32[]{:S(2)}, u32[]{:S(2)}) collective-permute-start(bf16[256,256]{1,0:T(8,128)(2,1)S(1)} %get-tuple-element.21), channel_id=1, source_target_pairs={{0,1},{1,0},{2,3},{3,2},{4,5},{5,4},{6,7},{7,6},{8,9},{9,8},{10,11... | collective-permute-start | bytes 393224 | tf_op jit(solution)/shard_map/ppermute | solution.py:122
  38.0 0.3 collective-permute-done.12
  38.3 0.1 collective-permute-done.11
  38.4 3.1 %collective-permute-done.6 = bf16[256,256]{1,0:T(8,128)(2,1)S(1)} collective-permute-done((bf16[256,256]{1,0:T(8,128)(2,1)S(1)}, bf16[256,256]{1,0:T(8,128)(2,1)S(1)}, u32[]{:S(2)}, u32[]{:S(2)}) %collective-permute-start.6) | collective-permute-done | bytes 131104 | tf_op jit(solution)/shard_map/ppermute | solution.py:122
  41.5 7.0 %collective-permute-done.5 = bf16[256,256]{1,0:T(8,128)(2,1)S(1)} collective-permute-done((bf16[256,256]{1,0:T(8,128)(2,1)S(1)}, bf16[256,256]{1,0:T(8,128)(2,1)S(1)}, u32[]{:S(2)}, u32[]{:S(2)}) %collective-permute-start.5) | collective-permute-done | bytes 131104 | tf_op jit(solution)/shard_map/ppermute | solution.py:122
  48.5 0.0 collective-permute-done.4
  48.5 0.2 fusion.2.refs_0_
  48.7 0.1 collective-permute-start.21
  48.7 3.0 %collective-permute-start.22 = (bf16[256,256]{1,0:T(8,128)(2,1)S(1)}, bf16[256,256]{1,0:T(8,128)(2,1)S(1)}, u32[]{:S(2)}, u32[]{:S(2)}) collective-permute-start(bf16[256,256]{1,0:T(8,128)(2,1)S(1)} %fusion.2.refs_0_), channel_id=1, source_target_pairs={{0,2},{1,3},{2,0},{3,1},{4,6},{5,7},{6,4},{7,5},{8,10},{9,11},{10,... | collective-permute-start | bytes 393224 | tf_op jit(solution)/shard_map/ppermute | solution.py:122
  51.7 1.4 %collective-permute-start.23 = (bf16[256,256]{1,0:T(8,128)(2,1)S(1)}, bf16[256,256]{1,0:T(8,128)(2,1)S(1)}, u32[]{:S(2)}, u32[]{:S(2)}) collective-permute-start(bf16[256,256]{1,0:T(8,128)(2,1)S(1)} %fusion.2.refs_0_), channel_id=1, source_target_pairs={{0,3},{1,2},{2,1},{3,0},{4,7},{5,6},{6,5},{7,4},{8,11},{9,10},{10,... | collective-permute-start | bytes 393224 | tf_op jit(solution)/shard_map/ppermute | solution.py:122
  53.1 2.8 %collective-permute-done.21.refs_1_ = bf16[256,256]{1,0:T(8,128)(2,1)S(1)} collective-permute-done((bf16[256,256]{1,0:T(8,128)(2,1)S(1)}, bf16[256,256]{1,0:T(8,128)(2,1)S(1)}, u32[]{:S(2)}, u32[]{:S(2)}) %collective-permute-start.21) | collective-permute-done | bytes 131104 | tf_op jit(solution)/shard_map/ppermute | solution.py:122
  55.9 5.8 %collective-permute-done.22.refs_2_ = bf16[256,256]{1,0:T(8,128)(2,1)S(1)} collective-permute-done((bf16[256,256]{1,0:T(8,128)(2,1)S(1)}, bf16[256,256]{1,0:T(8,128)(2,1)S(1)}, u32[]{:S(2)}, u32[]{:S(2)}) %collective-permute-start.22) | collective-permute-done | bytes 131104 | tf_op jit(solution)/shard_map/ppermute | solution.py:122
  61.7 0.0 collective-permute-done.23.refs_3_
  61.7 1.2 %shard_map.58 = (bf16[1024,256]{1,0:T(8,128)(2,1)S(1)}, bf16[1024,256]{1,0:T(8,128)(2,1)S(1)}) custom-call(bf16[2048,1024]{1,0:T(8,128)(2,1)S(1)} %get-tuple-element.24.m_ref, bf16[256,256]{1,0:T(8,128)(2,1)S(1)} %fusion.2.refs_0_, bf16[256,256]{1,0:T(8,128)(2,1)S(1)} %collective-permute-done.21.refs_1_, ...), custom_call_target="tpu_custom_call" | custom-call | flops 1073741824 | bytes 5767168 | tf_op jit(solution)/shard_map/pallas_call | solution.py:107
  63.0 0.1 collective-permute-start.24
  63.0 1.2 %collective-permute-start.14 = (bf16[256,256]{1,0:T(8,128)(2,1)S(1)}, bf16[256,256]{1,0:T(8,128)(2,1)S(1)}, u32[]{:S(2)}, u32[]{:S(2)}) collective-permute-start(bf16[256,256]{1,0:T(8,128)(2,1)S(1)} %fusion.2.refs_0_), channel_id=1, source_target_pairs={{0,8},{4,12},{8,0},{12,4},{16,24},{20,28},{24,16},{28,20},{1,9},{5... | collective-permute-start | bytes 393224 | tf_op jit(solution)/shard_map/ppermute | solution.py:122
  64.2 0.9 collective-permute-start.15
  65.2 1.4 %collective-permute-start.16 = (bf16[256,256]{1,0:T(8,128)(2,1)S(1)}, bf16[256,256]{1,0:T(8,128)(2,1)S(1)}, u32[]{:S(2)}, u32[]{:S(2)}) collective-permute-start(bf16[256,256]{1,0:T(8,128)(2,1)S(1)} %fusion.2.refs_0_), channel_id=1, source_target_pairs={{0,24},{4,28},{8,16},{12,20},{16,8},{20,12},{24,0},{28,4},{1,25},{... | collective-permute-start | bytes 393224 | tf_op jit(solution)/shard_map/ppermute | solution.py:122
  66.6 2.9 %collective-permute-done.14.refs_1_ = bf16[256,256]{1,0:T(8,128)(2,1)S(1)} collective-permute-done((bf16[256,256]{1,0:T(8,128)(2,1)S(1)}, bf16[256,256]{1,0:T(8,128)(2,1)S(1)}, u32[]{:S(2)}, u32[]{:S(2)}) %collective-permute-start.14) | collective-permute-done | bytes 131104 | tf_op jit(solution)/shard_map/ppermute | solution.py:122
  69.5 1.6 %collective-permute-done.15.refs_2_ = bf16[256,256]{1,0:T(8,128)(2,1)S(1)} collective-permute-done((bf16[256,256]{1,0:T(8,128)(2,1)S(1)}, bf16[256,256]{1,0:T(8,128)(2,1)S(1)}, u32[]{:S(2)}, u32[]{:S(2)}) %collective-permute-start.15) | collective-permute-done | bytes 131104 | tf_op jit(solution)/shard_map/ppermute | solution.py:122
  71.1 1.6 %collective-permute-done.16.refs_3_ = bf16[256,256]{1,0:T(8,128)(2,1)S(1)} collective-permute-done((bf16[256,256]{1,0:T(8,128)(2,1)S(1)}, bf16[256,256]{1,0:T(8,128)(2,1)S(1)}, u32[]{:S(2)}, u32[]{:S(2)}) %collective-permute-start.16) | collective-permute-done | bytes 131104 | tf_op jit(solution)/shard_map/ppermute | solution.py:122
  72.7 0.1 collective-permute-start.17
  72.8 0.0 collective-permute-done.24
  72.8 0.1 fusion.13
  73.0 1.8 %collective-permute-start.27 = (bf16[256,256]{1,0:T(8,128)(2,1)S(1)}, bf16[256,256]{1,0:T(8,128)(2,1)S(1)}, u32[]{:S(2)}, u32[]{:S(2)}) collective-permute-start(bf16[256,256]{1,0:T(8,128)(2,1)S(1)} %get-tuple-element.38), channel_id=1, source_target_pairs={{0,24},{4,28},{8,16},{12,20},{16,8},{20,12},{24,0},{28,4},{1,25},{... | collective-permute-start | bytes 393224 | tf_op jit(solution)/shard_map/ppermute | solution.py:122
  74.8 0.5 collective-permute-start.26
  75.3 1.2 %collective-permute-start.25 = (bf16[256,256]{1,0:T(8,128)(2,1)S(1)}, bf16[256,256]{1,0:T(8,128)(2,1)S(1)}, u32[]{:S(2)}, u32[]{:S(2)}) collective-permute-start(bf16[256,256]{1,0:T(8,128)(2,1)S(1)} %get-tuple-element.37), channel_id=1, source_target_pairs={{0,8},{4,12},{8,0},{12,4},{16,24},{20,28},{24,16},{28,20},{1,9},{5... | collective-permute-start | bytes 393224 | tf_op jit(solution)/shard_map/ppermute | solution.py:122
  76.6 0.0 collective-permute-done.17.refs_4_
  76.6 1.3 %shard_map.57 = (bf16[256,256]{1,0:T(8,128)(2,1)S(1)}, bf16[256,256]{1,0:T(8,128)(2,1)S(1)}, bf16[256,256]{1,0:T(8,128)(2,1)S(1)}, bf16[256,256]{1,0:T(8,128)(2,1)S(1)}) custom-call(bf16[1024,2048]{1,0:T(8,128)(2,1)S(1)} %get-tuple-element.19.m_ref, bf16[256,256]{1,0:T(8,128)(2,1)S(1)} %fusion.2.refs_0_, ...), custom_call_target="tpu_custom_call" | custom-call | flops 1073741824 | bytes 5767168 | tf_op jit(solution)/shard_map/pallas_call | solution.py:107
  77.8 2.4 %collective-permute-start.20 = (bf16[256,256]{1,0:T(8,128)(2,1)S(1)}, bf16[256,256]{1,0:T(8,128)(2,1)S(1)}, u32[]{:S(2)}, u32[]{:S(2)}) collective-permute-start(bf16[256,256]{1,0:T(8,128)(2,1)S(1)} %get-tuple-element.30), channel_id=1, source_target_pairs={{0,3},{1,2},{2,1},{3,0},{4,7},{5,6},{6,5},{7,4},{8,11},{9,10},{10,... | collective-permute-start | bytes 393224 | tf_op jit(solution)/shard_map/ppermute | solution.py:122
  80.3 1.3 %collective-permute-start.19 = (bf16[256,256]{1,0:T(8,128)(2,1)S(1)}, bf16[256,256]{1,0:T(8,128)(2,1)S(1)}, u32[]{:S(2)}, u32[]{:S(2)}) collective-permute-start(bf16[256,256]{1,0:T(8,128)(2,1)S(1)} %get-tuple-element.29), channel_id=1, source_target_pairs={{0,2},{1,3},{2,0},{3,1},{4,6},{5,7},{6,4},{7,5},{8,10},{9,11},{10,... | collective-permute-start | bytes 393224 | tf_op jit(solution)/shard_map/ppermute | solution.py:122
  81.6 0.0 collective-permute-done.27
  81.6 1.0 %collective-permute-start.18 = (bf16[256,256]{1,0:T(8,128)(2,1)S(1)}, bf16[256,256]{1,0:T(8,128)(2,1)S(1)}, u32[]{:S(2)}, u32[]{:S(2)}) collective-permute-start(bf16[256,256]{1,0:T(8,128)(2,1)S(1)} %get-tuple-element.28), channel_id=1, source_target_pairs={{0,1},{1,0},{2,3},{3,2},{4,5},{5,4},{6,7},{7,6},{8,9},{9,8},{10,11... | collective-permute-start | bytes 393224 | tf_op jit(solution)/shard_map/ppermute | solution.py:122
  82.6 0.1 collective-permute-done.26
  82.7 3.1 %collective-permute-done.20 = bf16[256,256]{1,0:T(8,128)(2,1)S(1)} collective-permute-done((bf16[256,256]{1,0:T(8,128)(2,1)S(1)}, bf16[256,256]{1,0:T(8,128)(2,1)S(1)}, u32[]{:S(2)}, u32[]{:S(2)}) %collective-permute-start.20) | collective-permute-done | bytes 131104 | tf_op jit(solution)/shard_map/ppermute | solution.py:122
  85.7 7.3 %collective-permute-done.19 = bf16[256,256]{1,0:T(8,128)(2,1)S(1)} collective-permute-done((bf16[256,256]{1,0:T(8,128)(2,1)S(1)}, bf16[256,256]{1,0:T(8,128)(2,1)S(1)}, u32[]{:S(2)}, u32[]{:S(2)}) %collective-permute-start.19) | collective-permute-done | bytes 131104 | tf_op jit(solution)/shard_map/ppermute | solution.py:122
  93.0 0.0 collective-permute-done.18
  93.0 0.8 fusion.3
  (13 shorter events, 0.1 us)
Async XLA Ops:
  0.0 15.6 %collective-permute-start.7 = (bf16[256,256]{1,0:T(8,128)(2,1)}, bf16[256,256]{1,0:T(8,128)(2,1)S(1)}, u32[]{:S(2)}, u32[]{:S(2)}) collective-permute-start(bf16[256,256]{1,0:T(8,128)(2,1)} %refs_0_.3), channel_id=1, source_target_pairs={{0,1},{1,0},{2,3},{3,2},{4,5},{5,4},{6,7},{7,6},{8,9},{9,8},{10,11... | collective-permute-start | bytes 393224 | tf_op jit(solution)/shard_map/ppermute | solution.py:122
  3.1 13.1 %collective-permute-start.8 = (bf16[256,256]{1,0:T(8,128)(2,1)}, bf16[256,256]{1,0:T(8,128)(2,1)S(1)}, u32[]{:S(2)}, u32[]{:S(2)}) collective-permute-start(bf16[256,256]{1,0:T(8,128)(2,1)} %refs_0_.3), channel_id=1, source_target_pairs={{0,2},{1,3},{2,0},{3,1},{4,6},{5,7},{6,4},{7,5},{8,10},{9,11},{10,... | collective-permute-start | bytes 393224 | tf_op jit(solution)/shard_map/ppermute | solution.py:122
  5.6 10.5 %collective-permute-start.9 = (bf16[256,256]{1,0:T(8,128)(2,1)}, bf16[256,256]{1,0:T(8,128)(2,1)S(1)}, u32[]{:S(2)}, u32[]{:S(2)}) collective-permute-start(bf16[256,256]{1,0:T(8,128)(2,1)} %refs_0_.3), channel_id=1, source_target_pairs={{0,3},{1,2},{2,1},{3,0},{4,7},{5,6},{6,5},{7,4},{8,11},{9,10},{10,... | collective-permute-start | bytes 393224 | tf_op jit(solution)/shard_map/ppermute | solution.py:122
  6.3 1.9 %copy-start.1 = (bf16[96,128,128]{2,1,0:T(8,128)(2,1)S(1)}, bf16[96,128,128]{2,1,0:T(8,128)(2,1)}, u32[]{:S(2)}) copy-start(bf16[96,128,128]{2,1,0:T(8,128)(2,1)} %tiles_ref.1) | copy-start | bytes 9437188
  8.2 0.7 copy-start.2
  8.8 0.7 copy-start.3
  16.2 0.9 copy-start
  18.3 10.1 %collective-permute-start.10 = (bf16[1024,256]{1,0:T(8,128)(2,1)S(1)}, bf16[1024,256]{1,0:T(8,128)(2,1)S(1)}, u32[]{:S(2)}, u32[]{:S(2)}) collective-permute-start(bf16[1024,256]{1,0:T(8,128)(2,1)S(1)} %get-tuple-element.26), channel_id=1, source_target_pairs={{0,4},{4,0},{8,12},{12,8},{16,20},{20,16},{24,28},{28,24},{1,5},{5... | collective-permute-start | bytes 1572872 | tf_op jit(solution)/shard_map/ppermute | solution.py:122
  18.4 6.3 %collective-permute-start = (bf16[256,256]{1,0:T(8,128)(2,1)S(1)}, bf16[256,256]{1,0:T(8,128)(2,1)S(1)}, u32[]{:S(2)}, u32[]{:S(2)}) collective-permute-start(bf16[256,256]{1,0:T(8,128)(2,1)S(1)} %copy-done), channel_id=1, source_target_pairs={{0,8},{4,12},{8,0},{12,4},{16,24},{20,28},{24,16},{28,20},{1,9},{5... | collective-permute-start | bytes 393224 | tf_op jit(solution)/shard_map/ppermute | solution.py:122
  20.0 8.4 %collective-permute-start.1 = (bf16[256,256]{1,0:T(8,128)(2,1)S(1)}, bf16[256,256]{1,0:T(8,128)(2,1)S(1)}, u32[]{:S(2)}, u32[]{:S(2)}) collective-permute-start(bf16[256,256]{1,0:T(8,128)(2,1)S(1)} %copy-done), channel_id=1, source_target_pairs={{0,16},{4,20},{8,24},{12,28},{16,0},{20,4},{24,8},{28,12},{1,17},{... | collective-permute-start | bytes 393224 | tf_op jit(solution)/shard_map/ppermute | solution.py:122
  21.5 6.8 %collective-permute-start.2 = (bf16[256,256]{1,0:T(8,128)(2,1)S(1)}, bf16[256,256]{1,0:T(8,128)(2,1)S(1)}, u32[]{:S(2)}, u32[]{:S(2)}) collective-permute-start(bf16[256,256]{1,0:T(8,128)(2,1)S(1)} %copy-done), channel_id=1, source_target_pairs={{0,24},{4,28},{8,16},{12,20},{16,8},{20,12},{24,0},{28,4},{1,25},{... | collective-permute-start | bytes 393224 | tf_op jit(solution)/shard_map/ppermute | solution.py:122
  28.4 3.8 %collective-permute-start.3 = (bf16[1024,256]{1,0:T(8,128)(2,1)S(1)}, bf16[1024,256]{1,0:T(8,128)(2,1)S(1)}, u32[]{:S(2)}, u32[]{:S(2)}) collective-permute-start(bf16[1024,256]{1,0:T(8,128)(2,1)S(1)} %pad_maximum_fusion), channel_id=1, source_target_pairs={{0,4},{4,0},{8,12},{12,8},{16,20},{20,16},{24,28},{28,24},{1,5},{5... | collective-permute-start | bytes 1572872 | tf_op jit(solution)/shard_map/ppermute | solution.py:122
  28.6 8.4 %collective-permute-start.13 = (bf16[256,256]{1,0:T(8,128)(2,1)S(1)}, bf16[256,256]{1,0:T(8,128)(2,1)S(1)}, u32[]{:S(2)}, u32[]{:S(2)}) collective-permute-start(bf16[256,256]{1,0:T(8,128)(2,1)S(1)} %get-tuple-element.41), channel_id=1, source_target_pairs={{0,24},{4,28},{8,16},{12,20},{16,8},{20,12},{24,0},{28,4},{1,25},{... | collective-permute-start | bytes 393224 | tf_op jit(solution)/shard_map/ppermute | solution.py:122
  30.2 8.1 %collective-permute-start.12 = (bf16[256,256]{1,0:T(8,128)(2,1)S(1)}, bf16[256,256]{1,0:T(8,128)(2,1)S(1)}, u32[]{:S(2)}, u32[]{:S(2)}) collective-permute-start(bf16[256,256]{1,0:T(8,128)(2,1)S(1)} %get-tuple-element.42), channel_id=1, source_target_pairs={{0,16},{4,20},{8,24},{12,28},{16,0},{20,4},{24,8},{28,12},{1,17},{... | collective-permute-start | bytes 393224 | tf_op jit(solution)/shard_map/ppermute | solution.py:122
  31.4 7.0 %collective-permute-start.11 = (bf16[256,256]{1,0:T(8,128)(2,1)S(1)}, bf16[256,256]{1,0:T(8,128)(2,1)S(1)}, u32[]{:S(2)}, u32[]{:S(2)}) collective-permute-start(bf16[256,256]{1,0:T(8,128)(2,1)S(1)} %get-tuple-element.40), channel_id=1, source_target_pairs={{0,8},{4,12},{8,0},{12,4},{16,24},{20,28},{24,16},{28,20},{1,9},{5... | collective-permute-start | bytes 393224 | tf_op jit(solution)/shard_map/ppermute | solution.py:122
  33.5 8.0 %collective-permute-start.6 = (bf16[256,256]{1,0:T(8,128)(2,1)S(1)}, bf16[256,256]{1,0:T(8,128)(2,1)S(1)}, u32[]{:S(2)}, u32[]{:S(2)}) collective-permute-start(bf16[256,256]{1,0:T(8,128)(2,1)S(1)} %get-tuple-element.23), channel_id=1, source_target_pairs={{0,3},{1,2},{2,1},{3,0},{4,7},{5,6},{6,5},{7,4},{8,11},{9,10},{10,... | collective-permute-start | bytes 393224 | tf_op jit(solution)/shard_map/ppermute | solution.py:122
  36.0 12.5 %collective-permute-start.5 = (bf16[256,256]{1,0:T(8,128)(2,1)S(1)}, bf16[256,256]{1,0:T(8,128)(2,1)S(1)}, u32[]{:S(2)}, u32[]{:S(2)}) collective-permute-start(bf16[256,256]{1,0:T(8,128)(2,1)S(1)} %get-tuple-element.22), channel_id=1, source_target_pairs={{0,2},{1,3},{2,0},{3,1},{4,6},{5,7},{6,4},{7,5},{8,10},{9,11},{10,... | collective-permute-start | bytes 393224 | tf_op jit(solution)/shard_map/ppermute | solution.py:122
  37.0 11.5 %collective-permute-start.4 = (bf16[256,256]{1,0:T(8,128)(2,1)S(1)}, bf16[256,256]{1,0:T(8,128)(2,1)S(1)}, u32[]{:S(2)}, u32[]{:S(2)}) collective-permute-start(bf16[256,256]{1,0:T(8,128)(2,1)S(1)} %get-tuple-element.21), channel_id=1, source_target_pairs={{0,1},{1,0},{2,3},{3,2},{4,5},{5,4},{6,7},{7,6},{8,9},{9,8},{10,11... | collective-permute-start | bytes 393224 | tf_op jit(solution)/shard_map/ppermute | solution.py:122
  48.7 7.2 %collective-permute-start.21 = (bf16[256,256]{1,0:T(8,128)(2,1)S(1)}, bf16[256,256]{1,0:T(8,128)(2,1)S(1)}, u32[]{:S(2)}, u32[]{:S(2)}) collective-permute-start(bf16[256,256]{1,0:T(8,128)(2,1)S(1)} %fusion.2.refs_0_), channel_id=1, source_target_pairs={{0,1},{1,0},{2,3},{3,2},{4,5},{5,4},{6,7},{7,6},{8,9},{9,8},{10,11... | collective-permute-start | bytes 393224 | tf_op jit(solution)/shard_map/ppermute | solution.py:122
  48.7 13.0 %collective-permute-start.22 = (bf16[256,256]{1,0:T(8,128)(2,1)S(1)}, bf16[256,256]{1,0:T(8,128)(2,1)S(1)}, u32[]{:S(2)}, u32[]{:S(2)}) collective-permute-start(bf16[256,256]{1,0:T(8,128)(2,1)S(1)} %fusion.2.refs_0_), channel_id=1, source_target_pairs={{0,2},{1,3},{2,0},{3,1},{4,6},{5,7},{6,4},{7,5},{8,10},{9,11},{10,... | collective-permute-start | bytes 393224 | tf_op jit(solution)/shard_map/ppermute | solution.py:122
  51.7 10.0 %collective-permute-start.23 = (bf16[256,256]{1,0:T(8,128)(2,1)S(1)}, bf16[256,256]{1,0:T(8,128)(2,1)S(1)}, u32[]{:S(2)}, u32[]{:S(2)}) collective-permute-start(bf16[256,256]{1,0:T(8,128)(2,1)S(1)} %fusion.2.refs_0_), channel_id=1, source_target_pairs={{0,3},{1,2},{2,1},{3,0},{4,7},{5,6},{6,5},{7,4},{8,11},{9,10},{10,... | collective-permute-start | bytes 393224 | tf_op jit(solution)/shard_map/ppermute | solution.py:122
  63.0 9.9 %collective-permute-start.24 = (bf16[1024,256]{1,0:T(8,128)(2,1)S(1)}, bf16[1024,256]{1,0:T(8,128)(2,1)S(1)}, u32[]{:S(2)}, u32[]{:S(2)}) collective-permute-start(bf16[1024,256]{1,0:T(8,128)(2,1)S(1)} %get-tuple-element.32), channel_id=1, source_target_pairs={{0,4},{4,0},{8,12},{12,8},{16,20},{20,16},{24,28},{28,24},{1,5},{5... | collective-permute-start | bytes 1572872 | tf_op jit(solution)/shard_map/ppermute | solution.py:122
  63.0 6.4 %collective-permute-start.14 = (bf16[256,256]{1,0:T(8,128)(2,1)S(1)}, bf16[256,256]{1,0:T(8,128)(2,1)S(1)}, u32[]{:S(2)}, u32[]{:S(2)}) collective-permute-start(bf16[256,256]{1,0:T(8,128)(2,1)S(1)} %fusion.2.refs_0_), channel_id=1, source_target_pairs={{0,8},{4,12},{8,0},{12,4},{16,24},{20,28},{24,16},{28,20},{1,9},{5... | collective-permute-start | bytes 393224 | tf_op jit(solution)/shard_map/ppermute | solution.py:122
  64.2 6.8 %collective-permute-start.15 = (bf16[256,256]{1,0:T(8,128)(2,1)S(1)}, bf16[256,256]{1,0:T(8,128)(2,1)S(1)}, u32[]{:S(2)}, u32[]{:S(2)}) collective-permute-start(bf16[256,256]{1,0:T(8,128)(2,1)S(1)} %fusion.2.refs_0_), channel_id=1, source_target_pairs={{0,16},{4,20},{8,24},{12,28},{16,0},{20,4},{24,8},{28,12},{1,17},{... | collective-permute-start | bytes 393224 | tf_op jit(solution)/shard_map/ppermute | solution.py:122
  65.2 7.5 %collective-permute-start.16 = (bf16[256,256]{1,0:T(8,128)(2,1)S(1)}, bf16[256,256]{1,0:T(8,128)(2,1)S(1)}, u32[]{:S(2)}, u32[]{:S(2)}) collective-permute-start(bf16[256,256]{1,0:T(8,128)(2,1)S(1)} %fusion.2.refs_0_), channel_id=1, source_target_pairs={{0,24},{4,28},{8,16},{12,20},{16,8},{20,12},{24,0},{28,4},{1,25},{... | collective-permute-start | bytes 393224 | tf_op jit(solution)/shard_map/ppermute | solution.py:122
  72.7 3.8 %collective-permute-start.17 = (bf16[1024,256]{1,0:T(8,128)(2,1)S(1)}, bf16[1024,256]{1,0:T(8,128)(2,1)S(1)}, u32[]{:S(2)}, u32[]{:S(2)}) collective-permute-start(bf16[1024,256]{1,0:T(8,128)(2,1)S(1)} %pad_maximum_fusion.1), channel_id=1, source_target_pairs={{0,4},{4,0},{8,12},{12,8},{16,20},{20,16},{24,28},{28,24},{1,5},{5... | collective-permute-start | bytes 1572872 | tf_op jit(solution)/shard_map/ppermute | solution.py:122
  73.0 8.6 %collective-permute-start.27 = (bf16[256,256]{1,0:T(8,128)(2,1)S(1)}, bf16[256,256]{1,0:T(8,128)(2,1)S(1)}, u32[]{:S(2)}, u32[]{:S(2)}) collective-permute-start(bf16[256,256]{1,0:T(8,128)(2,1)S(1)} %get-tuple-element.38), channel_id=1, source_target_pairs={{0,24},{4,28},{8,16},{12,20},{16,8},{20,12},{24,0},{28,4},{1,25},{... | collective-permute-start | bytes 393224 | tf_op jit(solution)/shard_map/ppermute | solution.py:122
  74.8 7.8 %collective-permute-start.26 = (bf16[256,256]{1,0:T(8,128)(2,1)S(1)}, bf16[256,256]{1,0:T(8,128)(2,1)S(1)}, u32[]{:S(2)}, u32[]{:S(2)}) collective-permute-start(bf16[256,256]{1,0:T(8,128)(2,1)S(1)} %get-tuple-element.39), channel_id=1, source_target_pairs={{0,16},{4,20},{8,24},{12,28},{16,0},{20,4},{24,8},{28,12},{1,17},{... | collective-permute-start | bytes 393224 | tf_op jit(solution)/shard_map/ppermute | solution.py:122
  75.3 7.3 %collective-permute-start.25 = (bf16[256,256]{1,0:T(8,128)(2,1)S(1)}, bf16[256,256]{1,0:T(8,128)(2,1)S(1)}, u32[]{:S(2)}, u32[]{:S(2)}) collective-permute-start(bf16[256,256]{1,0:T(8,128)(2,1)S(1)} %get-tuple-element.37), channel_id=1, source_target_pairs={{0,8},{4,12},{8,0},{12,4},{16,24},{20,28},{24,16},{28,20},{1,9},{5... | collective-permute-start | bytes 393224 | tf_op jit(solution)/shard_map/ppermute | solution.py:122
  77.8 7.9 %collective-permute-start.20 = (bf16[256,256]{1,0:T(8,128)(2,1)S(1)}, bf16[256,256]{1,0:T(8,128)(2,1)S(1)}, u32[]{:S(2)}, u32[]{:S(2)}) collective-permute-start(bf16[256,256]{1,0:T(8,128)(2,1)S(1)} %get-tuple-element.30), channel_id=1, source_target_pairs={{0,3},{1,2},{2,1},{3,0},{4,7},{5,6},{6,5},{7,4},{8,11},{9,10},{10,... | collective-permute-start | bytes 393224 | tf_op jit(solution)/shard_map/ppermute | solution.py:122
  80.3 12.7 %collective-permute-start.19 = (bf16[256,256]{1,0:T(8,128)(2,1)S(1)}, bf16[256,256]{1,0:T(8,128)(2,1)S(1)}, u32[]{:S(2)}, u32[]{:S(2)}) collective-permute-start(bf16[256,256]{1,0:T(8,128)(2,1)S(1)} %get-tuple-element.29), channel_id=1, source_target_pairs={{0,2},{1,3},{2,0},{3,1},{4,6},{5,7},{6,4},{7,5},{8,10},{9,11},{10,... | collective-permute-start | bytes 393224 | tf_op jit(solution)/shard_map/ppermute | solution.py:122
  81.6 11.4 %collective-permute-start.18 = (bf16[256,256]{1,0:T(8,128)(2,1)S(1)}, bf16[256,256]{1,0:T(8,128)(2,1)S(1)}, u32[]{:S(2)}, u32[]{:S(2)}) collective-permute-start(bf16[256,256]{1,0:T(8,128)(2,1)S(1)} %get-tuple-element.28), channel_id=1, source_target_pairs={{0,1},{1,0},{2,3},{3,2},{4,5},{5,4},{6,7},{7,6},{8,9},{9,8},{10,11... | collective-permute-start | bytes 393224 | tf_op jit(solution)/shard_map/ppermute | solution.py:122
where the time goes:
time: 94 us; the launch traced here: 93.8 us
  waiting for transfers between devices  42.5 us (45%)
  starting transfers between devices  33.8 us (36%)
  Pallas kernels  11.2 us (12%)
  local copies, waits for them, and re-layouts  4.15 us (4%)
  other arithmetic  1.32 us (1%)
    ppermute x28, waiting for transfers between devices, swap(): lax.ppermute(x, axis, [(i, i ^ j) for i in range(lax.axis_size(axis))])  42.5 us
    ppermute x28, starting transfers between devices, swap(): lax.ppermute(x, axis, [(i, i ^ j) for i in range(lax.axis_size(axis))])  33.8 us
    pallas_call x1, Pallas kernels, densify(): pl.pallas_call(functools.partial(densify_kernel, n_rows, n_cols, panel_bl...  6.09 us
    pallas_call x4, Pallas kernels, product(): pl.pallas_call(functools.partial(product_kernel, len(panels)), out_shape=...  5.08 us
    unnamed x8, local copies, waits for them, and re-layouts  4.1 us
  transfers between devices with their start and end apart: 28, of which 15 were waited for; matrix products, arithmetic and copies ran while one was open for 0% of the time, Pallas kernels for 9%

commit v1 on v0

--- a/solution.py
+++ b/solution.py
@@ -21,19 +21,49 @@
 
 
 def densify_kernel(
-    n_rows, n_cols, panel_blocks, rows_ref, cols_ref, count_ref, tiles_ref, a_ref, at_ref, table
+    n_rows,
+    n_cols,
+    panel_blocks,
+    rows_hbm,
+    cols_hbm,
+    count_hbm,
+    tiles_hbm,
+    a_ref,
+    at_ref,
+    rows_ref,
+    cols_ref,
+    count_ref,
+    tiles_ref,
+    table,
+    sems,
 ):
     slots = tiles_ref.shape[0]
     range_blocks = panel_blocks * n_cols
     set_blocks = panel_blocks * n_rows
     p = lax.axis_index("row")
     q = lax.axis_index("col")
-
-    def clear(i, carry):
-        table[i] = slots
+    moves = [
+        pltpu.make_async_copy(src, dst, sems.at[i])
+        for i, (src, dst) in enumerate(
+            (
+                (rows_hbm, rows_ref),
+                (cols_hbm, cols_ref),
+                (count_hbm, count_ref),
+                (tiles_hbm, tiles_ref),
+            )
+        )
+    ]
+    for move in moves:
+        move.start()
+
+    def clear(r, carry):
+        for c in range(set_blocks):
+            table[r * set_blocks + c] = slots
         return carry
 
-    lax.fori_loop(0, range_blocks * set_blocks, clear, 0)
+    lax.fori_loop(0, range_blocks, clear, 0)
+    for move in moves[:3]:
+        move.wait()
 
     def place(s, carry):
         row = rows_ref[s] - p * range_blocks
@@ -46,6 +76,7 @@
         return carry
 
     lax.fori_loop(0, jnp.minimum(count_ref[0], slots), place, 0)
+    moves[3].wait()
 
     def fill(r, carry):
         for c in range(set_blocks):
@@ -62,7 +93,7 @@
 def densify(n_rows, n_cols, panel_blocks, tile_rows, tile_cols, owner_counts, block_tiles):
     height = panel_blocks * n_cols * BS
     breadth = panel_blocks * n_rows * BS
-    smem = pl.BlockSpec(memory_space=pltpu.SMEM)
+    hbm = pl.BlockSpec(memory_space=pltpu.HBM)
     vmem = pl.BlockSpec(memory_space=pltpu.VMEM)
     return pl.pallas_call(
         functools.partial(densify_kernel, n_rows, n_cols, panel_blocks),
@@ -70,10 +101,17 @@
             jax.ShapeDtypeStruct((height, breadth), block_tiles.dtype),
             jax.ShapeDtypeStruct((breadth, height), block_tiles.dtype),
         ),
-        in_specs=[smem, smem, smem, vmem],
+        in_specs=[hbm] * 4,
         out_specs=(vmem, vmem),
-        scratch_shapes=[pltpu.SMEM((height // BS * (breadth // BS),), jnp.int32)],
-        compiler_params=pltpu.CompilerParams(vmem_limit_bytes=16 * MIB),
+        scratch_shapes=[
+            pltpu.SMEM(tile_rows.shape, jnp.int32),
+            pltpu.SMEM(tile_cols.shape, jnp.int32),
+            pltpu.SMEM(owner_counts.shape, jnp.int32),
+            pltpu.VMEM(block_tiles.shape, block_tiles.dtype),
+            pltpu.SMEM((height // BS * (breadth // BS),), jnp.int32),
+            pltpu.SemaphoreType.DMA((4,)),
+        ],
+        compiler_params=pltpu.CompilerParams(vmem_limit_bytes=20 * MIB),
         cost_estimate=pl.CostEstimate(
             flops=0, transcendentals=0, bytes_accessed=2 * block_tiles.size + 4 * height * breadth
         ),
@@ -81,9 +119,9 @@
     )(tile_rows, tile_cols, owner_counts, block_tiles)
 
 
-def product_kernel(n_in, m_ref, *refs):
+def product_kernel(n_in, start, m_ref, *refs):
     panels, outs = refs[:n_in], refs[n_in:]
-    done = 0
+    done = start
     for out in outs:
         for top in range(0, out.shape[0], 256):
             total = None
@@ -101,19 +139,19 @@
             done += 256
 
 
-def product(matrix, panels, out_rows):
+def product(matrix, panels, start, out_rows):
     width = panels[0].shape[1]
     vmem = pl.BlockSpec(memory_space=pltpu.VMEM)
     return pl.pallas_call(
-        functools.partial(product_kernel, len(panels)),
+        functools.partial(product_kernel, len(panels), start),
         out_shape=tuple(jax.ShapeDtypeStruct((rows, width), jnp.bfloat16) for rows in out_rows),
         in_specs=[vmem] * (1 + len(panels)),
         out_specs=tuple(vmem for _ in out_rows),
         compiler_params=pltpu.CompilerParams(vmem_limit_bytes=16 * MIB),
         cost_estimate=pl.CostEstimate(
-            flops=2 * matrix.size * width,
+            flops=2 * sum(out_rows) * matrix.shape[1] * width,
             transcendentals=0,
-            bytes_accessed=2 * (matrix.size + sum(matrix.shape) * width),
+            bytes_accessed=2 * (sum(out_rows) * (matrix.shape[1] + width) + matrix.shape[1] * width),
         ),
     )(matrix, *panels)
 
@@ -130,11 +168,12 @@
     range_panels = [panel] + [swap(panel, "col", j) for j in range(1, n_cols)]
     near = [panel] + [swap(panel, "row", 2 * k) for k in range(1, half)]
     far = swap(jnp.concatenate(near), "row", 1)
-    upper = product(matrix, near + [far], [rows] * n_cols)
+    upper = product(matrix, near + [far], 0, [rows] * n_cols)
     own = upper[0].astype(jnp.float32)
     for j in range(1, n_cols):
         own += swap(upper[j], "col", j).astype(jnp.float32)
-    keep, give = product(matrix_t, range_panels, [half * rows] * 2)
+    (give,) = product(matrix_t, range_panels, half * rows, [half * rows])
+    (keep,) = product(matrix_t, range_panels, 0, [half * rows])
     paired = keep.astype(jnp.float32) + swap(give, "row", 1).astype(jnp.float32)
     paired = paired.reshape(half, rows, width)
     own += paired[0]

time: 94 us -> 83.7 us (0.89)
  waiting for transfers between devices: 42.5 us -> 33.8 us
  starting transfers between devices: 33.8 us -> 32.7 us
  other arithmetic: 1.32 us -> 2.29 us
    ppermute x28, waiting for transfers between devices: 42.5 us -> 33.8 us  [swap(): lax.ppermute(x, axis, [(i, i ^ j) for i in range(lax.axis_size(axis))])]
    ppermute x28, starting transfers between devices: 33.8 us -> 32.7 us  [swap(): lax.ppermute(x, axis, [(i, i ^ j) for i in range(lax.axis_size(axis))])]
    pallas_call x4 -> x6, Pallas kernels: 5.08 us -> 5.37 us  [product(): pl.pallas_call(functools.partial(product_kernel, len(panels), start), out...]
  transfers between devices with their start and end apart: 28 -> 28, of which waited for: 15 -> 12; matrix products, arithmetic and copies ran while one was open for 0% -> 2% of each run, Pallas kernels for 9% -> 12%
where the time goes in v1:
time: 83.7 us; the launch traced here: 83.5 us
  waiting for transfers between devices  33.8 us (40%)
  starting transfers between devices  32.7 us (39%)
  Pallas kernels  10.7 us (13%)
  local copies, waits for them, and re-layouts  3.25 us (4%)
  other arithmetic  2.29 us (3%)
  between operations  0.87 us (1%)
    ppermute x28, waiting for transfers between devices, swap(): lax.ppermute(x, axis, [(i, i ^ j) for i in range(lax.axis_size(axis))])  33.8 us
    ppermute x28, starting transfers between devices, swap(): lax.ppermute(x, axis, [(i, i ^ j) for i in range(lax.axis_size(axis))])  32.7 us
    pallas_call x6, Pallas kernels, product(): pl.pallas_call(functools.partial(product_kernel, len(panels), start), out...  5.37 us
    pallas_call x1, Pallas kernels, densify(): pl.pallas_call(functools.partial(densify_kernel, n_rows, n_cols, panel_bl...  5.29 us
    unnamed x8, local copies, waits for them, and re-layouts  3.2 us
  transfers between devices with their start and end apart: 28, of which 12 were waited for; matrix products, arithmetic and copies ran while one was open for 2% of the time, Pallas kernels for 12%

profile of v1, /device:TPU:0, one launch (start us, length us, event | category | flops | bytes accessed | tf_op | source)
XLA Modules:
  0.0 83.5 jit_solution(15804247899715815249)
XLA Ops:
  0.0 3.9 %collective-permute-start.2 = (bf16[256,256]{1,0:T(8,128)(2,1)}, bf16[256,256]{1,0:T(8,128)(2,1)S(1)}, u32[]{:S(2)}, u32[]{:S(2)}) collective-permute-start(bf16[256,256]{1,0:T(8,128)(2,1)} %refs_0_.5), channel_id=1, source_target_pairs={{0,24},{4,28},{8,16},{12,20},{16,8},{20,12},{24,0},{28,4},{1,25},{... | collective-permute-start | bytes 393224 | tf_op jit(solution)/shard_map/ppermute | solution.py:160
  3.9 0.5 collective-permute-start.1
  4.4 0.1 collective-permute-start
  4.6 4.0 %collective-permute-start.9 = (bf16[256,256]{1,0:T(8,128)(2,1)}, bf16[256,256]{1,0:T(8,128)(2,1)S(1)}, u32[]{:S(2)}, u32[]{:S(2)}) collective-permute-start(bf16[256,256]{1,0:T(8,128)(2,1)} %refs_0_.5), channel_id=1, source_target_pairs={{0,3},{1,2},{2,1},{3,0},{4,7},{5,6},{6,5},{7,4},{8,11},{9,10},{10,... | collective-permute-start | bytes 393224 | tf_op jit(solution)/shard_map/ppermute | solution.py:160
  8.6 0.0 collective-permute-start.8
  8.6 0.0 collective-permute-done.2.refs_3_
  8.6 1.2 %collective-permute-start.7 = (bf16[256,256]{1,0:T(8,128)(2,1)}, bf16[256,256]{1,0:T(8,128)(2,1)S(1)}, u32[]{:S(2)}, u32[]{:S(2)}) collective-permute-start(bf16[256,256]{1,0:T(8,128)(2,1)} %refs_0_.5), channel_id=1, source_target_pairs={{0,1},{1,0},{2,3},{3,2},{4,5},{5,4},{6,7},{7,6},{8,9},{9,8},{10,11... | collective-permute-start | bytes 393224 | tf_op jit(solution)/shard_map/ppermute | solution.py:160
  9.8 0.8 collective-permute-done.1.refs_2_
  10.5 0.2 collective-permute-done.refs_1_
  10.7 0.9 %pad_maximum_fusion = bf16[1024,256]{1,0:T(8,128)(2,1)S(1)} fusion(bf16[256,256]{1,0:T(8,128)(2,1)S(1)} %collective-permute-done.2.refs_3_, bf16[256,256]{1,0:T(8,128)(2,1)S(1)} %collective-permute-done.1.refs_2_, bf16[256,256]{1,0:T(8,128)(2,1)S(1)} %collective-permute-done.refs_1_, bf16[256,256]{1,0:T(8,128)(2,1)} %refs_0_.5), kind=kLoop, calls=%fused_computation.2 | loop fusion | flops 2097152 | bytes 1048576 | tf_op jit(solution)/shard_map/concatenate | solution.py:170
  11.6 0.1 collective-permute-start.3
  12.4 0.0 copy-start.1
  12.4 1.9 %copy-done.1 = bf16[96,128,128]{2,1,0:T(8,128)(2,1)S(1)} copy-done((bf16[96,128,128]{2,1,0:T(8,128)(2,1)S(1)}, bf16[96,128,128]{2,1,0:T(8,128)(2,1)}, u32[]{:S(2)}) %copy-start.1) | copy-done | bytes 3145752
  14.3 0.7 copy-done.2
  14.9 0.7 copy-done.3
  15.6 5.3 %densify.1 = (bf16[1024,2048]{1,0:T(8,128)(2,1)S(1)}, bf16[2048,1024]{1,0:T(8,128)(2,1)S(1)}) custom-call(s32[96]{0:T(128)S(1)} %copy-done.2, s32[96]{0:T(128)S(1)} %copy-done.3, s32[1]{0:T(128)S(6)} %copy.6.count_hbm, bf16[96,128,128]{2,1,0:T(8,128)(2,1)S(1)} %copy-done.1), custom_call_target="tpu_custom_call" | custom-call | bytes 11534336 | tf_op jit(solution)/shard_map/densify/pallas_call | solution.py:98
  20.9 0.0 collective-permute-done.8.refs_2_
  20.9 0.0 collective-permute-done.7.refs_1_
  20.9 0.7 shard_map.57
  21.6 0.6 collective-permute-start.10
  22.2 0.7 shard_map.56
  22.9 0.0 collective-permute-done.3.refs_4_
  22.9 1.2 %shard_map.55 = (bf16[256,256]{1,0:T(8,128)(2,1)S(1)}, bf16[256,256]{1,0:T(8,128)(2,1)S(1)}, bf16[256,256]{1,0:T(8,128)(2,1)S(1)}, bf16[256,256]{1,0:T(8,128)(2,1)S(1)}) custom-call(bf16[1024,2048]{1,0:T(8,128)(2,1)S(1)} %get-tuple-element.15.m_ref, bf16[256,256]{1,0:T(8,128)(2,1)S(1)} %copy-done, bf16[256,256]{1,0:T(8,128)(2,1)S(1)} %collective-permute-done.refs_1_, ...), custom_call_target="tpu_custom_call" | custom-call | flops 1073741824 | bytes 5767168 | tf_op jit(solution)/shard_map/pallas_call | solution.py:145
  24.2 1.5 %collective-permute-start.4 = (bf16[256,256]{1,0:T(8,128)(2,1)S(1)}, bf16[256,256]{1,0:T(8,128)(2,1)S(1)}, u32[]{:S(2)}, u32[]{:S(2)}) collective-permute-start(bf16[256,256]{1,0:T(8,128)(2,1)S(1)} %get-tuple-element.17), channel_id=1, source_target_pairs={{0,1},{1,0},{2,3},{3,2},{4,5},{5,4},{6,7},{7,6},{8,9},{9,8},{10,11... | collective-permute-start | bytes 393224 | tf_op jit(solution)/shard_map/ppermute | solution.py:160
  25.7 2.6 %collective-permute-start.5 = (bf16[256,256]{1,0:T(8,128)(2,1)S(1)}, bf16[256,256]{1,0:T(8,128)(2,1)S(1)}, u32[]{:S(2)}, u32[]{:S(2)}) collective-permute-start(bf16[256,256]{1,0:T(8,128)(2,1)S(1)} %get-tuple-element.18), channel_id=1, source_target_pairs={{0,2},{1,3},{2,0},{3,1},{4,6},{5,7},{6,4},{7,5},{8,10},{9,11},{10,... | collective-permute-start | bytes 393224 | tf_op jit(solution)/shard_map/ppermute | solution.py:160
  28.3 0.3 collective-permute-start.6
  28.6 0.1 fusion.12
  28.8 0.5 collective-permute-start.11
  29.3 0.8 collective-permute-start.13
  30.1 1.9 %collective-permute-done.4 = bf16[256,256]{1,0:T(8,128)(2,1)S(1)} collective-permute-done((bf16[256,256]{1,0:T(8,128)(2,1)S(1)}, bf16[256,256]{1,0:T(8,128)(2,1)S(1)}, u32[]{:S(2)}, u32[]{:S(2)}) %collective-permute-start.4) | collective-permute-done | bytes 131104 | tf_op jit(solution)/shard_map/ppermute | solution.py:160
  32.0 0.3 collective-permute-start.12
  32.3 6.3 %collective-permute-done.5 = bf16[256,256]{1,0:T(8,128)(2,1)S(1)} collective-permute-done((bf16[256,256]{1,0:T(8,128)(2,1)S(1)}, bf16[256,256]{1,0:T(8,128)(2,1)S(1)}, u32[]{:S(2)}, u32[]{:S(2)}) %collective-permute-start.5) | collective-permute-done | bytes 131104 | tf_op jit(solution)/shard_map/ppermute | solution.py:160
  38.6 0.0 collective-permute-done.6
  38.6 0.0 collective-permute-done.11
  38.6 0.0 collective-permute-done.13
  38.6 0.2 fusion.2.refs_0_
  38.8 3.6 %collective-permute-start.23 = (bf16[256,256]{1,0:T(8,128)(2,1)S(1)}, bf16[256,256]{1,0:T(8,128)(2,1)S(1)}, u32[]{:S(2)}, u32[]{:S(2)}) collective-permute-start(bf16[256,256]{1,0:T(8,128)(2,1)S(1)} %fusion.2.refs_0_), channel_id=1, source_target_pairs={{0,3},{1,2},{2,1},{3,0},{4,7},{5,6},{6,5},{7,4},{8,11},{9,10},{10,... | collective-permute-start | bytes 393224 | tf_op jit(solution)/shard_map/ppermute | solution.py:160
  42.4 0.6 collective-permute-start.22
  42.9 0.3 collective-permute-start.21
  43.3 3.2 %collective-permute-done.23.refs_3_ = bf16[256,256]{1,0:T(8,128)(2,1)S(1)} collective-permute-done((bf16[256,256]{1,0:T(8,128)(2,1)S(1)}, bf16[256,256]{1,0:T(8,128)(2,1)S(1)}, u32[]{:S(2)}, u32[]{:S(2)}) %collective-permute-start.23) | collective-permute-done | bytes 131104 | tf_op jit(solution)/shard_map/ppermute | solution.py:160
  46.4 7.7 %collective-permute-done.22.refs_2_ = bf16[256,256]{1,0:T(8,128)(2,1)S(1)} collective-permute-done((bf16[256,256]{1,0:T(8,128)(2,1)S(1)}, bf16[256,256]{1,0:T(8,128)(2,1)S(1)}, u32[]{:S(2)}, u32[]{:S(2)}) %collective-permute-start.22) | collective-permute-done | bytes 131104 | tf_op jit(solution)/shard_map/ppermute | solution.py:160
  54.1 0.7 shard_map.60
  54.8 0.1 collective-permute-start.24
  54.9 0.2 collective-permute-start.16
  55.1 1.8 %collective-permute-start.15 = (bf16[256,256]{1,0:T(8,128)(2,1)S(1)}, bf16[256,256]{1,0:T(8,128)(2,1)S(1)}, u32[]{:S(2)}, u32[]{:S(2)}) collective-permute-start(bf16[256,256]{1,0:T(8,128)(2,1)S(1)} %fusion.2.refs_0_), channel_id=1, source_target_pairs={{0,16},{4,20},{8,24},{12,28},{16,0},{20,4},{24,8},{28,12},{1,17},{... | collective-permute-start | bytes 393224 | tf_op jit(solution)/shard_map/ppermute | solution.py:160
  57.0 1.5 %collective-permute-start.14 = (bf16[256,256]{1,0:T(8,128)(2,1)S(1)}, bf16[256,256]{1,0:T(8,128)(2,1)S(1)}, u32[]{:S(2)}, u32[]{:S(2)}) collective-permute-start(bf16[256,256]{1,0:T(8,128)(2,1)S(1)} %fusion.2.refs_0_), channel_id=1, source_target_pairs={{0,8},{4,12},{8,0},{12,4},{16,24},{20,28},{24,16},{28,20},{1,9},{5... | collective-permute-start | bytes 393224 | tf_op jit(solution)/shard_map/ppermute | solution.py:160
  58.5 3.8 %collective-permute-done.16.refs_3_ = bf16[256,256]{1,0:T(8,128)(2,1)S(1)} collective-permute-done((bf16[256,256]{1,0:T(8,128)(2,1)S(1)}, bf16[256,256]{1,0:T(8,128)(2,1)S(1)}, u32[]{:S(2)}, u32[]{:S(2)}) %collective-permute-start.16) | collective-permute-done | bytes 131104 | tf_op jit(solution)/shard_map/ppermute | solution.py:160
  62.3 1.3 %collective-permute-done.15.refs_2_ = bf16[256,256]{1,0:T(8,128)(2,1)S(1)} collective-permute-done((bf16[256,256]{1,0:T(8,128)(2,1)S(1)}, bf16[256,256]{1,0:T(8,128)(2,1)S(1)}, u32[]{:S(2)}, u32[]{:S(2)}) %collective-permute-start.15) | collective-permute-done | bytes 131104 | tf_op jit(solution)/shard_map/ppermute | solution.py:160
  63.6 0.0 collective-permute-done.14.refs_1_
  63.7 0.1 collective-permute-start.17
  63.7 0.7 shard_map.59
  64.5 0.2 fusion.13
  64.7 1.5 %collective-permute-start.25 = (bf16[256,256]{1,0:T(8,128)(2,1)S(1)}, bf16[256,256]{1,0:T(8,128)(2,1)S(1)}, u32[]{:S(2)}, u32[]{:S(2)}) collective-permute-start(bf16[256,256]{1,0:T(8,128)(2,1)S(1)} %get-tuple-element.29), channel_id=1, source_target_pairs={{0,8},{4,12},{8,0},{12,4},{16,24},{20,28},{24,16},{28,20},{1,9},{5... | collective-permute-start | bytes 393224 | tf_op jit(solution)/shard_map/ppermute | solution.py:160
  66.2 1.5 %collective-permute-start.27 = (bf16[256,256]{1,0:T(8,128)(2,1)S(1)}, bf16[256,256]{1,0:T(8,128)(2,1)S(1)}, u32[]{:S(2)}, u32[]{:S(2)}) collective-permute-start(bf16[256,256]{1,0:T(8,128)(2,1)S(1)} %get-tuple-element.30), channel_id=1, source_target_pairs={{0,24},{4,28},{8,16},{12,20},{16,8},{20,12},{24,0},{28,4},{1,25},{... | collective-permute-start | bytes 393224 | tf_op jit(solution)/shard_map/ppermute | solution.py:160
  67.7 0.5 collective-permute-start.26
  68.3 1.3 %shard_map.58 = (bf16[256,256]{1,0:T(8,128)(2,1)S(1)}, bf16[256,256]{1,0:T(8,128)(2,1)S(1)}, bf16[256,256]{1,0:T(8,128)(2,1)S(1)}, bf16[256,256]{1,0:T(8,128)(2,1)S(1)}) custom-call(bf16[1024,2048]{1,0:T(8,128)(2,1)S(1)} %get-tuple-element.15.m_ref, bf16[256,256]{1,0:T(8,128)(2,1)S(1)} %fusion.2.refs_0_, ...), custom_call_target="tpu_custom_call" | custom-call | flops 1073741824 | bytes 5767168 | tf_op jit(solution)/shard_map/pallas_call | solution.py:145
  69.5 0.1 collective-permute-start.18
  69.6 3.1 %collective-permute-start.19 = (bf16[256,256]{1,0:T(8,128)(2,1)S(1)}, bf16[256,256]{1,0:T(8,128)(2,1)S(1)}, u32[]{:S(2)}, u32[]{:S(2)}) collective-permute-start(bf16[256,256]{1,0:T(8,128)(2,1)S(1)} %get-tuple-element.23), channel_id=1, source_target_pairs={{0,2},{1,3},{2,0},{3,1},{4,6},{5,7},{6,4},{7,5},{8,10},{9,11},{10,... | collective-permute-start | bytes 393224 | tf_op jit(solution)/shard_map/ppermute | solution.py:160
  72.7 1.3 %collective-permute-start.20 = (bf16[256,256]{1,0:T(8,128)(2,1)S(1)}, bf16[256,256]{1,0:T(8,128)(2,1)S(1)}, u32[]{:S(2)}, u32[]{:S(2)}) collective-permute-start(bf16[256,256]{1,0:T(8,128)(2,1)S(1)} %get-tuple-element.24), channel_id=1, source_target_pairs={{0,3},{1,2},{2,1},{3,0},{4,7},{5,6},{6,5},{7,4},{8,11},{9,10},{10,... | collective-permute-start | bytes 393224 | tf_op jit(solution)/shard_map/ppermute | solution.py:160
  74.0 0.5 collective-permute-done.27
  74.5 1.4 %collective-permute-done.26 = bf16[256,256]{1,0:T(8,128)(2,1)S(1)} collective-permute-done((bf16[256,256]{1,0:T(8,128)(2,1)S(1)}, bf16[256,256]{1,0:T(8,128)(2,1)S(1)}, u32[]{:S(2)}, u32[]{:S(2)}) %collective-permute-start.26) | collective-permute-done | bytes 131104 | tf_op jit(solution)/shard_map/ppermute | solution.py:160
  75.9 0.9 %collective-permute-done.18 = bf16[256,256]{1,0:T(8,128)(2,1)S(1)} collective-permute-done((bf16[256,256]{1,0:T(8,128)(2,1)S(1)}, bf16[256,256]{1,0:T(8,128)(2,1)S(1)}, u32[]{:S(2)}, u32[]{:S(2)}) %collective-permute-start.18) | collective-permute-done | bytes 131104 | tf_op jit(solution)/shard_map/ppermute | solution.py:160
  76.7 5.9 %collective-permute-done.19 = bf16[256,256]{1,0:T(8,128)(2,1)S(1)} collective-permute-done((bf16[256,256]{1,0:T(8,128)(2,1)S(1)}, bf16[256,256]{1,0:T(8,128)(2,1)S(1)}, u32[]{:S(2)}, u32[]{:S(2)}) %collective-permute-start.19) | collective-permute-done | bytes 131104 | tf_op jit(solution)/shard_map/ppermute | solution.py:160
  82.7 0.9 %fusion.3 = bf16[256,256]{1,0:T(8,128)(2,1)} fusion(bf16[256,256]{1,0:T(8,128)(2,1)S(1)} %copy-done, f32[1024,256]{1,0:T(8,128)S(1)} %get-tuple-element.26, bf16[256,256]{1,0:T(8,128)(2,1)S(1)} %fusion.2.refs_0_, bf16[256,256]{1,0:T(8,128)(2,1)S(1)} %collective-permute-done.27, bf16[256,256]{1,0:T(8,128)(2,1)S(1)} %collective-permute-done.26, ...), kind=kLoop, calls=%fused_computation.9 | loop fusion | flops 1376256 | bytes 1572864 | tf_op jit(solution)/shard_map/convert_element_type | solution.py:272
  (15 shorter events, 0.1 us)
Async XLA Ops:
  0.0 20.9 %copy-start = (bf16[256,256]{1,0:T(8,128)(2,1)S(1)}, bf16[256,256]{1,0:T(8,128)(2,1)}, u32[]{:S(2)}) copy-start(bf16[256,256]{1,0:T(8,128)(2,1)} %refs_0_.5) | copy-start | bytes 393220
  0.0 8.6 %collective-permute-start.2 = (bf16[256,256]{1,0:T(8,128)(2,1)}, bf16[256,256]{1,0:T(8,128)(2,1)S(1)}, u32[]{:S(2)}, u32[]{:S(2)}) collective-permute-start(bf16[256,256]{1,0:T(8,128)(2,1)} %refs_0_.5), channel_id=1, source_target_pairs={{0,24},{4,28},{8,16},{12,20},{16,8},{20,12},{24,0},{28,4},{1,25},{... | collective-permute-start | bytes 393224 | tf_op jit(solution)/shard_map/ppermute | solution.py:160
  3.9 6.6 %collective-permute-start.1 = (bf16[256,256]{1,0:T(8,128)(2,1)}, bf16[256,256]{1,0:T(8,128)(2,1)S(1)}, u32[]{:S(2)}, u32[]{:S(2)}) collective-permute-start(bf16[256,256]{1,0:T(8,128)(2,1)} %refs_0_.5), channel_id=1, source_target_pairs={{0,16},{4,20},{8,24},{12,28},{16,0},{20,4},{24,8},{28,12},{1,17},{... | collective-permute-start | bytes 393224 | tf_op jit(solution)/shard_map/ppermute | solution.py:160
  4.4 6.3 %collective-permute-start = (bf16[256,256]{1,0:T(8,128)(2,1)}, bf16[256,256]{1,0:T(8,128)(2,1)S(1)}, u32[]{:S(2)}, u32[]{:S(2)}) collective-permute-start(bf16[256,256]{1,0:T(8,128)(2,1)} %refs_0_.5), channel_id=1, source_target_pairs={{0,8},{4,12},{8,0},{12,4},{16,24},{20,28},{24,16},{28,20},{1,9},{5... | collective-permute-start | bytes 393224 | tf_op jit(solution)/shard_map/ppermute | solution.py:160
  4.6 16.3 %collective-permute-start.9 = (bf16[256,256]{1,0:T(8,128)(2,1)}, bf16[256,256]{1,0:T(8,128)(2,1)S(1)}, u32[]{:S(2)}, u32[]{:S(2)}) collective-permute-start(bf16[256,256]{1,0:T(8,128)(2,1)} %refs_0_.5), channel_id=1, source_target_pairs={{0,3},{1,2},{2,1},{3,0},{4,7},{5,6},{6,5},{7,4},{8,11},{9,10},{10,... | collective-permute-start | bytes 393224 | tf_op jit(solution)/shard_map/ppermute | solution.py:160
  8.6 12.3 %collective-permute-start.8 = (bf16[256,256]{1,0:T(8,128)(2,1)}, bf16[256,256]{1,0:T(8,128)(2,1)S(1)}, u32[]{:S(2)}, u32[]{:S(2)}) collective-permute-start(bf16[256,256]{1,0:T(8,128)(2,1)} %refs_0_.5), channel_id=1, source_target_pairs={{0,2},{1,3},{2,0},{3,1},{4,6},{5,7},{6,4},{7,5},{8,10},{9,11},{10,... | collective-permute-start | bytes 393224 | tf_op jit(solution)/shard_map/ppermute | solution.py:160
  8.6 12.3 %collective-permute-start.7 = (bf16[256,256]{1,0:T(8,128)(2,1)}, bf16[256,256]{1,0:T(8,128)(2,1)S(1)}, u32[]{:S(2)}, u32[]{:S(2)}) collective-permute-start(bf16[256,256]{1,0:T(8,128)(2,1)} %refs_0_.5), channel_id=1, source_target_pairs={{0,1},{1,0},{2,3},{3,2},{4,5},{5,4},{6,7},{7,6},{8,9},{9,8},{10,11... | collective-permute-start | bytes 393224 | tf_op jit(solution)/shard_map/ppermute | solution.py:160
  11.6 11.3 %collective-permute-start.3 = (bf16[1024,256]{1,0:T(8,128)(2,1)S(1)}, bf16[1024,256]{1,0:T(8,128)(2,1)S(1)}, u32[]{:S(2)}, u32[]{:S(2)}) collective-permute-start(bf16[1024,256]{1,0:T(8,128)(2,1)S(1)} %pad_maximum_fusion), channel_id=1, source_target_pairs={{0,4},{4,0},{8,12},{12,8},{16,20},{20,16},{24,28},{28,24},{1,5},{5... | collective-permute-start | bytes 1572872 | tf_op jit(solution)/shard_map/ppermute | solution.py:160
  12.4 1.9 %copy-start.1 = (bf16[96,128,128]{2,1,0:T(8,128)(2,1)S(1)}, bf16[96,128,128]{2,1,0:T(8,128)(2,1)}, u32[]{:S(2)}) copy-start(bf16[96,128,128]{2,1,0:T(8,128)(2,1)} %tiles_hbm.1) | copy-start | bytes 9437188
  14.3 0.7 copy-start.2
  14.9 0.7 copy-start.3
  21.6 7.0 %collective-permute-start.10 = (bf16[1024,256]{1,0:T(8,128)(2,1)S(1)}, bf16[1024,256]{1,0:T(8,128)(2,1)S(1)}, u32[]{:S(2)}, u32[]{:S(2)}) collective-permute-start(bf16[1024,256]{1,0:T(8,128)(2,1)S(1)} %shard_map.57), channel_id=1, source_target_pairs={{0,4},{4,0},{8,12},{12,8},{16,20},{20,16},{24,28},{28,24},{1,5},{5... | collective-permute-start | bytes 1572872 | tf_op jit(solution)/shard_map/ppermute | solution.py:160
  24.2 7.8 %collective-permute-start.4 = (bf16[256,256]{1,0:T(8,128)(2,1)S(1)}, bf16[256,256]{1,0:T(8,128)(2,1)S(1)}, u32[]{:S(2)}, u32[]{:S(2)}) collective-permute-start(bf16[256,256]{1,0:T(8,128)(2,1)S(1)} %get-tuple-element.17), channel_id=1, source_target_pairs={{0,1},{1,0},{2,3},{3,2},{4,5},{5,4},{6,7},{7,6},{8,9},{9,8},{10,11... | collective-permute-start | bytes 393224 | tf_op jit(solution)/shard_map/ppermute | solution.py:160
  25.7 12.9 %collective-permute-start.5 = (bf16[256,256]{1,0:T(8,128)(2,1)S(1)}, bf16[256,256]{1,0:T(8,128)(2,1)S(1)}, u32[]{:S(2)}, u32[]{:S(2)}) collective-permute-start(bf16[256,256]{1,0:T(8,128)(2,1)S(1)} %get-tuple-element.18), channel_id=1, source_target_pairs={{0,2},{1,3},{2,0},{3,1},{4,6},{5,7},{6,4},{7,5},{8,10},{9,11},{10,... | collective-permute-start | bytes 393224 | tf_op jit(solution)/shard_map/ppermute | solution.py:160
  28.3 10.3 %collective-permute-start.6 = (bf16[256,256]{1,0:T(8,128)(2,1)S(1)}, bf16[256,256]{1,0:T(8,128)(2,1)S(1)}, u32[]{:S(2)}, u32[]{:S(2)}) collective-permute-start(bf16[256,256]{1,0:T(8,128)(2,1)S(1)} %get-tuple-element.19), channel_id=1, source_target_pairs={{0,3},{1,2},{2,1},{3,0},{4,7},{5,6},{6,5},{7,4},{8,11},{9,10},{10,... | collective-permute-start | bytes 393224 | tf_op jit(solution)/shard_map/ppermute | solution.py:160
  28.8 9.8 %collective-permute-start.11 = (bf16[256,256]{1,0:T(8,128)(2,1)S(1)}, bf16[256,256]{1,0:T(8,128)(2,1)S(1)}, u32[]{:S(2)}, u32[]{:S(2)}) collective-permute-start(bf16[256,256]{1,0:T(8,128)(2,1)S(1)} %get-tuple-element.32), channel_id=1, source_target_pairs={{0,8},{4,12},{8,0},{12,4},{16,24},{20,28},{24,16},{28,20},{1,9},{5... | collective-permute-start | bytes 393224 | tf_op jit(solution)/shard_map/ppermute | solution.py:160
  29.3 9.3 %collective-permute-start.13 = (bf16[256,256]{1,0:T(8,128)(2,1)S(1)}, bf16[256,256]{1,0:T(8,128)(2,1)S(1)}, u32[]{:S(2)}, u32[]{:S(2)}) collective-permute-start(bf16[256,256]{1,0:T(8,128)(2,1)S(1)} %get-tuple-element.33), channel_id=1, source_target_pairs={{0,24},{4,28},{8,16},{12,20},{16,8},{20,12},{24,0},{28,4},{1,25},{... | collective-permute-start | bytes 393224 | tf_op jit(solution)/shard_map/ppermute | solution.py:160
  32.0 6.6 %collective-permute-start.12 = (bf16[256,256]{1,0:T(8,128)(2,1)S(1)}, bf16[256,256]{1,0:T(8,128)(2,1)S(1)}, u32[]{:S(2)}, u32[]{:S(2)}) collective-permute-start(bf16[256,256]{1,0:T(8,128)(2,1)S(1)} %get-tuple-element.34), channel_id=1, source_target_pairs={{0,16},{4,20},{8,24},{12,28},{16,0},{20,4},{24,8},{28,12},{1,17},{... | collective-permute-start | bytes 393224 | tf_op jit(solution)/shard_map/ppermute | solution.py:160
  38.8 7.6 %collective-permute-start.23 = (bf16[256,256]{1,0:T(8,128)(2,1)S(1)}, bf16[256,256]{1,0:T(8,128)(2,1)S(1)}, u32[]{:S(2)}, u32[]{:S(2)}) collective-permute-start(bf16[256,256]{1,0:T(8,128)(2,1)S(1)} %fusion.2.refs_0_), channel_id=1, source_target_pairs={{0,3},{1,2},{2,1},{3,0},{4,7},{5,6},{6,5},{7,4},{8,11},{9,10},{10,... | collective-permute-start | bytes 393224 | tf_op jit(solution)/shard_map/ppermute | solution.py:160
  42.4 11.7 %collective-permute-start.22 = (bf16[256,256]{1,0:T(8,128)(2,1)S(1)}, bf16[256,256]{1,0:T(8,128)(2,1)S(1)}, u32[]{:S(2)}, u32[]{:S(2)}) collective-permute-start(bf16[256,256]{1,0:T(8,128)(2,1)S(1)} %fusion.2.refs_0_), channel_id=1, source_target_pairs={{0,2},{1,3},{2,0},{3,1},{4,6},{5,7},{6,4},{7,5},{8,10},{9,11},{10,... | collective-permute-start | bytes 393224 | tf_op jit(solution)/shard_map/ppermute | solution.py:160
  42.9 11.2 %collective-permute-start.21 = (bf16[256,256]{1,0:T(8,128)(2,1)S(1)}, bf16[256,256]{1,0:T(8,128)(2,1)S(1)}, u32[]{:S(2)}, u32[]{:S(2)}) collective-permute-start(bf16[256,256]{1,0:T(8,128)(2,1)S(1)} %fusion.2.refs_0_), channel_id=1, source_target_pairs={{0,1},{1,0},{2,3},{3,2},{4,5},{5,4},{6,7},{7,6},{8,9},{9,8},{10,11... | collective-permute-start | bytes 393224 | tf_op jit(solution)/shard_map/ppermute | solution.py:160
  54.8 9.6 %collective-permute-start.24 = (bf16[1024,256]{1,0:T(8,128)(2,1)S(1)}, bf16[1024,256]{1,0:T(8,128)(2,1)S(1)}, u32[]{:S(2)}, u32[]{:S(2)}) collective-permute-start(bf16[1024,256]{1,0:T(8,128)(2,1)S(1)} %shard_map.60), channel_id=1, source_target_pairs={{0,4},{4,0},{8,12},{12,8},{16,20},{20,16},{24,28},{28,24},{1,5},{5... | collective-permute-start | bytes 1572872 | tf_op jit(solution)/shard_map/ppermute | solution.py:160
  54.9 7.4 %collective-permute-start.16 = (bf16[256,256]{1,0:T(8,128)(2,1)S(1)}, bf16[256,256]{1,0:T(8,128)(2,1)S(1)}, u32[]{:S(2)}, u32[]{:S(2)}) collective-permute-start(bf16[256,256]{1,0:T(8,128)(2,1)S(1)} %fusion.2.refs_0_), channel_id=1, source_target_pairs={{0,24},{4,28},{8,16},{12,20},{16,8},{20,12},{24,0},{28,4},{1,25},{... | collective-permute-start | bytes 393224 | tf_op jit(solution)/shard_map/ppermute | solution.py:160
  55.1 8.5 %collective-permute-start.15 = (bf16[256,256]{1,0:T(8,128)(2,1)S(1)}, bf16[256,256]{1,0:T(8,128)(2,1)S(1)}, u32[]{:S(2)}, u32[]{:S(2)}) collective-permute-start(bf16[256,256]{1,0:T(8,128)(2,1)S(1)} %fusion.2.refs_0_), channel_id=1, source_target_pairs={{0,16},{4,20},{8,24},{12,28},{16,0},{20,4},{24,8},{28,12},{1,17},{... | collective-permute-start | bytes 393224 | tf_op jit(solution)/shard_map/ppermute | solution.py:160
  57.0 6.6 %collective-permute-start.14 = (bf16[256,256]{1,0:T(8,128)(2,1)S(1)}, bf16[256,256]{1,0:T(8,128)(2,1)S(1)}, u32[]{:S(2)}, u32[]{:S(2)}) collective-permute-start(bf16[256,256]{1,0:T(8,128)(2,1)S(1)} %fusion.2.refs_0_), channel_id=1, source_target_pairs={{0,8},{4,12},{8,0},{12,4},{16,24},{20,28},{24,16},{28,20},{1,9},{5... | collective-permute-start | bytes 393224 | tf_op jit(solution)/shard_map/ppermute | solution.py:160
  63.7 4.6 %collective-permute-start.17 = (bf16[1024,256]{1,0:T(8,128)(2,1)S(1)}, bf16[1024,256]{1,0:T(8,128)(2,1)S(1)}, u32[]{:S(2)}, u32[]{:S(2)}) collective-permute-start(bf16[1024,256]{1,0:T(8,128)(2,1)S(1)} %pad_maximum_fusion.1), channel_id=1, source_target_pairs={{0,4},{4,0},{8,12},{12,8},{16,20},{20,16},{24,28},{28,24},{1,5},{5... | collective-permute-start | bytes 1572872 | tf_op jit(solution)/shard_map/ppermute | solution.py:160
  64.7 8.0 %collective-permute-start.25 = (bf16[256,256]{1,0:T(8,128)(2,1)S(1)}, bf16[256,256]{1,0:T(8,128)(2,1)S(1)}, u32[]{:S(2)}, u32[]{:S(2)}) collective-permute-start(bf16[256,256]{1,0:T(8,128)(2,1)S(1)} %get-tuple-element.29), channel_id=1, source_target_pairs={{0,8},{4,12},{8,0},{12,4},{16,24},{20,28},{24,16},{28,20},{1,9},{5... | collective-permute-start | bytes 393224 | tf_op jit(solution)/shard_map/ppermute | solution.py:160
  66.2 8.3 %collective-permute-start.27 = (bf16[256,256]{1,0:T(8,128)(2,1)S(1)}, bf16[256,256]{1,0:T(8,128)(2,1)S(1)}, u32[]{:S(2)}, u32[]{:S(2)}) collective-permute-start(bf16[256,256]{1,0:T(8,128)(2,1)S(1)} %get-tuple-element.30), channel_id=1, source_target_pairs={{0,24},{4,28},{8,16},{12,20},{16,8},{20,12},{24,0},{28,4},{1,25},{... | collective-permute-start | bytes 393224 | tf_op jit(solution)/shard_map/ppermute | solution.py:160
  67.7 8.1 %collective-permute-start.26 = (bf16[256,256]{1,0:T(8,128)(2,1)S(1)}, bf16[256,256]{1,0:T(8,128)(2,1)S(1)}, u32[]{:S(2)}, u32[]{:S(2)}) collective-permute-start(bf16[256,256]{1,0:T(8,128)(2,1)S(1)} %get-tuple-element.31), channel_id=1, source_target_pairs={{0,16},{4,20},{8,24},{12,28},{16,0},{20,4},{24,8},{28,12},{1,17},{... | collective-permute-start | bytes 393224 | tf_op jit(solution)/shard_map/ppermute | solution.py:160
  69.5 7.2 %collective-permute-start.18 = (bf16[256,256]{1,0:T(8,128)(2,1)S(1)}, bf16[256,256]{1,0:T(8,128)(2,1)S(1)}, u32[]{:S(2)}, u32[]{:S(2)}) collective-permute-start(bf16[256,256]{1,0:T(8,128)(2,1)S(1)} %get-tuple-element.22), channel_id=1, source_target_pairs={{0,1},{1,0},{2,3},{3,2},{4,5},{5,4},{6,7},{7,6},{8,9},{9,8},{10,11... | collective-permute-start | bytes 393224 | tf_op jit(solution)/shard_map/ppermute | solution.py:160
  69.6 13.0 %collective-permute-start.19 = (bf16[256,256]{1,0:T(8,128)(2,1)S(1)}, bf16[256,256]{1,0:T(8,128)(2,1)S(1)}, u32[]{:S(2)}, u32[]{:S(2)}) collective-permute-start(bf16[256,256]{1,0:T(8,128)(2,1)S(1)} %get-tuple-element.23), channel_id=1, source_target_pairs={{0,2},{1,3},{2,0},{3,1},{4,6},{5,7},{6,4},{7,5},{8,10},{9,11},{10,... | collective-permute-start | bytes 393224 | tf_op jit(solution)/shard_map/ppermute | solution.py:160
  72.7 10.0 %collective-permute-start.20 = (bf16[256,256]{1,0:T(8,128)(2,1)S(1)}, bf16[256,256]{1,0:T(8,128)(2,1)S(1)}, u32[]{:S(2)}, u32[]{:S(2)}) collective-permute-start(bf16[256,256]{1,0:T(8,128)(2,1)S(1)} %get-tuple-element.24), channel_id=1, source_target_pairs={{0,3},{1,2},{2,1},{3,0},{4,7},{5,6},{6,5},{7,4},{8,11},{9,10},{10,... | collective-permute-start | bytes 393224 | tf_op jit(solution)/shard_map/ppermute | solution.py:160

commit v2 on v0

--- a/solution.py
+++ b/solution.py
@@ -20,32 +20,26 @@
     return n & (n - 1) == 0
 
 
-def densify_kernel(
-    n_rows, n_cols, panel_blocks, rows_ref, cols_ref, count_ref, tiles_ref, a_ref, at_ref, table
-):
-    slots = tiles_ref.shape[0]
+def slot_table(n_rows, n_cols, panel_blocks, tile_rows, tile_cols, owner_counts):
+    slots = tile_rows.shape[0]
     range_blocks = panel_blocks * n_cols
     set_blocks = panel_blocks * n_rows
     p = lax.axis_index("row")
     q = lax.axis_index("col")
-
-    def clear(i, carry):
-        table[i] = slots
-        return carry
-
-    lax.fori_loop(0, range_blocks * set_blocks, clear, 0)
-
-    def place(s, carry):
-        row = rows_ref[s] - p * range_blocks
-        row_at = ((row // panel_blocks) ^ q) * panel_blocks + row % panel_blocks
-        col = cols_ref[s]
-        relative = (col // (panel_blocks * n_cols)) ^ p
-        unit = (relative % 2) * (n_rows // 2) + relative // 2
-        col_at = unit * panel_blocks + col % panel_blocks
-        table[row_at * set_blocks + col_at] = s
-        return carry
-
-    lax.fori_loop(0, jnp.minimum(count_ref[0], slots), place, 0)
+    row = tile_rows - p * range_blocks
+    row_at = ((row // panel_blocks) ^ q) * panel_blocks + row % panel_blocks
+    relative = (tile_cols // range_blocks) ^ p
+    unit = (relative % 2) * (n_rows // 2) + relative // 2
+    place = row_at * set_blocks + unit * panel_blocks + tile_cols % panel_blocks
+    slot = jnp.arange(slots, dtype=jnp.int32)
+    place = jnp.where(slot < owner_counts[0], place, -1)
+    blocks = jnp.arange(range_blocks * set_blocks, dtype=jnp.int32)
+    return jnp.min(jnp.where(place[None, :] == blocks[:, None], slot[None, :], slots), axis=1)
+
+
+def densify_kernel(table, tiles_ref, a_ref):
+    slots = tiles_ref.shape[0]
+    set_blocks = a_ref.shape[1] // BS
 
     def fill(r, carry):
         for c in range(set_blocks):
@@ -53,37 +47,55 @@
             tile = tiles_ref[jnp.minimum(s, slots - 1)]
             tile = jnp.where(s < slots, tile, jnp.zeros_like(tile))
             a_ref[pl.ds(pl.multiple_of(r * BS, BS), BS), c * BS : (c + 1) * BS] = tile
-            at_ref[c * BS : (c + 1) * BS, pl.ds(pl.multiple_of(r * BS, BS), BS)] = tile.T
         return carry
 
-    lax.fori_loop(0, range_blocks, fill, 0)
-
-
-def densify(n_rows, n_cols, panel_blocks, tile_rows, tile_cols, owner_counts, block_tiles):
-    height = panel_blocks * n_cols * BS
-    breadth = panel_blocks * n_rows * BS
-    smem = pl.BlockSpec(memory_space=pltpu.SMEM)
+    lax.fori_loop(0, a_ref.shape[0] // BS, fill, 0)
+
+
+def densify(height, breadth, table, block_tiles):
     vmem = pl.BlockSpec(memory_space=pltpu.VMEM)
     return pl.pallas_call(
-        functools.partial(densify_kernel, n_rows, n_cols, panel_blocks),
-        out_shape=(
-            jax.ShapeDtypeStruct((height, breadth), block_tiles.dtype),
-            jax.ShapeDtypeStruct((breadth, height), block_tiles.dtype),
-        ),
-        in_specs=[smem, smem, smem, vmem],
-        out_specs=(vmem, vmem),
-        scratch_shapes=[pltpu.SMEM((height // BS * (breadth // BS),), jnp.int32)],
+        densify_kernel,
+        out_shape=jax.ShapeDtypeStruct((height, breadth), block_tiles.dtype),
+        in_specs=[pl.BlockSpec(memory_space=pltpu.SMEM), vmem],
+        out_specs=vmem,
         compiler_params=pltpu.CompilerParams(vmem_limit_bytes=16 * MIB),
         cost_estimate=pl.CostEstimate(
-            flops=0, transcendentals=0, bytes_accessed=2 * block_tiles.size + 4 * height * breadth
+            flops=0, transcendentals=0, bytes_accessed=2 * (block_tiles.size + height * breadth)
         ),
         name="densify",
-    )(tile_rows, tile_cols, owner_counts, block_tiles)
-
-
-def product_kernel(n_in, m_ref, *refs):
+    )(table, block_tiles)
+
+
+def transpose_kernel(a_ref, at_ref):
+    def fill(r, carry):
+        rows = pl.ds(pl.multiple_of(r * BS, BS), BS)
+        for c in range(a_ref.shape[1] // BS):
+            at_ref[c * BS : (c + 1) * BS, rows] = a_ref[rows, c * BS : (c + 1) * BS].T
+        return carry
+
+    lax.fori_loop(0, a_ref.shape[0] // BS, fill, 0)
+
+
+def transpose(matrix):
+    height, breadth = matrix.shape
+    vmem = pl.BlockSpec(memory_space=pltpu.VMEM)
+    return pl.pallas_call(
+        transpose_kernel,
+        out_shape=jax.ShapeDtypeStruct((breadth, height), matrix.dtype),
+        in_specs=[vmem],
+        out_specs=vmem,
+        compiler_params=pltpu.CompilerParams(vmem_limit_bytes=16 * MIB),
+        cost_estimate=pl.CostEstimate(
+            flops=0, transcendentals=0, bytes_accessed=4 * height * breadth
+        ),
+        name="mirror",
+    )(matrix)
+
+
+def product_kernel(n_in, start, m_ref, *refs):
     panels, outs = refs[:n_in], refs[n_in:]
-    done = 0
+    done = start
     for out in outs:
         for top in range(0, out.shape[0], 256):
             total = None
@@ -101,25 +113,33 @@
             done += 256
 
 
-def product(matrix, panels, out_rows):
+def product(matrix, panels, start, out_rows):
     width = panels[0].shape[1]
     vmem = pl.BlockSpec(memory_space=pltpu.VMEM)
     return pl.pallas_call(
-        functools.partial(product_kernel, len(panels)),
+        functools.partial(product_kernel, len(panels), start),
         out_shape=tuple(jax.ShapeDtypeStruct((rows, width), jnp.bfloat16) for rows in out_rows),
         in_specs=[vmem] * (1 + len(panels)),
         out_specs=tuple(vmem for _ in out_rows),
         compiler_params=pltpu.CompilerParams(vmem_limit_bytes=16 * MIB),
         cost_estimate=pl.CostEstimate(
-            flops=2 * matrix.size * width,
+            flops=2 * sum(out_rows) * matrix.shape[1] * width,
             transcendentals=0,
-            bytes_accessed=2 * (matrix.size + sum(matrix.shape) * width),
+            bytes_accessed=2 * (sum(out_rows) * (matrix.shape[1] + width) + matrix.shape[1] * width),
         ),
     )(matrix, *panels)
 
 
 def swap(x, axis, j):
     return lax.ppermute(x, axis, [(i, i ^ j) for i in range(lax.axis_size(axis))])
+
+
+def hops(j):
+    masks = []
+    while j:
+        masks.append((1 << j.bit_length()) - 1)
+        j ^= masks[-1]
+    return masks
 
 
 def apply_dense(panel, matrix, matrix_t):
@@ -127,14 +147,22 @@
     n_cols = lax.axis_size("col")
     rows, width = panel.shape
     half = n_rows // 2
-    range_panels = [panel] + [swap(panel, "col", j) for j in range(1, n_cols)]
+    by_hops = sorted(range(1, n_cols), key=lambda j: (len(hops(j)), -j))
+
+    range_panels = [panel] + [None] * (n_cols - 1)
+    for j in by_hops:
+        last = hops(j)[-1]
+        range_panels[j] = swap(range_panels[j ^ last], "col", last)
     near = [panel] + [swap(panel, "row", 2 * k) for k in range(1, half)]
     far = swap(jnp.concatenate(near), "row", 1)
-    upper = product(matrix, near + [far], [rows] * n_cols)
+    upper = list(product(matrix, near + [far], 0, [rows] * n_cols))
+    for j in reversed(by_hops):
+        last = hops(j)[-1]
+        part = swap(upper[j].astype(jnp.bfloat16), "col", last)
+        upper[j ^ last] = upper[j ^ last].astype(jnp.float32) + part.astype(jnp.float32)
     own = upper[0].astype(jnp.float32)
-    for j in range(1, n_cols):
-        own += swap(upper[j], "col", j).astype(jnp.float32)
-    keep, give = product(matrix_t, range_panels, [half * rows] * 2)
+    (give,) = product(matrix_t, range_panels, half * rows, [half * rows])
+    (keep,) = product(matrix_t, range_panels, 0, [half * rows])
     paired = keep.astype(jnp.float32) + swap(give, "row", 1).astype(jnp.float32)
     paired = paired.reshape(half, rows, width)
     own += paired[0]
@@ -217,9 +245,11 @@
     n_cols = lax.axis_size("col")
     panel_blocks = vector_panel.shape[0] // BS
     if is_dense(n_rows, n_cols, panel_blocks, block_tiles.shape[0]):
-        matrix, matrix_t = densify(
-            n_rows, n_cols, panel_blocks, tile_rows, tile_cols, owner_counts, block_tiles
+        table = slot_table(
+            n_rows, n_cols, panel_blocks, tile_rows, tile_cols, owner_counts
         )
+        matrix = densify(panel_blocks * n_cols * BS, panel_blocks * n_rows * BS, table, block_tiles)
+        matrix_t = transpose(matrix)
         operate = functools.partial(apply_dense, matrix=matrix, matrix_t=matrix_t)
     else:
         operate = slot_operator(panel_blocks, block_tiles, tile_rows, tile_cols, owner_counts)

time: 94 us -> 71.3 us (0.76)
  waiting for transfers between devices: 42.5 us -> 22.6 us
  Pallas kernels: 11.2 us -> 8.83 us
  local copies, waits for them, and re-layouts: 4.15 us -> 1.95 us
  other arithmetic: 1.32 us -> 3.08 us
    ppermute x28, waiting for transfers between devices: 42.5 us -> 22.6 us  [swap(): lax.ppermute(x, axis, [(i, i ^ j) for i in range(lax.axis_size(axis))])]
    pallas_call x5 -> x8, Pallas kernels: 11.2 us -> 8.83 us  [the longest x6 5.32 us: product(): pl.pallas_call(functools.partial(product_kernel, len(panels), start), out...]
    unnamed x8 -> x4, local copies, waits for them, and re-layouts: 4.1 us -> 1.89 us
  transfers between devices with their start and end apart: 28 -> 28, of which waited for: 15 -> 13; matrix products, arithmetic and copies ran while one was open for 0% -> 3% of each run, Pallas kernels for 9% -> 12%
where the time goes in v2:
time: 71.3 us; the launch traced here: 71.2 us
  starting transfers between devices  33.8 us (47%)
  waiting for transfers between devices  22.6 us (32%)
  Pallas kernels  8.83 us (12%)
  other arithmetic  3.08 us (4%)
  local copies, waits for them, and re-layouts  1.95 us (3%)
  between operations  0.88 us (1%)
    ppermute x28, starting transfers between devices, swap(): lax.ppermute(x, axis, [(i, i ^ j) for i in range(lax.axis_size(axis))])  33.8 us
    ppermute x28, waiting for transfers between devices, swap(): lax.ppermute(x, axis, [(i, i ^ j) for i in range(lax.axis_size(axis))])  22.6 us
    pallas_call x6, Pallas kernels, product(): pl.pallas_call(functools.partial(product_kernel, len(panels), start), out...  5.32 us
    unnamed x4, local copies, waits for them, and re-layouts  1.89 us
    pallas_call x1, Pallas kernels, densify(): pl.pallas_call(densify_kernel, out_shape=jax.ShapeDtypeStruct((height, br...  1.81 us
    pallas_call x1, Pallas kernels, transpose(): pl.pallas_call(transpose_kernel, out_shape=jax.ShapeDtypeStruct((breadth,...  1.71 us
  transfers between devices with their start and end apart: 28, of which 13 were waited for; matrix products, arithmetic and copies ran while one was open for 3% of the time, Pallas kernels for 12%

profile of v2, /device:TPU:0, one launch (start us, length us, event | category | flops | bytes accessed | tf_op | source)
XLA Modules:
  0.0 71.2 jit_solution(6377366197871309336)
XLA Ops:
  0.0 5.1 %collective-permute-start.8 = (bf16[256,256]{1,0:T(8,128)(2,1)}, bf16[256,256]{1,0:T(8,128)(2,1)S(1)}, u32[]{:S(2)}, u32[]{:S(2)}) collective-permute-start(bf16[256,256]{1,0:T(8,128)(2,1)} %refs_0_.5), channel_id=1, source_target_pairs={{0,3},{1,2},{2,1},{3,0},{4,7},{5,6},{6,5},{7,4},{8,11},{9,10},{10,... | collective-permute-start | bytes 393224 | tf_op jit(solution)/shard_map/ppermute | solution.py:134
  5.1 0.0 collective-permute-start.7
  5.1 2.4 %collective-permute-start.2 = (bf16[256,256]{1,0:T(8,128)(2,1)}, bf16[256,256]{1,0:T(8,128)(2,1)S(1)}, u32[]{:S(2)}, u32[]{:S(2)}) collective-permute-start(bf16[256,256]{1,0:T(8,128)(2,1)} %refs_0_.5), channel_id=1, source_target_pairs={{0,24},{4,28},{8,16},{12,20},{16,8},{20,12},{24,0},{28,4},{1,25},{... | collective-permute-start | bytes 393224 | tf_op jit(solution)/shard_map/ppermute | solution.py:134
  7.5 0.5 collective-permute-start.1
  8.0 0.5 collective-permute-start
  9.2 0.7 compare_select_fusion
  9.9 0.0 collective-permute-done.8.refs_3_
  9.9 2.1 %collective-permute-start.9 = (bf16[256,256]{1,0:T(8,128)(2,1)S(1)}, bf16[256,256]{1,0:T(8,128)(2,1)S(1)}, u32[]{:S(2)}, u32[]{:S(2)}) collective-permute-start(bf16[256,256]{1,0:T(8,128)(2,1)S(1)} %collective-permute-done.8.refs_3_), channel_id=1, source_target_pairs={{0,1},{1,0},{2,3},{3,2},{4,5},{5,4},{6,7},{7,6},{8,9},{9,8},{10,11... | collective-permute-start | bytes 393224 | tf_op jit(solution)/shard_map/ppermute | solution.py:134
  12.0 0.0 collective-permute-done.2.refs_3_
  12.0 1.9 %collective-permute-done.1.refs_2_ = bf16[256,256]{1,0:T(8,128)(2,1)S(1)} collective-permute-done((bf16[256,256]{1,0:T(8,128)(2,1)}, bf16[256,256]{1,0:T(8,128)(2,1)S(1)}, u32[]{:S(2)}, u32[]{:S(2)}) %collective-permute-start.1) | collective-permute-done | bytes 131104 | tf_op jit(solution)/shard_map/ppermute | solution.py:134
  14.0 0.1 collective-permute-done.refs_1_
  14.0 0.9 %pad_maximum_fusion = bf16[1024,256]{1,0:T(8,128)(2,1)S(1)} fusion(bf16[256,256]{1,0:T(8,128)(2,1)S(1)} %collective-permute-done.2.refs_3_, bf16[256,256]{1,0:T(8,128)(2,1)S(1)} %collective-permute-done.1.refs_2_, bf16[256,256]{1,0:T(8,128)(2,1)S(1)} %collective-permute-done.refs_1_, bf16[256,256]{1,0:T(8,128)(2,1)} %refs_0_.5), kind=kLoop, calls=%fused_computation.2 | loop fusion | flops 2097152 | bytes 1048576 | tf_op jit(solution)/shard_map/concatenate | solution.py:157
  15.0 0.1 collective-permute-start.3
  15.0 0.1 select_reduce_fusion.table
  15.1 0.0 copy-start.1
  15.2 1.9 %copy-done.1 = bf16[96,128,128]{2,1,0:T(8,128)(2,1)S(1)} copy-done((bf16[96,128,128]{2,1,0:T(8,128)(2,1)S(1)}, bf16[96,128,128]{2,1,0:T(8,128)(2,1)}, u32[]{:S(2)}) %copy-start.1) | copy-done | bytes 3145752
  17.0 1.8 %densify.1.m_ref.a_ref = bf16[1024,2048]{1,0:T(8,128)(2,1)S(1)} custom-call(s32[128]{0:T(128)S(1)} %select_reduce_fusion.table, bf16[96,128,128]{2,1,0:T(8,128)(2,1)S(1)} %copy-done.1), custom_call_target="tpu_custom_call" | custom-call | bytes 7340032 | tf_op jit(solution)/shard_map/densify/pallas_call | solution.py:57
  18.9 0.0 copy-start
  18.9 1.7 %mirror.1.m_ref = bf16[2048,1024]{1,0:T(8,128)(2,1)S(1)} custom-call(bf16[1024,2048]{1,0:T(8,128)(2,1)S(1)} %densify.1.m_ref.a_ref), custom_call_target="tpu_custom_call" | custom-call | bytes 8388608 | tf_op jit(solution)/shard_map/mirror/pallas_call | solution.py:83
  20.6 0.0 collective-permute-done.7.refs_1_
  20.6 0.0 collective-permute-done.9.refs_2_
  20.6 0.7 shard_map.57
  21.3 0.6 collective-permute-start.10
  21.9 0.7 shard_map.56
  22.6 1.3 %shard_map.55 = (bf16[256,256]{1,0:T(8,128)(2,1)S(1)}, bf16[256,256]{1,0:T(8,128)(2,1)S(1)}, bf16[256,256]{1,0:T(8,128)(2,1)S(1)}, bf16[256,256]{1,0:T(8,128)(2,1)S(1)}) custom-call(bf16[1024,2048]{1,0:T(8,128)(2,1)S(1)} %densify.1.m_ref.a_ref, bf16[256,256]{1,0:T(8,128)(2,1)S(1)} %copy-done, bf16[256,256]{1,0:T(8,128)(2,1)S(1)} %collective-permute-done.refs_1_, ...), custom_call_target="tpu_custom_call" | custom-call | flops 1073741824 | bytes 5767168 | tf_op jit(solution)/shard_map/pallas_call | solution.py:119
  23.9 1.8 %collective-permute-start.4 = (bf16[256,256]{1,0:T(8,128)(2,1)S(1)}, bf16[256,256]{1,0:T(8,128)(2,1)S(1)}, u32[]{:S(2)}, u32[]{:S(2)}) collective-permute-start(bf16[256,256]{1,0:T(8,128)(2,1)S(1)} %get-tuple-element.14), channel_id=1, source_target_pairs={{0,1},{1,0},{2,3},{3,2},{4,5},{5,4},{6,7},{7,6},{8,9},{9,8},{10,11... | collective-permute-start | bytes 393224 | tf_op jit(solution)/shard_map/ppermute | solution.py:134
  25.7 0.3 collective-permute-start.5
  26.0 0.0 collective-permute-done.10
  26.0 0.2 fusion.16
  26.2 1.6 %collective-permute-start.11 = (bf16[256,256]{1,0:T(8,128)(2,1)S(1)}, bf16[256,256]{1,0:T(8,128)(2,1)S(1)}, u32[]{:S(2)}, u32[]{:S(2)}) collective-permute-start(bf16[256,256]{1,0:T(8,128)(2,1)S(1)} %get-tuple-element.28), channel_id=1, source_target_pairs={{0,8},{4,12},{8,0},{12,4},{16,24},{20,28},{24,16},{28,20},{1,9},{5... | collective-permute-start | bytes 393224 | tf_op jit(solution)/shard_map/ppermute | solution.py:134
  27.8 1.4 %collective-permute-start.13 = (bf16[256,256]{1,0:T(8,128)(2,1)S(1)}, bf16[256,256]{1,0:T(8,128)(2,1)S(1)}, u32[]{:S(2)}, u32[]{:S(2)}) collective-permute-start(bf16[256,256]{1,0:T(8,128)(2,1)S(1)} %get-tuple-element.29), channel_id=1, source_target_pairs={{0,24},{4,28},{8,16},{12,20},{16,8},{20,12},{24,0},{28,4},{1,25},{... | collective-permute-start | bytes 393224 | tf_op jit(solution)/shard_map/ppermute | solution.py:134
  29.2 0.6 collective-permute-start.12
  29.7 2.5 %collective-permute-done.5 = bf16[256,256]{1,0:T(8,128)(2,1)S(1)} collective-permute-done((bf16[256,256]{1,0:T(8,128)(2,1)S(1)}, bf16[256,256]{1,0:T(8,128)(2,1)S(1)}, u32[]{:S(2)}, u32[]{:S(2)}) %collective-permute-start.5) | collective-permute-done | bytes 131104 | tf_op jit(solution)/shard_map/ppermute | solution.py:134
  32.2 0.7 collective-permute-start.6
  32.9 2.1 %collective-permute-done.13 = bf16[256,256]{1,0:T(8,128)(2,1)S(1)} collective-permute-done((bf16[256,256]{1,0:T(8,128)(2,1)S(1)}, bf16[256,256]{1,0:T(8,128)(2,1)S(1)}, u32[]{:S(2)}, u32[]{:S(2)}) %collective-permute-start.13) | collective-permute-done | bytes 131104 | tf_op jit(solution)/shard_map/ppermute | solution.py:134
  35.0 1.3 %collective-permute-done.12 = bf16[256,256]{1,0:T(8,128)(2,1)S(1)} collective-permute-done((bf16[256,256]{1,0:T(8,128)(2,1)S(1)}, bf16[256,256]{1,0:T(8,128)(2,1)S(1)}, u32[]{:S(2)}, u32[]{:S(2)}) %collective-permute-start.12) | collective-permute-done | bytes 131104 | tf_op jit(solution)/shard_map/ppermute | solution.py:134
  36.3 2.8 %collective-permute-done.6 = bf16[256,256]{1,0:T(8,128)(2,1)S(1)} collective-permute-done((bf16[256,256]{1,0:T(8,128)(2,1)S(1)}, bf16[256,256]{1,0:T(8,128)(2,1)S(1)}, u32[]{:S(2)}, u32[]{:S(2)}) %collective-permute-start.6) | collective-permute-done | bytes 131104 | tf_op jit(solution)/shard_map/ppermute | solution.py:134
  39.1 0.1 fusion.2.refs_0_
  39.2 0.7 collective-permute-start.22
  39.9 1.7 %collective-permute-start.16 = (bf16[256,256]{1,0:T(8,128)(2,1)S(1)}, bf16[256,256]{1,0:T(8,128)(2,1)S(1)}, u32[]{:S(2)}, u32[]{:S(2)}) collective-permute-start(bf16[256,256]{1,0:T(8,128)(2,1)S(1)} %fusion.2.refs_0_), channel_id=1, source_target_pairs={{0,24},{4,28},{8,16},{12,20},{16,8},{20,12},{24,0},{28,4},{1,25},{... | collective-permute-start | bytes 393224 | tf_op jit(solution)/shard_map/ppermute | solution.py:134
  41.5 1.3 %collective-permute-start.15 = (bf16[256,256]{1,0:T(8,128)(2,1)S(1)}, bf16[256,256]{1,0:T(8,128)(2,1)S(1)}, u32[]{:S(2)}, u32[]{:S(2)}) collective-permute-start(bf16[256,256]{1,0:T(8,128)(2,1)S(1)} %fusion.2.refs_0_), channel_id=1, source_target_pairs={{0,16},{4,20},{8,24},{12,28},{16,0},{20,4},{24,8},{28,12},{1,17},{... | collective-permute-start | bytes 393224 | tf_op jit(solution)/shard_map/ppermute | solution.py:134
  42.9 0.5 collective-permute-start.14
  43.4 2.0 %collective-permute-start.21 = (bf16[256,256]{1,0:T(8,128)(2,1)S(1)}, bf16[256,256]{1,0:T(8,128)(2,1)S(1)}, u32[]{:S(2)}, u32[]{:S(2)}) collective-permute-start(bf16[256,256]{1,0:T(8,128)(2,1)S(1)} %fusion.2.refs_0_), channel_id=1, source_target_pairs={{0,1},{1,0},{2,3},{3,2},{4,5},{5,4},{6,7},{7,6},{8,9},{9,8},{10,11... | collective-permute-start | bytes 393224 | tf_op jit(solution)/shard_map/ppermute | solution.py:134
  45.4 0.8 %collective-permute-done.22.refs_3_ = bf16[256,256]{1,0:T(8,128)(2,1)S(1)} collective-permute-done((bf16[256,256]{1,0:T(8,128)(2,1)S(1)}, bf16[256,256]{1,0:T(8,128)(2,1)S(1)}, u32[]{:S(2)}, u32[]{:S(2)}) %collective-permute-start.22) | collective-permute-done | bytes 131104 | tf_op jit(solution)/shard_map/ppermute | solution.py:134
  46.2 1.7 %collective-permute-start.23 = (bf16[256,256]{1,0:T(8,128)(2,1)S(1)}, bf16[256,256]{1,0:T(8,128)(2,1)S(1)}, u32[]{:S(2)}, u32[]{:S(2)}) collective-permute-start(bf16[256,256]{1,0:T(8,128)(2,1)S(1)} %collective-permute-done.22.refs_3_), channel_id=1, source_target_pairs={{0,1},{1,0},{2,3},{3,2},{4,5},{5,4},{6,7},{7,6},{8,9},{9,8},{10,11... | collective-permute-start | bytes 393224 | tf_op jit(solution)/shard_map/ppermute | solution.py:134
  48.0 0.1 collective-permute-start.17
  48.1 1.6 %collective-permute-done.21.refs_1_ = bf16[256,256]{1,0:T(8,128)(2,1)S(1)} collective-permute-done((bf16[256,256]{1,0:T(8,128)(2,1)S(1)}, bf16[256,256]{1,0:T(8,128)(2,1)S(1)}, u32[]{:S(2)}, u32[]{:S(2)}) %collective-permute-start.21) | collective-permute-done | bytes 131104 | tf_op jit(solution)/shard_map/ppermute | solution.py:134
  49.7 2.0 %collective-permute-done.23.refs_2_ = bf16[256,256]{1,0:T(8,128)(2,1)S(1)} collective-permute-done((bf16[256,256]{1,0:T(8,128)(2,1)S(1)}, bf16[256,256]{1,0:T(8,128)(2,1)S(1)}, u32[]{:S(2)}, u32[]{:S(2)}) %collective-permute-start.23) | collective-permute-done | bytes 131104 | tf_op jit(solution)/shard_map/ppermute | solution.py:134
  51.8 0.7 shard_map.60
  52.5 0.1 collective-permute-start.24
  52.6 0.7 shard_map.59
  53.3 1.2 %shard_map.58 = (bf16[256,256]{1,0:T(8,128)(2,1)S(1)}, bf16[256,256]{1,0:T(8,128)(2,1)S(1)}, bf16[256,256]{1,0:T(8,128)(2,1)S(1)}, bf16[256,256]{1,0:T(8,128)(2,1)S(1)}) custom-call(bf16[1024,2048]{1,0:T(8,128)(2,1)S(1)} %densify.1.m_ref.a_ref, bf16[256,256]{1,0:T(8,128)(2,1)S(1)} %fusion.2.refs_0_, bf16[256,256]{1,0:T(8,128)(2,1)S(1)} %collective-permute-done.14.refs_1_, ...), custom_call_target="tpu_custom_call" | custom-call | flops 1073741824 | bytes 5767168 | tf_op jit(solution)/shard_map/pallas_call | solution.py:119
  54.5 1.3 %collective-permute-start.18 = (bf16[256,256]{1,0:T(8,128)(2,1)S(1)}, bf16[256,256]{1,0:T(8,128)(2,1)S(1)}, u32[]{:S(2)}, u32[]{:S(2)}) collective-permute-start(bf16[256,256]{1,0:T(8,128)(2,1)S(1)} %get-tuple-element.18), channel_id=1, source_target_pairs={{0,1},{1,0},{2,3},{3,2},{4,5},{5,4},{6,7},{7,6},{8,9},{9,8},{10,11... | collective-permute-start | bytes 393224 | tf_op jit(solution)/shard_map/ppermute | solution.py:134
  55.8 0.8 %collective-permute-start.19 = (bf16[256,256]{1,0:T(8,128)(2,1)S(1)}, bf16[256,256]{1,0:T(8,128)(2,1)S(1)}, u32[]{:S(2)}, u32[]{:S(2)}) collective-permute-start(bf16[256,256]{1,0:T(8,128)(2,1)S(1)} %get-tuple-element.20), channel_id=1, source_target_pairs={{0,1},{1,0},{2,3},{3,2},{4,5},{5,4},{6,7},{7,6},{8,9},{9,8},{10,11... | collective-permute-start | bytes 393224 | tf_op jit(solution)/shard_map/ppermute | solution.py:134
  56.6 0.1 fusion.17
  56.8 1.6 %collective-permute-start.25 = (bf16[256,256]{1,0:T(8,128)(2,1)S(1)}, bf16[256,256]{1,0:T(8,128)(2,1)S(1)}, u32[]{:S(2)}, u32[]{:S(2)}) collective-permute-start(bf16[256,256]{1,0:T(8,128)(2,1)S(1)} %get-tuple-element.25), channel_id=1, source_target_pairs={{0,8},{4,12},{8,0},{12,4},{16,24},{20,28},{24,16},{28,20},{1,9},{5... | collective-permute-start | bytes 393224 | tf_op jit(solution)/shard_map/ppermute | solution.py:134
  58.4 1.4 %collective-permute-start.27 = (bf16[256,256]{1,0:T(8,128)(2,1)S(1)}, bf16[256,256]{1,0:T(8,128)(2,1)S(1)}, u32[]{:S(2)}, u32[]{:S(2)}) collective-permute-start(bf16[256,256]{1,0:T(8,128)(2,1)S(1)} %get-tuple-element.26), channel_id=1, source_target_pairs={{0,24},{4,28},{8,16},{12,20},{16,8},{20,12},{24,0},{28,4},{1,25},{... | collective-permute-start | bytes 393224 | tf_op jit(solution)/shard_map/ppermute | solution.py:134
  59.8 0.6 collective-permute-start.26
  60.3 3.0 %collective-permute-done.19 = bf16[256,256]{1,0:T(8,128)(2,1)S(1)} collective-permute-done((bf16[256,256]{1,0:T(8,128)(2,1)S(1)}, bf16[256,256]{1,0:T(8,128)(2,1)S(1)}, u32[]{:S(2)}, u32[]{:S(2)}) %collective-permute-start.19) | collective-permute-done | bytes 131104 | tf_op jit(solution)/shard_map/ppermute | solution.py:134
  63.3 2.5 %collective-permute-start.20 = (bf16[256,256]{1,0:T(8,128)(2,1)S(1)}, bf16[256,256]{1,0:T(8,128)(2,1)S(1)}, u32[]{:S(2)}, u32[]{:S(2)}) collective-permute-start(bf16[256,256]{1,0:T(8,128)(2,1)S(1)} %add_convert_fusion), channel_id=1, source_target_pairs={{0,3},{1,2},{2,1},{3,0},{4,7},{5,6},{6,5},{7,4},{8,11},{9,10},{10,... | collective-permute-start | bytes 393224 | tf_op jit(solution)/shard_map/ppermute | solution.py:134
  65.9 0.1 collective-permute-done.27
  66.0 1.4 %collective-permute-done.26 = bf16[256,256]{1,0:T(8,128)(2,1)S(1)} collective-permute-done((bf16[256,256]{1,0:T(8,128)(2,1)S(1)}, bf16[256,256]{1,0:T(8,128)(2,1)S(1)}, u32[]{:S(2)}, u32[]{:S(2)}) %collective-permute-start.26) | collective-permute-done | bytes 131104 | tf_op jit(solution)/shard_map/ppermute | solution.py:134
  67.3 3.0 %collective-permute-done.20 = bf16[256,256]{1,0:T(8,128)(2,1)S(1)} collective-permute-done((bf16[256,256]{1,0:T(8,128)(2,1)S(1)}, bf16[256,256]{1,0:T(8,128)(2,1)S(1)}, u32[]{:S(2)}, u32[]{:S(2)}) %collective-permute-start.20) | collective-permute-done | bytes 131104 | tf_op jit(solution)/shard_map/ppermute | solution.py:134
  70.3 0.8 %fusion.3 = bf16[256,256]{1,0:T(8,128)(2,1)} fusion(bf16[256,256]{1,0:T(8,128)(2,1)S(1)} %copy-done, f32[1024,256]{1,0:T(8,128)S(1)} %get-tuple-element.22, bf16[256,256]{1,0:T(8,128)(2,1)S(1)} %fusion.2.refs_0_, bf16[256,256]{1,0:T(8,128)(2,1)S(1)} %collective-permute-done.27, bf16[256,256]{1,0:T(8,128)(2,1)S(1)} %collective-permute-done.26, ...), kind=kLoop, calls=%fused_computation.9 | loop fusion | flops 1245184 | bytes 1441792 | tf_op jit(solution)/shard_map/convert_element_type | solution.py:263
  (16 shorter events, 0.2 us)
Async XLA Ops:
  0.0 9.9 %collective-permute-start.8 = (bf16[256,256]{1,0:T(8,128)(2,1)}, bf16[256,256]{1,0:T(8,128)(2,1)S(1)}, u32[]{:S(2)}, u32[]{:S(2)}) collective-permute-start(bf16[256,256]{1,0:T(8,128)(2,1)} %refs_0_.5), channel_id=1, source_target_pairs={{0,3},{1,2},{2,1},{3,0},{4,7},{5,6},{6,5},{7,4},{8,11},{9,10},{10,... | collective-permute-start | bytes 393224 | tf_op jit(solution)/shard_map/ppermute | solution.py:134
  5.1 15.5 %collective-permute-start.7 = (bf16[256,256]{1,0:T(8,128)(2,1)}, bf16[256,256]{1,0:T(8,128)(2,1)S(1)}, u32[]{:S(2)}, u32[]{:S(2)}) collective-permute-start(bf16[256,256]{1,0:T(8,128)(2,1)} %refs_0_.5), channel_id=1, source_target_pairs={{0,1},{1,0},{2,3},{3,2},{4,5},{5,4},{6,7},{7,6},{8,9},{9,8},{10,11... | collective-permute-start | bytes 393224 | tf_op jit(solution)/shard_map/ppermute | solution.py:134
  5.1 6.9 %collective-permute-start.2 = (bf16[256,256]{1,0:T(8,128)(2,1)}, bf16[256,256]{1,0:T(8,128)(2,1)S(1)}, u32[]{:S(2)}, u32[]{:S(2)}) collective-permute-start(bf16[256,256]{1,0:T(8,128)(2,1)} %refs_0_.5), channel_id=1, source_target_pairs={{0,24},{4,28},{8,16},{12,20},{16,8},{20,12},{24,0},{28,4},{1,25},{... | collective-permute-start | bytes 393224 | tf_op jit(solution)/shard_map/ppermute | solution.py:134
  7.5 6.4 %collective-permute-start.1 = (bf16[256,256]{1,0:T(8,128)(2,1)}, bf16[256,256]{1,0:T(8,128)(2,1)S(1)}, u32[]{:S(2)}, u32[]{:S(2)}) collective-permute-start(bf16[256,256]{1,0:T(8,128)(2,1)} %refs_0_.5), channel_id=1, source_target_pairs={{0,16},{4,20},{8,24},{12,28},{16,0},{20,4},{24,8},{28,12},{1,17},{... | collective-permute-start | bytes 393224 | tf_op jit(solution)/shard_map/ppermute | solution.py:134
  8.0 6.0 %collective-permute-start = (bf16[256,256]{1,0:T(8,128)(2,1)}, bf16[256,256]{1,0:T(8,128)(2,1)S(1)}, u32[]{:S(2)}, u32[]{:S(2)}) collective-permute-start(bf16[256,256]{1,0:T(8,128)(2,1)} %refs_0_.5), channel_id=1, source_target_pairs={{0,8},{4,12},{8,0},{12,4},{16,24},{20,28},{24,16},{28,20},{1,9},{5... | collective-permute-start | bytes 393224 | tf_op jit(solution)/shard_map/ppermute | solution.py:134
  9.9 10.7 %collective-permute-start.9 = (bf16[256,256]{1,0:T(8,128)(2,1)S(1)}, bf16[256,256]{1,0:T(8,128)(2,1)S(1)}, u32[]{:S(2)}, u32[]{:S(2)}) collective-permute-start(bf16[256,256]{1,0:T(8,128)(2,1)S(1)} %collective-permute-done.8.refs_3_), channel_id=1, source_target_pairs={{0,1},{1,0},{2,3},{3,2},{4,5},{5,4},{6,7},{7,6},{8,9},{9,8},{10,11... | collective-permute-start | bytes 393224 | tf_op jit(solution)/shard_map/ppermute | solution.py:134
  15.0 7.6 %collective-permute-start.3 = (bf16[1024,256]{1,0:T(8,128)(2,1)S(1)}, bf16[1024,256]{1,0:T(8,128)(2,1)S(1)}, u32[]{:S(2)}, u32[]{:S(2)}) collective-permute-start(bf16[1024,256]{1,0:T(8,128)(2,1)S(1)} %pad_maximum_fusion), channel_id=1, source_target_pairs={{0,4},{4,0},{8,12},{12,8},{16,20},{20,16},{24,28},{28,24},{1,5},{5... | collective-permute-start | bytes 1572872 | tf_op jit(solution)/shard_map/ppermute | solution.py:134
  15.1 1.9 %copy-start.1 = (bf16[96,128,128]{2,1,0:T(8,128)(2,1)S(1)}, bf16[96,128,128]{2,1,0:T(8,128)(2,1)}, u32[]{:S(2)}) copy-start(bf16[96,128,128]{2,1,0:T(8,128)(2,1)} %tiles_ref.1) | copy-start | bytes 9437188
  18.9 1.8 %copy-start = (bf16[256,256]{1,0:T(8,128)(2,1)S(1)}, bf16[256,256]{1,0:T(8,128)(2,1)}, u32[]{:S(2)}) copy-start(bf16[256,256]{1,0:T(8,128)(2,1)} %refs_0_.5) | copy-start | bytes 393220
  21.3 4.6 %collective-permute-start.10 = (bf16[1024,256]{1,0:T(8,128)(2,1)S(1)}, bf16[1024,256]{1,0:T(8,128)(2,1)S(1)}, u32[]{:S(2)}, u32[]{:S(2)}) collective-permute-start(bf16[1024,256]{1,0:T(8,128)(2,1)S(1)} %shard_map.57), channel_id=1, source_target_pairs={{0,4},{4,0},{8,12},{12,8},{16,20},{20,16},{24,28},{28,24},{1,5},{5... | collective-permute-start | bytes 1572872 | tf_op jit(solution)/shard_map/ppermute | solution.py:134
  23.9 9.0 %collective-permute-start.4 = (bf16[256,256]{1,0:T(8,128)(2,1)S(1)}, bf16[256,256]{1,0:T(8,128)(2,1)S(1)}, u32[]{:S(2)}, u32[]{:S(2)}) collective-permute-start(bf16[256,256]{1,0:T(8,128)(2,1)S(1)} %get-tuple-element.14), channel_id=1, source_target_pairs={{0,1},{1,0},{2,3},{3,2},{4,5},{5,4},{6,7},{7,6},{8,9},{9,8},{10,11... | collective-permute-start | bytes 393224 | tf_op jit(solution)/shard_map/ppermute | solution.py:134
  25.7 6.5 %collective-permute-start.5 = (bf16[256,256]{1,0:T(8,128)(2,1)S(1)}, bf16[256,256]{1,0:T(8,128)(2,1)S(1)}, u32[]{:S(2)}, u32[]{:S(2)}) collective-permute-start(bf16[256,256]{1,0:T(8,128)(2,1)S(1)} %get-tuple-element.16), channel_id=1, source_target_pairs={{0,1},{1,0},{2,3},{3,2},{4,5},{5,4},{6,7},{7,6},{8,9},{9,8},{10,11... | collective-permute-start | bytes 393224 | tf_op jit(solution)/shard_map/ppermute | solution.py:134
  26.2 6.7 %collective-permute-start.11 = (bf16[256,256]{1,0:T(8,128)(2,1)S(1)}, bf16[256,256]{1,0:T(8,128)(2,1)S(1)}, u32[]{:S(2)}, u32[]{:S(2)}) collective-permute-start(bf16[256,256]{1,0:T(8,128)(2,1)S(1)} %get-tuple-element.28), channel_id=1, source_target_pairs={{0,8},{4,12},{8,0},{12,4},{16,24},{20,28},{24,16},{28,20},{1,9},{5... | collective-permute-start | bytes 393224 | tf_op jit(solution)/shard_map/ppermute | solution.py:134
  27.8 7.2 %collective-permute-start.13 = (bf16[256,256]{1,0:T(8,128)(2,1)S(1)}, bf16[256,256]{1,0:T(8,128)(2,1)S(1)}, u32[]{:S(2)}, u32[]{:S(2)}) collective-permute-start(bf16[256,256]{1,0:T(8,128)(2,1)S(1)} %get-tuple-element.29), channel_id=1, source_target_pairs={{0,24},{4,28},{8,16},{12,20},{16,8},{20,12},{24,0},{28,4},{1,25},{... | collective-permute-start | bytes 393224 | tf_op jit(solution)/shard_map/ppermute | solution.py:134
  29.2 7.1 %collective-permute-start.12 = (bf16[256,256]{1,0:T(8,128)(2,1)S(1)}, bf16[256,256]{1,0:T(8,128)(2,1)S(1)}, u32[]{:S(2)}, u32[]{:S(2)}) collective-permute-start(bf16[256,256]{1,0:T(8,128)(2,1)S(1)} %get-tuple-element.30), channel_id=1, source_target_pairs={{0,16},{4,20},{8,24},{12,28},{16,0},{20,4},{24,8},{28,12},{1,17},{... | collective-permute-start | bytes 393224 | tf_op jit(solution)/shard_map/ppermute | solution.py:134
  32.2 6.8 %collective-permute-start.6 = (bf16[256,256]{1,0:T(8,128)(2,1)S(1)}, bf16[256,256]{1,0:T(8,128)(2,1)S(1)}, u32[]{:S(2)}, u32[]{:S(2)}) collective-permute-start(bf16[256,256]{1,0:T(8,128)(2,1)S(1)} %add_convert_fusion.1), channel_id=1, source_target_pairs={{0,3},{1,2},{2,1},{3,0},{4,7},{5,6},{6,5},{7,4},{8,11},{9,10},{10,... | collective-permute-start | bytes 393224 | tf_op jit(solution)/shard_map/ppermute | solution.py:134
  39.2 7.0 %collective-permute-start.22 = (bf16[256,256]{1,0:T(8,128)(2,1)S(1)}, bf16[256,256]{1,0:T(8,128)(2,1)S(1)}, u32[]{:S(2)}, u32[]{:S(2)}) collective-permute-start(bf16[256,256]{1,0:T(8,128)(2,1)S(1)} %fusion.2.refs_0_), channel_id=1, source_target_pairs={{0,3},{1,2},{2,1},{3,0},{4,7},{5,6},{6,5},{7,4},{8,11},{9,10},{10,... | collective-permute-start | bytes 393224 | tf_op jit(solution)/shard_map/ppermute | solution.py:134
  39.9 8.1 %collective-permute-start.16 = (bf16[256,256]{1,0:T(8,128)(2,1)S(1)}, bf16[256,256]{1,0:T(8,128)(2,1)S(1)}, u32[]{:S(2)}, u32[]{:S(2)}) collective-permute-start(bf16[256,256]{1,0:T(8,128)(2,1)S(1)} %fusion.2.refs_0_), channel_id=1, source_target_pairs={{0,24},{4,28},{8,16},{12,20},{16,8},{20,12},{24,0},{28,4},{1,25},{... | collective-permute-start | bytes 393224 | tf_op jit(solution)/shard_map/ppermute | solution.py:134
  41.5 6.5 %collective-permute-start.15 = (bf16[256,256]{1,0:T(8,128)(2,1)S(1)}, bf16[256,256]{1,0:T(8,128)(2,1)S(1)}, u32[]{:S(2)}, u32[]{:S(2)}) collective-permute-start(bf16[256,256]{1,0:T(8,128)(2,1)S(1)} %fusion.2.refs_0_), channel_id=1, source_target_pairs={{0,16},{4,20},{8,24},{12,28},{16,0},{20,4},{24,8},{28,12},{1,17},{... | collective-permute-start | bytes 393224 | tf_op jit(solution)/shard_map/ppermute | solution.py:134
  42.9 5.1 %collective-permute-start.14 = (bf16[256,256]{1,0:T(8,128)(2,1)S(1)}, bf16[256,256]{1,0:T(8,128)(2,1)S(1)}, u32[]{:S(2)}, u32[]{:S(2)}) collective-permute-start(bf16[256,256]{1,0:T(8,128)(2,1)S(1)} %fusion.2.refs_0_), channel_id=1, source_target_pairs={{0,8},{4,12},{8,0},{12,4},{16,24},{20,28},{24,16},{28,20},{1,9},{5... | collective-permute-start | bytes 393224 | tf_op jit(solution)/shard_map/ppermute | solution.py:134
  43.4 6.4 %collective-permute-start.21 = (bf16[256,256]{1,0:T(8,128)(2,1)S(1)}, bf16[256,256]{1,0:T(8,128)(2,1)S(1)}, u32[]{:S(2)}, u32[]{:S(2)}) collective-permute-start(bf16[256,256]{1,0:T(8,128)(2,1)S(1)} %fusion.2.refs_0_), channel_id=1, source_target_pairs={{0,1},{1,0},{2,3},{3,2},{4,5},{5,4},{6,7},{7,6},{8,9},{9,8},{10,11... | collective-permute-start | bytes 393224 | tf_op jit(solution)/shard_map/ppermute | solution.py:134
  46.2 5.5 %collective-permute-start.23 = (bf16[256,256]{1,0:T(8,128)(2,1)S(1)}, bf16[256,256]{1,0:T(8,128)(2,1)S(1)}, u32[]{:S(2)}, u32[]{:S(2)}) collective-permute-start(bf16[256,256]{1,0:T(8,128)(2,1)S(1)} %collective-permute-done.22.refs_3_), channel_id=1, source_target_pairs={{0,1},{1,0},{2,3},{3,2},{4,5},{5,4},{6,7},{7,6},{8,9},{9,8},{10,11... | collective-permute-start | bytes 393224 | tf_op jit(solution)/shard_map/ppermute | solution.py:134
  48.0 5.2 %collective-permute-start.17 = (bf16[1024,256]{1,0:T(8,128)(2,1)S(1)}, bf16[1024,256]{1,0:T(8,128)(2,1)S(1)}, u32[]{:S(2)}, u32[]{:S(2)}) collective-permute-start(bf16[1024,256]{1,0:T(8,128)(2,1)S(1)} %pad_maximum_fusion.1), channel_id=1, source_target_pairs={{0,4},{4,0},{8,12},{12,8},{16,20},{20,16},{24,28},{28,24},{1,5},{5... | collective-permute-start | bytes 1572872 | tf_op jit(solution)/shard_map/ppermute | solution.py:134
  52.5 4.2 %collective-permute-start.24 = (bf16[1024,256]{1,0:T(8,128)(2,1)S(1)}, bf16[1024,256]{1,0:T(8,128)(2,1)S(1)}, u32[]{:S(2)}, u32[]{:S(2)}) collective-permute-start(bf16[1024,256]{1,0:T(8,128)(2,1)S(1)} %shard_map.60), channel_id=1, source_target_pairs={{0,4},{4,0},{8,12},{12,8},{16,20},{20,16},{24,28},{28,24},{1,5},{5... | collective-permute-start | bytes 1572872 | tf_op jit(solution)/shard_map/ppermute | solution.py:134
  54.5 11.3 %collective-permute-start.18 = (bf16[256,256]{1,0:T(8,128)(2,1)S(1)}, bf16[256,256]{1,0:T(8,128)(2,1)S(1)}, u32[]{:S(2)}, u32[]{:S(2)}) collective-permute-start(bf16[256,256]{1,0:T(8,128)(2,1)S(1)} %get-tuple-element.18), channel_id=1, source_target_pairs={{0,1},{1,0},{2,3},{3,2},{4,5},{5,4},{6,7},{7,6},{8,9},{9,8},{10,11... | collective-permute-start | bytes 393224 | tf_op jit(solution)/shard_map/ppermute | solution.py:134
  55.8 7.5 %collective-permute-start.19 = (bf16[256,256]{1,0:T(8,128)(2,1)S(1)}, bf16[256,256]{1,0:T(8,128)(2,1)S(1)}, u32[]{:S(2)}, u32[]{:S(2)}) collective-permute-start(bf16[256,256]{1,0:T(8,128)(2,1)S(1)} %get-tuple-element.20), channel_id=1, source_target_pairs={{0,1},{1,0},{2,3},{3,2},{4,5},{5,4},{6,7},{7,6},{8,9},{9,8},{10,11... | collective-permute-start | bytes 393224 | tf_op jit(solution)/shard_map/ppermute | solution.py:134
  56.8 9.1 %collective-permute-start.25 = (bf16[256,256]{1,0:T(8,128)(2,1)S(1)}, bf16[256,256]{1,0:T(8,128)(2,1)S(1)}, u32[]{:S(2)}, u32[]{:S(2)}) collective-permute-start(bf16[256,256]{1,0:T(8,128)(2,1)S(1)} %get-tuple-element.25), channel_id=1, source_target_pairs={{0,8},{4,12},{8,0},{12,4},{16,24},{20,28},{24,16},{28,20},{1,9},{5... | collective-permute-start | bytes 393224 | tf_op jit(solution)/shard_map/ppermute | solution.py:134
  58.4 7.6 %collective-permute-start.27 = (bf16[256,256]{1,0:T(8,128)(2,1)S(1)}, bf16[256,256]{1,0:T(8,128)(2,1)S(1)}, u32[]{:S(2)}, u32[]{:S(2)}) collective-permute-start(bf16[256,256]{1,0:T(8,128)(2,1)S(1)} %get-tuple-element.26), channel_id=1, source_target_pairs={{0,24},{4,28},{8,16},{12,20},{16,8},{20,12},{24,0},{28,4},{1,25},{... | collective-permute-start | bytes 393224 | tf_op jit(solution)/shard_map/ppermute | solution.py:134
  59.8 7.6 %collective-permute-start.26 = (bf16[256,256]{1,0:T(8,128)(2,1)S(1)}, bf16[256,256]{1,0:T(8,128)(2,1)S(1)}, u32[]{:S(2)}, u32[]{:S(2)}) collective-permute-start(bf16[256,256]{1,0:T(8,128)(2,1)S(1)} %get-tuple-element.27), channel_id=1, source_target_pairs={{0,16},{4,20},{8,24},{12,28},{16,0},{20,4},{24,8},{28,12},{1,17},{... | collective-permute-start | bytes 393224 | tf_op jit(solution)/shard_map/ppermute | solution.py:134
  63.3 7.0 %collective-permute-start.20 = (bf16[256,256]{1,0:T(8,128)(2,1)S(1)}, bf16[256,256]{1,0:T(8,128)(2,1)S(1)}, u32[]{:S(2)}, u32[]{:S(2)}) collective-permute-start(bf16[256,256]{1,0:T(8,128)(2,1)S(1)} %add_convert_fusion), channel_id=1, source_target_pairs={{0,3},{1,2},{2,1},{3,0},{4,7},{5,6},{6,5},{7,4},{8,11},{9,10},{10,... | collective-permute-start | bytes 393224 | tf_op jit(solution)/shard_map/ppermute | solution.py:134

commit v3 on v2

--- a/solution.py
+++ b/solution.py
@@ -93,13 +93,13 @@
     )(matrix)
 
 
-def product_kernel(n_in, start, m_ref, *refs):
-    panels, outs = refs[:n_in], refs[n_in:]
-    done = start
-    for out in outs:
+def product_kernel(n_in, starts, left, added, m_ref, *refs):
+    panels, outs = refs[:n_in], refs[n_in + added :]
+    for start, out in zip(starts, outs):
         for top in range(0, out.shape[0], 256):
-            total = None
-            at = 0
+            done = start + top
+            total = refs[n_in][done : done + 256, :] if added else None
+            at = left
             for panel in panels:
                 rows = panel.shape[0]
                 term = jnp.dot(
@@ -110,24 +110,28 @@
                 total = term if total is None else total + term
                 at += rows
             out[top : top + 256, :] = total.astype(out.dtype)
-            done += 256
-
-
-def product(matrix, panels, start, out_rows):
+
+
+def product(matrix, panels, pieces, left=0, added=None, dtype=jnp.bfloat16):
     width = panels[0].shape[1]
+    depth = sum(panel.shape[0] for panel in panels)
+    height = sum(rows for _, rows in pieces)
+    extra = [] if added is None else [added]
     vmem = pl.BlockSpec(memory_space=pltpu.VMEM)
     return pl.pallas_call(
-        functools.partial(product_kernel, len(panels), start),
-        out_shape=tuple(jax.ShapeDtypeStruct((rows, width), jnp.bfloat16) for rows in out_rows),
-        in_specs=[vmem] * (1 + len(panels)),
-        out_specs=tuple(vmem for _ in out_rows),
+        functools.partial(
+            product_kernel, len(panels), [first for first, _ in pieces], left, len(extra)
+        ),
+        out_shape=tuple(jax.ShapeDtypeStruct((rows, width), dtype) for _, rows in pieces),
+        in_specs=[vmem] * (1 + len(panels) + len(extra)),
+        out_specs=tuple(vmem for _ in pieces),
         compiler_params=pltpu.CompilerParams(vmem_limit_bytes=16 * MIB),
         cost_estimate=pl.CostEstimate(
-            flops=2 * sum(out_rows) * matrix.shape[1] * width,
+            flops=2 * height * depth * width,
             transcendentals=0,
-            bytes_accessed=2 * (sum(out_rows) * (matrix.shape[1] + width) + matrix.shape[1] * width),
-        ),
-    )(matrix, *panels)
+            bytes_accessed=2 * (height * (depth + width) + depth * width),
+        ),
+    )(matrix, *panels, *extra)
 
 
 def swap(x, axis, j):
@@ -155,14 +159,22 @@
         range_panels[j] = swap(range_panels[j ^ last], "col", last)
     near = [panel] + [swap(panel, "row", 2 * k) for k in range(1, half)]
     far = swap(jnp.concatenate(near), "row", 1)
-    upper = list(product(matrix, near + [far], 0, [rows] * n_cols))
+    (begun,) = product(matrix, near, [(0, n_cols * rows)], dtype=jnp.float32)
+    upper = [None] * n_cols
+    early = [j for j in by_hops if len(hops(j)) == len(hops(by_hops[-1]))]
+    late = [j for j in range(n_cols) if j not in early]
+    for units in (early, late):
+        pieces = [(j * rows, rows) for j in units]
+        done = product(matrix, [far], pieces, half * rows, begun)
+        for j, unit in zip(units, done):
+            upper[j] = unit
     for j in reversed(by_hops):
         last = hops(j)[-1]
         part = swap(upper[j].astype(jnp.bfloat16), "col", last)
         upper[j ^ last] = upper[j ^ last].astype(jnp.float32) + part.astype(jnp.float32)
     own = upper[0].astype(jnp.float32)
-    (give,) = product(matrix_t, range_panels, half * rows, [half * rows])
-    (keep,) = product(matrix_t, range_panels, 0, [half * rows])
+    (give,) = product(matrix_t, range_panels, [(half * rows, half * rows)])
+    (keep,) = product(matrix_t, range_panels, [(0, half * rows)])
     paired = keep.astype(jnp.float32) + swap(give, "row", 1).astype(jnp.float32)
     paired = paired.reshape(half, rows, width)
     own += paired[0]

time: 71.3 us -> 69 us (0.968)
  waiting for transfers between devices: 22.6 us -> 19.7 us
  other arithmetic: 3.08 us -> 2.16 us
  starting transfers between devices: 33.8 us -> 34.6 us
    ppermute x28, waiting for transfers between devices: 22.6 us -> 19.7 us  [swap(): lax.ppermute(x, axis, [(i, i ^ j) for i in range(lax.axis_size(axis))])]
    concatenate x2, other arithmetic: 0.98 us -> 0.07 us  [apply_dense(): far = swap(jnp.concatenate(near), 'row', 1)]
    ppermute x28, starting transfers between devices: 33.8 us -> 34.6 us  [swap(): lax.ppermute(x, axis, [(i, i ^ j) for i in range(lax.axis_size(axis))])]
    pallas_call x6 -> x10, Pallas kernels: 5.32 us -> 5.98 us  [product(): pl.pallas_call(functools.partial(product_kernel, len(panels), [first for...]
  transfers between devices with their start and end apart: 28 -> 28, of which waited for: 13 -> 12; matrix products, arithmetic and copies ran while one was open for 3% -> 2% of each run, Pallas kernels for 12% -> 14%
where the time goes in v3:
time: 69 us; the launch traced here: 68.8 us
  starting transfers between devices  34.6 us (50%)
  waiting for transfers between devices  19.7 us (29%)
  Pallas kernels  9.49 us (14%)
  other arithmetic  2.16 us (3%)
  local copies, waits for them, and re-layouts  1.94 us (3%)
  between operations  0.93 us (1%)
    ppermute x28, starting transfers between devices, swap(): lax.ppermute(x, axis, [(i, i ^ j) for i in range(lax.axis_size(axis))])  34.6 us
    ppermute x28, waiting for transfers between devices, swap(): lax.ppermute(x, axis, [(i, i ^ j) for i in range(lax.axis_size(axis))])  19.7 us
    pallas_call x10, Pallas kernels, product(): pl.pallas_call(functools.partial(product_kernel, len(panels), [first for...  5.98 us
    unnamed x4, local copies, waits for them, and re-layouts  1.89 us
    pallas_call x1, Pallas kernels, densify(): pl.pallas_call(densify_kernel, out_shape=jax.ShapeDtypeStruct((height, br...  1.81 us
    pallas_call x1, Pallas kernels, transpose(): pl.pallas_call(transpose_kernel, out_shape=jax.ShapeDtypeStruct((breadth,...  1.71 us
  transfers between devices with their start and end apart: 28, of which 12 were waited for; matrix products, arithmetic and copies ran while one was open for 2% of the time, Pallas kernels for 14%

profile of v3, /device:TPU:0, one launch (start us, length us, event | category | flops | bytes accessed | tf_op | source)
XLA Modules:
  0.0 68.8 jit_solution(9721956637086725132)
XLA Ops:
  0.0 5.1 %collective-permute-start.8 = (bf16[256,256]{1,0:T(8,128)(2,1)}, bf16[256,256]{1,0:T(8,128)(2,1)S(1)}, u32[]{:S(2)}, u32[]{:S(2)}) collective-permute-start(bf16[256,256]{1,0:T(8,128)(2,1)} %refs_0_.5), channel_id=1, source_target_pairs={{0,3},{1,2},{2,1},{3,0},{4,7},{5,6},{6,5},{7,4},{8,11},{9,10},{10,... | collective-permute-start | bytes 393224 | tf_op jit(solution)/shard_map/ppermute | solution.py:138
  5.1 0.0 collective-permute-start.7
  5.1 2.4 %collective-permute-start.2 = (bf16[256,256]{1,0:T(8,128)(2,1)}, bf16[256,256]{1,0:T(8,128)(2,1)S(1)}, u32[]{:S(2)}, u32[]{:S(2)}) collective-permute-start(bf16[256,256]{1,0:T(8,128)(2,1)} %refs_0_.5), channel_id=1, source_target_pairs={{0,24},{4,28},{8,16},{12,20},{16,8},{20,12},{24,0},{28,4},{1,25},{... | collective-permute-start | bytes 393224 | tf_op jit(solution)/shard_map/ppermute | solution.py:138
  7.5 0.5 collective-permute-start.1
  8.0 0.5 collective-permute-start
  9.2 0.7 %compare_select_fusion = s32[96]{0:T(128)S(1)} fusion(s32[96]{0:T(128)} %param.8, s32[96]{0:T(128)} %param.7, s32[]{:T(128)S(6)} %axis_index.23, s32[]{:T(128)S(6)} %axis_index.25, s32[]{:T(128)S(6)} %mul.29, s32[]{:T(128)} %bitcast.1), kind=kLoop, calls=%fused_computation.30 | loop fusion | flops 7104 | bytes 1168 | tf_op jit(solution)/shard_map/jit(_where)/select_n | solution.py:35
  9.9 2.1 %collective-permute-start.9 = (bf16[256,256]{1,0:T(8,128)(2,1)S(1)}, bf16[256,256]{1,0:T(8,128)(2,1)S(1)}, u32[]{:S(2)}, u32[]{:S(2)}) collective-permute-start(bf16[256,256]{1,0:T(8,128)(2,1)S(1)} %collective-permute-done.8.refs_3_), channel_id=1, source_target_pairs={{0,1},{1,0},{2,3},{3,2},{4,5},{5,4},{6,7},{7,6},{8,9},{9,8},{10,11... | collective-permute-start | bytes 393224 | tf_op jit(solution)/shard_map/ppermute | solution.py:138
  12.0 0.1 select_reduce_fusion.table
  12.1 0.0 copy-start.1
  12.1 1.9 %copy-done.1 = bf16[96,128,128]{2,1,0:T(8,128)(2,1)S(1)} copy-done((bf16[96,128,128]{2,1,0:T(8,128)(2,1)S(1)}, bf16[96,128,128]{2,1,0:T(8,128)(2,1)}, u32[]{:S(2)}) %copy-start.1) | copy-done | bytes 3145752
  14.0 1.8 %densify.1.m_ref.a_ref = bf16[1024,2048]{1,0:T(8,128)(2,1)S(1)} custom-call(s32[128]{0:T(128)S(1)} %select_reduce_fusion.table, bf16[96,128,128]{2,1,0:T(8,128)(2,1)S(1)} %copy-done.1), custom_call_target="tpu_custom_call" | custom-call | bytes 7340032 | tf_op jit(solution)/shard_map/densify/pallas_call | solution.py:57
  15.8 0.0 collective-permute-done.1.refs_2_
  15.8 0.0 collective-permute-done.refs_1_
  15.9 0.1 collective-permute-start.3
  16.0 1.7 %mirror.1.m_ref = bf16[2048,1024]{1,0:T(8,128)(2,1)S(1)} custom-call(bf16[1024,2048]{1,0:T(8,128)(2,1)S(1)} %densify.1.m_ref.a_ref), custom_call_target="tpu_custom_call" | custom-call | bytes 8388608 | tf_op jit(solution)/shard_map/mirror/pallas_call | solution.py:83
  17.7 0.0 collective-permute-done.9.refs_2_
  17.7 0.7 %shard_map.59 = bf16[1024,256]{1,0:T(8,128)(2,1)S(1)} custom-call(bf16[2048,1024]{1,0:T(8,128)(2,1)S(1)} %mirror.1.m_ref, bf16[256,256]{1,0:T(8,128)(2,1)S(1)} %copy-done, bf16[256,256]{1,0:T(8,128)(2,1)S(1)} %collective-permute-done.7.refs_1_, bf16[256,256]{1,0:T(8,128)(2,1)S(1)} %collective-permute-done.9.refs_2_, ...), custom_call_target="tpu_custom_call" | custom-call | flops 536870912 | bytes 3145728 | tf_op jit(solution)/shard_map/pallas_call | solution.py:121
  18.4 0.6 collective-permute-start.10
  19.0 0.7 %shard_map.55.refs_1_ = f32[1024,256]{1,0:T(8,128)S(1)} custom-call(bf16[1024,2048]{1,0:T(8,128)(2,1)S(1)} %densify.1.m_ref.a_ref, bf16[256,256]{1,0:T(8,128)(2,1)S(1)} %copy-done, bf16[256,256]{1,0:T(8,128)(2,1)S(1)} %collective-permute-done.refs_1_, bf16[256,256]{1,0:T(8,128)(2,1)S(1)} %collective-permute-done.1.refs_2_, ...), custom_call_target="tpu_custom_call" | custom-call | flops 536870912 | bytes 3145728 | tf_op jit(solution)/shard_map/pallas_call | solution.py:121
  19.7 0.7 %shard_map.58 = bf16[1024,256]{1,0:T(8,128)(2,1)S(1)} custom-call(bf16[2048,1024]{1,0:T(8,128)(2,1)S(1)} %mirror.1.m_ref, bf16[256,256]{1,0:T(8,128)(2,1)S(1)} %copy-done, bf16[256,256]{1,0:T(8,128)(2,1)S(1)} %collective-permute-done.7.refs_1_, bf16[256,256]{1,0:T(8,128)(2,1)S(1)} %collective-permute-done.9.refs_2_, ...), custom_call_target="tpu_custom_call" | custom-call | flops 536870912 | bytes 3145728 | tf_op jit(solution)/shard_map/pallas_call | solution.py:121
  20.4 0.0 collective-permute-done.3.refs_0_
  20.4 0.6 shard_map.56
  21.0 0.1 collective-permute-start.4
  21.1 0.3 shard_map.57
  21.4 2.1 %collective-permute-start.5 = (bf16[256,256]{1,0:T(8,128)(2,1)S(1)}, bf16[256,256]{1,0:T(8,128)(2,1)S(1)}, u32[]{:S(2)}, u32[]{:S(2)}) collective-permute-start(bf16[256,256]{1,0:T(8,128)(2,1)S(1)} %shard_map.57), channel_id=1, source_target_pairs={{0,1},{1,0},{2,3},{3,2},{4,5},{5,4},{6,7},{7,6},{8,9},{9,8},{10,11... | collective-permute-start | bytes 393224 | tf_op jit(solution)/shard_map/ppermute | solution.py:138
  23.5 0.1 fusion.16
  23.7 1.6 %collective-permute-start.11 = (bf16[256,256]{1,0:T(8,128)(2,1)S(1)}, bf16[256,256]{1,0:T(8,128)(2,1)S(1)}, u32[]{:S(2)}, u32[]{:S(2)}) collective-permute-start(bf16[256,256]{1,0:T(8,128)(2,1)S(1)} %get-tuple-element.24), channel_id=1, source_target_pairs={{0,8},{4,12},{8,0},{12,4},{16,24},{20,28},{24,16},{28,20},{1,9},{5... | collective-permute-start | bytes 393224 | tf_op jit(solution)/shard_map/ppermute | solution.py:138
  25.2 1.5 %collective-permute-start.13 = (bf16[256,256]{1,0:T(8,128)(2,1)S(1)}, bf16[256,256]{1,0:T(8,128)(2,1)S(1)}, u32[]{:S(2)}, u32[]{:S(2)}) collective-permute-start(bf16[256,256]{1,0:T(8,128)(2,1)S(1)} %get-tuple-element.25), channel_id=1, source_target_pairs={{0,24},{4,28},{8,16},{12,20},{16,8},{20,12},{24,0},{28,4},{1,25},{... | collective-permute-start | bytes 393224 | tf_op jit(solution)/shard_map/ppermute | solution.py:138
  26.7 0.5 collective-permute-start.12
  27.2 2.1 %collective-permute-done.5 = bf16[256,256]{1,0:T(8,128)(2,1)S(1)} collective-permute-done((bf16[256,256]{1,0:T(8,128)(2,1)S(1)}, bf16[256,256]{1,0:T(8,128)(2,1)S(1)}, u32[]{:S(2)}, u32[]{:S(2)}) %collective-permute-start.5) | collective-permute-done | bytes 131104 | tf_op jit(solution)/shard_map/ppermute | solution.py:138
  29.3 1.8 %collective-permute-start.6 = (bf16[256,256]{1,0:T(8,128)(2,1)S(1)}, bf16[256,256]{1,0:T(8,128)(2,1)S(1)}, u32[]{:S(2)}, u32[]{:S(2)}) collective-permute-start(bf16[256,256]{1,0:T(8,128)(2,1)S(1)} %add_convert_fusion.1), channel_id=1, source_target_pairs={{0,3},{1,2},{2,1},{3,0},{4,7},{5,6},{6,5},{7,4},{8,11},{9,10},{10,... | collective-permute-start | bytes 393224 | tf_op jit(solution)/shard_map/ppermute | solution.py:138
  31.1 1.2 %collective-permute-done.13 = bf16[256,256]{1,0:T(8,128)(2,1)S(1)} collective-permute-done((bf16[256,256]{1,0:T(8,128)(2,1)S(1)}, bf16[256,256]{1,0:T(8,128)(2,1)S(1)}, u32[]{:S(2)}, u32[]{:S(2)}) %collective-permute-start.13) | collective-permute-done | bytes 131104 | tf_op jit(solution)/shard_map/ppermute | solution.py:138
  32.3 1.4 %collective-permute-done.12 = bf16[256,256]{1,0:T(8,128)(2,1)S(1)} collective-permute-done((bf16[256,256]{1,0:T(8,128)(2,1)S(1)}, bf16[256,256]{1,0:T(8,128)(2,1)S(1)}, u32[]{:S(2)}, u32[]{:S(2)}) %collective-permute-start.12) | collective-permute-done | bytes 131104 | tf_op jit(solution)/shard_map/ppermute | solution.py:138
  33.7 2.4 %collective-permute-done.6 = bf16[256,256]{1,0:T(8,128)(2,1)S(1)} collective-permute-done((bf16[256,256]{1,0:T(8,128)(2,1)S(1)}, bf16[256,256]{1,0:T(8,128)(2,1)S(1)}, u32[]{:S(2)}, u32[]{:S(2)}) %collective-permute-start.6) | collective-permute-done | bytes 131104 | tf_op jit(solution)/shard_map/ppermute | solution.py:138
  36.2 0.1 fusion.2.refs_0_
  36.3 1.8 %collective-permute-start.22 = (bf16[256,256]{1,0:T(8,128)(2,1)S(1)}, bf16[256,256]{1,0:T(8,128)(2,1)S(1)}, u32[]{:S(2)}, u32[]{:S(2)}) collective-permute-start(bf16[256,256]{1,0:T(8,128)(2,1)S(1)} %fusion.2.refs_0_), channel_id=1, source_target_pairs={{0,3},{1,2},{2,1},{3,0},{4,7},{5,6},{6,5},{7,4},{8,11},{9,10},{10,... | collective-permute-start | bytes 393224 | tf_op jit(solution)/shard_map/ppermute | solution.py:138
  38.1 2.4 %collective-permute-start.16 = (bf16[256,256]{1,0:T(8,128)(2,1)S(1)}, bf16[256,256]{1,0:T(8,128)(2,1)S(1)}, u32[]{:S(2)}, u32[]{:S(2)}) collective-permute-start(bf16[256,256]{1,0:T(8,128)(2,1)S(1)} %fusion.2.refs_0_), channel_id=1, source_target_pairs={{0,24},{4,28},{8,16},{12,20},{16,8},{20,12},{24,0},{28,4},{1,25},{... | collective-permute-start | bytes 393224 | tf_op jit(solution)/shard_map/ppermute | solution.py:138
  40.6 0.5 collective-permute-start.15
  41.1 0.5 collective-permute-start.14
  41.6 1.4 %collective-permute-start.21 = (bf16[256,256]{1,0:T(8,128)(2,1)S(1)}, bf16[256,256]{1,0:T(8,128)(2,1)S(1)}, u32[]{:S(2)}, u32[]{:S(2)}) collective-permute-start(bf16[256,256]{1,0:T(8,128)(2,1)S(1)} %fusion.2.refs_0_), channel_id=1, source_target_pairs={{0,1},{1,0},{2,3},{3,2},{4,5},{5,4},{6,7},{7,6},{8,9},{9,8},{10,11... | collective-permute-start | bytes 393224 | tf_op jit(solution)/shard_map/ppermute | solution.py:138
  43.1 0.4 collective-permute-done.22.refs_3_
  43.5 1.6 %collective-permute-start.23 = (bf16[256,256]{1,0:T(8,128)(2,1)S(1)}, bf16[256,256]{1,0:T(8,128)(2,1)S(1)}, u32[]{:S(2)}, u32[]{:S(2)}) collective-permute-start(bf16[256,256]{1,0:T(8,128)(2,1)S(1)} %collective-permute-done.22.refs_3_), channel_id=1, source_target_pairs={{0,1},{1,0},{2,3},{3,2},{4,5},{5,4},{6,7},{7,6},{8,9},{9,8},{10,11... | collective-permute-start | bytes 393224 | tf_op jit(solution)/shard_map/ppermute | solution.py:138
  45.1 1.1 %collective-permute-done.15.refs_2_ = bf16[256,256]{1,0:T(8,128)(2,1)S(1)} collective-permute-done((bf16[256,256]{1,0:T(8,128)(2,1)S(1)}, bf16[256,256]{1,0:T(8,128)(2,1)S(1)}, u32[]{:S(2)}, u32[]{:S(2)}) %collective-permute-start.15) | collective-permute-done | bytes 131104 | tf_op jit(solution)/shard_map/ppermute | solution.py:138
  46.2 0.1 collective-permute-start.17
  46.3 1.5 %collective-permute-done.21.refs_1_ = bf16[256,256]{1,0:T(8,128)(2,1)S(1)} collective-permute-done((bf16[256,256]{1,0:T(8,128)(2,1)S(1)}, bf16[256,256]{1,0:T(8,128)(2,1)S(1)}, u32[]{:S(2)}, u32[]{:S(2)}) %collective-permute-start.21) | collective-permute-done | bytes 131104 | tf_op jit(solution)/shard_map/ppermute | solution.py:138
  47.8 1.6 %collective-permute-done.23.refs_2_ = bf16[256,256]{1,0:T(8,128)(2,1)S(1)} collective-permute-done((bf16[256,256]{1,0:T(8,128)(2,1)S(1)}, bf16[256,256]{1,0:T(8,128)(2,1)S(1)}, u32[]{:S(2)}, u32[]{:S(2)}) %collective-permute-start.23) | collective-permute-done | bytes 131104 | tf_op jit(solution)/shard_map/ppermute | solution.py:138
  49.4 0.7 %shard_map.64 = bf16[1024,256]{1,0:T(8,128)(2,1)S(1)} custom-call(bf16[2048,1024]{1,0:T(8,128)(2,1)S(1)} %mirror.1.m_ref, bf16[256,256]{1,0:T(8,128)(2,1)S(1)} %fusion.2.refs_0_, bf16[256,256]{1,0:T(8,128)(2,1)S(1)} %collective-permute-done.21.refs_1_, bf16[256,256]{1,0:T(8,128)(2,1)S(1)} %collective-permute-done.23.refs_2_, ...), custom_call_target="tpu_custom_call" | custom-call | flops 536870912 | bytes 3145728 | tf_op jit(solution)/shard_map/pallas_call | solution.py:121
  50.1 0.1 collective-permute-start.24
  50.2 0.7 %shard_map.60.refs_1_ = f32[1024,256]{1,0:T(8,128)S(1)} custom-call(bf16[1024,2048]{1,0:T(8,128)(2,1)S(1)} %densify.1.m_ref.a_ref, bf16[256,256]{1,0:T(8,128)(2,1)S(1)} %fusion.2.refs_0_, bf16[256,256]{1,0:T(8,128)(2,1)S(1)} %collective-permute-done.14.refs_1_, bf16[256,256]{1,0:T(8,128)(2,1)S(1)} %collective-permute-done.15.refs_2_, ...), custom_call_target="tpu_custom_call" | custom-call | flops 536870912 | bytes 3145728 | tf_op jit(solution)/shard_map/pallas_call | solution.py:121
  50.9 0.7 %shard_map.63 = bf16[1024,256]{1,0:T(8,128)(2,1)S(1)} custom-call(bf16[2048,1024]{1,0:T(8,128)(2,1)S(1)} %mirror.1.m_ref, bf16[256,256]{1,0:T(8,128)(2,1)S(1)} %fusion.2.refs_0_, bf16[256,256]{1,0:T(8,128)(2,1)S(1)} %collective-permute-done.21.refs_1_, bf16[256,256]{1,0:T(8,128)(2,1)S(1)} %collective-permute-done.23.refs_2_, ...), custom_call_target="tpu_custom_call" | custom-call | flops 536870912 | bytes 3145728 | tf_op jit(solution)/shard_map/pallas_call | solution.py:121
  51.6 0.6 shard_map.61
  52.2 1.5 %collective-permute-start.18 = (bf16[256,256]{1,0:T(8,128)(2,1)S(1)}, bf16[256,256]{1,0:T(8,128)(2,1)S(1)}, u32[]{:S(2)}, u32[]{:S(2)}) collective-permute-start(bf16[256,256]{1,0:T(8,128)(2,1)S(1)} %get-tuple-element.15), channel_id=1, source_target_pairs={{0,1},{1,0},{2,3},{3,2},{4,5},{5,4},{6,7},{7,6},{8,9},{9,8},{10,11... | collective-permute-start | bytes 393224 | tf_op jit(solution)/shard_map/ppermute | solution.py:138
  53.7 0.3 shard_map.62
  54.0 0.6 collective-permute-start.19
  54.7 0.1 fusion.17
  54.8 1.6 %collective-permute-start.25 = (bf16[256,256]{1,0:T(8,128)(2,1)S(1)}, bf16[256,256]{1,0:T(8,128)(2,1)S(1)}, u32[]{:S(2)}, u32[]{:S(2)}) collective-permute-start(bf16[256,256]{1,0:T(8,128)(2,1)S(1)} %get-tuple-element.21), channel_id=1, source_target_pairs={{0,8},{4,12},{8,0},{12,4},{16,24},{20,28},{24,16},{28,20},{1,9},{5... | collective-permute-start | bytes 393224 | tf_op jit(solution)/shard_map/ppermute | solution.py:138
  56.4 1.5 %collective-permute-start.27 = (bf16[256,256]{1,0:T(8,128)(2,1)S(1)}, bf16[256,256]{1,0:T(8,128)(2,1)S(1)}, u32[]{:S(2)}, u32[]{:S(2)}) collective-permute-start(bf16[256,256]{1,0:T(8,128)(2,1)S(1)} %get-tuple-element.22), channel_id=1, source_target_pairs={{0,24},{4,28},{8,16},{12,20},{16,8},{20,12},{24,0},{28,4},{1,25},{... | collective-permute-start | bytes 393224 | tf_op jit(solution)/shard_map/ppermute | solution.py:138
  57.9 0.5 collective-permute-start.26
  58.4 2.6 %collective-permute-done.19 = bf16[256,256]{1,0:T(8,128)(2,1)S(1)} collective-permute-done((bf16[256,256]{1,0:T(8,128)(2,1)S(1)}, bf16[256,256]{1,0:T(8,128)(2,1)S(1)}, u32[]{:S(2)}, u32[]{:S(2)}) %collective-permute-start.19) | collective-permute-done | bytes 131104 | tf_op jit(solution)/shard_map/ppermute | solution.py:138
  61.0 1.6 %collective-permute-start.20 = (bf16[256,256]{1,0:T(8,128)(2,1)S(1)}, bf16[256,256]{1,0:T(8,128)(2,1)S(1)}, u32[]{:S(2)}, u32[]{:S(2)}) collective-permute-start(bf16[256,256]{1,0:T(8,128)(2,1)S(1)} %add_convert_fusion), channel_id=1, source_target_pairs={{0,3},{1,2},{2,1},{3,0},{4,7},{5,6},{6,5},{7,4},{8,11},{9,10},{10,... | collective-permute-start | bytes 393224 | tf_op jit(solution)/shard_map/ppermute | solution.py:138
  62.6 1.5 %collective-permute-done.27 = bf16[256,256]{1,0:T(8,128)(2,1)S(1)} collective-permute-done((bf16[256,256]{1,0:T(8,128)(2,1)S(1)}, bf16[256,256]{1,0:T(8,128)(2,1)S(1)}, u32[]{:S(2)}, u32[]{:S(2)}) %collective-permute-start.27) | collective-permute-done | bytes 131104 | tf_op jit(solution)/shard_map/ppermute | solution.py:138
  64.1 1.4 %collective-permute-done.26 = bf16[256,256]{1,0:T(8,128)(2,1)S(1)} collective-permute-done((bf16[256,256]{1,0:T(8,128)(2,1)S(1)}, bf16[256,256]{1,0:T(8,128)(2,1)S(1)}, u32[]{:S(2)}, u32[]{:S(2)}) %collective-permute-start.26) | collective-permute-done | bytes 131104 | tf_op jit(solution)/shard_map/ppermute | solution.py:138
  65.5 2.5 %collective-permute-done.20 = bf16[256,256]{1,0:T(8,128)(2,1)S(1)} collective-permute-done((bf16[256,256]{1,0:T(8,128)(2,1)S(1)}, bf16[256,256]{1,0:T(8,128)(2,1)S(1)}, u32[]{:S(2)}, u32[]{:S(2)}) %collective-permute-start.20) | collective-permute-done | bytes 131104 | tf_op jit(solution)/shard_map/ppermute | solution.py:138
  68.0 0.8 %fusion.3 = bf16[256,256]{1,0:T(8,128)(2,1)} fusion(bf16[256,256]{1,0:T(8,128)(2,1)S(1)} %copy-done, f32[1024,256]{1,0:T(8,128)S(1)} %get-tuple-element.18, bf16[256,256]{1,0:T(8,128)(2,1)S(1)} %fusion.2.refs_0_, bf16[256,256]{1,0:T(8,128)(2,1)S(1)} %collective-permute-done.27, bf16[256,256]{1,0:T(8,128)(2,1)S(1)} %collective-permute-done.26, ...), kind=kLoop, calls=%fused_computation.9 | loop fusion | flops 1245184 | bytes 1441792 | tf_op jit(solution)/shard_map/convert_element_type | solution.py:275
  (20 shorter events, 0.2 us)
Async XLA Ops:
  0.0 15.9 %copy-start = (bf16[256,256]{1,0:T(8,128)(2,1)S(1)}, bf16[256,256]{1,0:T(8,128)(2,1)}, u32[]{:S(2)}) copy-start(bf16[256,256]{1,0:T(8,128)(2,1)} %refs_0_.5) | copy-start | bytes 393220
  0.0 9.9 %collective-permute-start.8 = (bf16[256,256]{1,0:T(8,128)(2,1)}, bf16[256,256]{1,0:T(8,128)(2,1)S(1)}, u32[]{:S(2)}, u32[]{:S(2)}) collective-permute-start(bf16[256,256]{1,0:T(8,128)(2,1)} %refs_0_.5), channel_id=1, source_target_pairs={{0,3},{1,2},{2,1},{3,0},{4,7},{5,6},{6,5},{7,4},{8,11},{9,10},{10,... | collective-permute-start | bytes 393224 | tf_op jit(solution)/shard_map/ppermute | solution.py:138
  5.1 12.6 %collective-permute-start.7 = (bf16[256,256]{1,0:T(8,128)(2,1)}, bf16[256,256]{1,0:T(8,128)(2,1)S(1)}, u32[]{:S(2)}, u32[]{:S(2)}) collective-permute-start(bf16[256,256]{1,0:T(8,128)(2,1)} %refs_0_.5), channel_id=1, source_target_pairs={{0,1},{1,0},{2,3},{3,2},{4,5},{5,4},{6,7},{7,6},{8,9},{9,8},{10,11... | collective-permute-start | bytes 393224 | tf_op jit(solution)/shard_map/ppermute | solution.py:138
  5.1 10.7 %collective-permute-start.2 = (bf16[256,256]{1,0:T(8,128)(2,1)}, bf16[256,256]{1,0:T(8,128)(2,1)S(1)}, u32[]{:S(2)}, u32[]{:S(2)}) collective-permute-start(bf16[256,256]{1,0:T(8,128)(2,1)} %refs_0_.5), channel_id=1, source_target_pairs={{0,24},{4,28},{8,16},{12,20},{16,8},{20,12},{24,0},{28,4},{1,25},{... | collective-permute-start | bytes 393224 | tf_op jit(solution)/shard_map/ppermute | solution.py:138
  7.5 8.3 %collective-permute-start.1 = (bf16[256,256]{1,0:T(8,128)(2,1)}, bf16[256,256]{1,0:T(8,128)(2,1)S(1)}, u32[]{:S(2)}, u32[]{:S(2)}) collective-permute-start(bf16[256,256]{1,0:T(8,128)(2,1)} %refs_0_.5), channel_id=1, source_target_pairs={{0,16},{4,20},{8,24},{12,28},{16,0},{20,4},{24,8},{28,12},{1,17},{... | collective-permute-start | bytes 393224 | tf_op jit(solution)/shard_map/ppermute | solution.py:138
  8.0 7.8 %collective-permute-start = (bf16[256,256]{1,0:T(8,128)(2,1)}, bf16[256,256]{1,0:T(8,128)(2,1)S(1)}, u32[]{:S(2)}, u32[]{:S(2)}) collective-permute-start(bf16[256,256]{1,0:T(8,128)(2,1)} %refs_0_.5), channel_id=1, source_target_pairs={{0,8},{4,12},{8,0},{12,4},{16,24},{20,28},{24,16},{28,20},{1,9},{5... | collective-permute-start | bytes 393224 | tf_op jit(solution)/shard_map/ppermute | solution.py:138
  9.9 7.8 %collective-permute-start.9 = (bf16[256,256]{1,0:T(8,128)(2,1)S(1)}, bf16[256,256]{1,0:T(8,128)(2,1)S(1)}, u32[]{:S(2)}, u32[]{:S(2)}) collective-permute-start(bf16[256,256]{1,0:T(8,128)(2,1)S(1)} %collective-permute-done.8.refs_3_), channel_id=1, source_target_pairs={{0,1},{1,0},{2,3},{3,2},{4,5},{5,4},{6,7},{7,6},{8,9},{9,8},{10,11... | collective-permute-start | bytes 393224 | tf_op jit(solution)/shard_map/ppermute | solution.py:138
  12.1 1.9 %copy-start.1 = (bf16[96,128,128]{2,1,0:T(8,128)(2,1)S(1)}, bf16[96,128,128]{2,1,0:T(8,128)(2,1)}, u32[]{:S(2)}) copy-start(bf16[96,128,128]{2,1,0:T(8,128)(2,1)} %tiles_ref.1) | copy-start | bytes 9437188
  15.9 4.5 %collective-permute-start.3 = (bf16[1024,256]{1,0:T(8,128)(2,1)S(1)}, bf16[1024,256]{1,0:T(8,128)(2,1)S(1)}, u32[]{:S(2)}, u32[]{:S(2)}) collective-permute-start(bf16[1024,256]{1,0:T(8,128)(2,1)S(1)} %pad_maximum_fusion), channel_id=1, source_target_pairs={{0,4},{4,0},{8,12},{12,8},{16,20},{20,16},{24,28},{28,24},{1,5},{5... | collective-permute-start | bytes 1572872 | tf_op jit(solution)/shard_map/ppermute | solution.py:138
  18.4 5.0 %collective-permute-start.10 = (bf16[1024,256]{1,0:T(8,128)(2,1)S(1)}, bf16[1024,256]{1,0:T(8,128)(2,1)S(1)}, u32[]{:S(2)}, u32[]{:S(2)}) collective-permute-start(bf16[1024,256]{1,0:T(8,128)(2,1)S(1)} %shard_map.59), channel_id=1, source_target_pairs={{0,4},{4,0},{8,12},{12,8},{16,20},{20,16},{24,28},{28,24},{1,5},{5... | collective-permute-start | bytes 1572872 | tf_op jit(solution)/shard_map/ppermute | solution.py:138
  21.0 10.1 %collective-permute-start.4 = (bf16[256,256]{1,0:T(8,128)(2,1)S(1)}, bf16[256,256]{1,0:T(8,128)(2,1)S(1)}, u32[]{:S(2)}, u32[]{:S(2)}) collective-permute-start(bf16[256,256]{1,0:T(8,128)(2,1)S(1)} %get-tuple-element.12), channel_id=1, source_target_pairs={{0,1},{1,0},{2,3},{3,2},{4,5},{5,4},{6,7},{7,6},{8,9},{9,8},{10,11... | collective-permute-start | bytes 393224 | tf_op jit(solution)/shard_map/ppermute | solution.py:138
  21.4 7.9 %collective-permute-start.5 = (bf16[256,256]{1,0:T(8,128)(2,1)S(1)}, bf16[256,256]{1,0:T(8,128)(2,1)S(1)}, u32[]{:S(2)}, u32[]{:S(2)}) collective-permute-start(bf16[256,256]{1,0:T(8,128)(2,1)S(1)} %shard_map.57), channel_id=1, source_target_pairs={{0,1},{1,0},{2,3},{3,2},{4,5},{5,4},{6,7},{7,6},{8,9},{9,8},{10,11... | collective-permute-start | bytes 393224 | tf_op jit(solution)/shard_map/ppermute | solution.py:138
  23.7 7.5 %collective-permute-start.11 = (bf16[256,256]{1,0:T(8,128)(2,1)S(1)}, bf16[256,256]{1,0:T(8,128)(2,1)S(1)}, u32[]{:S(2)}, u32[]{:S(2)}) collective-permute-start(bf16[256,256]{1,0:T(8,128)(2,1)S(1)} %get-tuple-element.24), channel_id=1, source_target_pairs={{0,8},{4,12},{8,0},{12,4},{16,24},{20,28},{24,16},{28,20},{1,9},{5... | collective-permute-start | bytes 393224 | tf_op jit(solution)/shard_map/ppermute | solution.py:138
  25.2 7.1 %collective-permute-start.13 = (bf16[256,256]{1,0:T(8,128)(2,1)S(1)}, bf16[256,256]{1,0:T(8,128)(2,1)S(1)}, u32[]{:S(2)}, u32[]{:S(2)}) collective-permute-start(bf16[256,256]{1,0:T(8,128)(2,1)S(1)} %get-tuple-element.25), channel_id=1, source_target_pairs={{0,24},{4,28},{8,16},{12,20},{16,8},{20,12},{24,0},{28,4},{1,25},{... | collective-permute-start | bytes 393224 | tf_op jit(solution)/shard_map/ppermute | solution.py:138
  26.7 7.0 %collective-permute-start.12 = (bf16[256,256]{1,0:T(8,128)(2,1)S(1)}, bf16[256,256]{1,0:T(8,128)(2,1)S(1)}, u32[]{:S(2)}, u32[]{:S(2)}) collective-permute-start(bf16[256,256]{1,0:T(8,128)(2,1)S(1)} %get-tuple-element.26), channel_id=1, source_target_pairs={{0,16},{4,20},{8,24},{12,28},{16,0},{20,4},{24,8},{28,12},{1,17},{... | collective-permute-start | bytes 393224 | tf_op jit(solution)/shard_map/ppermute | solution.py:138
  29.3 6.8 %collective-permute-start.6 = (bf16[256,256]{1,0:T(8,128)(2,1)S(1)}, bf16[256,256]{1,0:T(8,128)(2,1)S(1)}, u32[]{:S(2)}, u32[]{:S(2)}) collective-permute-start(bf16[256,256]{1,0:T(8,128)(2,1)S(1)} %add_convert_fusion.1), channel_id=1, source_target_pairs={{0,3},{1,2},{2,1},{3,0},{4,7},{5,6},{6,5},{7,4},{8,11},{9,10},{10,... | collective-permute-start | bytes 393224 | tf_op jit(solution)/shard_map/ppermute | solution.py:138
  36.3 7.1 %collective-permute-start.22 = (bf16[256,256]{1,0:T(8,128)(2,1)S(1)}, bf16[256,256]{1,0:T(8,128)(2,1)S(1)}, u32[]{:S(2)}, u32[]{:S(2)}) collective-permute-start(bf16[256,256]{1,0:T(8,128)(2,1)S(1)} %fusion.2.refs_0_), channel_id=1, source_target_pairs={{0,3},{1,2},{2,1},{3,0},{4,7},{5,6},{6,5},{7,4},{8,11},{9,10},{10,... | collective-permute-start | bytes 393224 | tf_op jit(solution)/shard_map/ppermute | solution.py:138
  38.1 7.0 %collective-permute-start.16 = (bf16[256,256]{1,0:T(8,128)(2,1)S(1)}, bf16[256,256]{1,0:T(8,128)(2,1)S(1)}, u32[]{:S(2)}, u32[]{:S(2)}) collective-permute-start(bf16[256,256]{1,0:T(8,128)(2,1)S(1)} %fusion.2.refs_0_), channel_id=1, source_target_pairs={{0,24},{4,28},{8,16},{12,20},{16,8},{20,12},{24,0},{28,4},{1,25},{... | collective-permute-start | bytes 393224 | tf_op jit(solution)/shard_map/ppermute | solution.py:138
  40.6 5.6 %collective-permute-start.15 = (bf16[256,256]{1,0:T(8,128)(2,1)S(1)}, bf16[256,256]{1,0:T(8,128)(2,1)S(1)}, u32[]{:S(2)}, u32[]{:S(2)}) collective-permute-start(bf16[256,256]{1,0:T(8,128)(2,1)S(1)} %fusion.2.refs_0_), channel_id=1, source_target_pairs={{0,16},{4,20},{8,24},{12,28},{16,0},{20,4},{24,8},{28,12},{1,17},{... | collective-permute-start | bytes 393224 | tf_op jit(solution)/shard_map/ppermute | solution.py:138
  41.1 5.1 %collective-permute-start.14 = (bf16[256,256]{1,0:T(8,128)(2,1)S(1)}, bf16[256,256]{1,0:T(8,128)(2,1)S(1)}, u32[]{:S(2)}, u32[]{:S(2)}) collective-permute-start(bf16[256,256]{1,0:T(8,128)(2,1)S(1)} %fusion.2.refs_0_), channel_id=1, source_target_pairs={{0,8},{4,12},{8,0},{12,4},{16,24},{20,28},{24,16},{28,20},{1,9},{5... | collective-permute-start | bytes 393224 | tf_op jit(solution)/shard_map/ppermute | solution.py:138
  41.6 6.1 %collective-permute-start.21 = (bf16[256,256]{1,0:T(8,128)(2,1)S(1)}, bf16[256,256]{1,0:T(8,128)(2,1)S(1)}, u32[]{:S(2)}, u32[]{:S(2)}) collective-permute-start(bf16[256,256]{1,0:T(8,128)(2,1)S(1)} %fusion.2.refs_0_), channel_id=1, source_target_pairs={{0,1},{1,0},{2,3},{3,2},{4,5},{5,4},{6,7},{7,6},{8,9},{9,8},{10,11... | collective-permute-start | bytes 393224 | tf_op jit(solution)/shard_map/ppermute | solution.py:138
  43.5 5.9 %collective-permute-start.23 = (bf16[256,256]{1,0:T(8,128)(2,1)S(1)}, bf16[256,256]{1,0:T(8,128)(2,1)S(1)}, u32[]{:S(2)}, u32[]{:S(2)}) collective-permute-start(bf16[256,256]{1,0:T(8,128)(2,1)S(1)} %collective-permute-done.22.refs_3_), channel_id=1, source_target_pairs={{0,1},{1,0},{2,3},{3,2},{4,5},{5,4},{6,7},{7,6},{8,9},{9,8},{10,11... | collective-permute-start | bytes 393224 | tf_op jit(solution)/shard_map/ppermute | solution.py:138
  46.2 5.4 %collective-permute-start.17 = (bf16[1024,256]{1,0:T(8,128)(2,1)S(1)}, bf16[1024,256]{1,0:T(8,128)(2,1)S(1)}, u32[]{:S(2)}, u32[]{:S(2)}) collective-permute-start(bf16[1024,256]{1,0:T(8,128)(2,1)S(1)} %pad_maximum_fusion.1), channel_id=1, source_target_pairs={{0,4},{4,0},{8,12},{12,8},{16,20},{20,16},{24,28},{28,24},{1,5},{5... | collective-permute-start | bytes 1572872 | tf_op jit(solution)/shard_map/ppermute | solution.py:138
  50.1 4.6 %collective-permute-start.24 = (bf16[1024,256]{1,0:T(8,128)(2,1)S(1)}, bf16[1024,256]{1,0:T(8,128)(2,1)S(1)}, u32[]{:S(2)}, u32[]{:S(2)}) collective-permute-start(bf16[1024,256]{1,0:T(8,128)(2,1)S(1)} %shard_map.64), channel_id=1, source_target_pairs={{0,4},{4,0},{8,12},{12,8},{16,20},{20,16},{24,28},{28,24},{1,5},{5... | collective-permute-start | bytes 1572872 | tf_op jit(solution)/shard_map/ppermute | solution.py:138
  52.2 10.4 %collective-permute-start.18 = (bf16[256,256]{1,0:T(8,128)(2,1)S(1)}, bf16[256,256]{1,0:T(8,128)(2,1)S(1)}, u32[]{:S(2)}, u32[]{:S(2)}) collective-permute-start(bf16[256,256]{1,0:T(8,128)(2,1)S(1)} %get-tuple-element.15), channel_id=1, source_target_pairs={{0,1},{1,0},{2,3},{3,2},{4,5},{5,4},{6,7},{7,6},{8,9},{9,8},{10,11... | collective-permute-start | bytes 393224 | tf_op jit(solution)/shard_map/ppermute | solution.py:138
  54.0 7.0 %collective-permute-start.19 = (bf16[256,256]{1,0:T(8,128)(2,1)S(1)}, bf16[256,256]{1,0:T(8,128)(2,1)S(1)}, u32[]{:S(2)}, u32[]{:S(2)}) collective-permute-start(bf16[256,256]{1,0:T(8,128)(2,1)S(1)} %shard_map.62), channel_id=1, source_target_pairs={{0,1},{1,0},{2,3},{3,2},{4,5},{5,4},{6,7},{7,6},{8,9},{9,8},{10,11... | collective-permute-start | bytes 393224 | tf_op jit(solution)/shard_map/ppermute | solution.py:138
  54.8 7.8 %collective-permute-start.25 = (bf16[256,256]{1,0:T(8,128)(2,1)S(1)}, bf16[256,256]{1,0:T(8,128)(2,1)S(1)}, u32[]{:S(2)}, u32[]{:S(2)}) collective-permute-start(bf16[256,256]{1,0:T(8,128)(2,1)S(1)} %get-tuple-element.21), channel_id=1, source_target_pairs={{0,8},{4,12},{8,0},{12,4},{16,24},{20,28},{24,16},{28,20},{1,9},{5... | collective-permute-start | bytes 393224 | tf_op jit(solution)/shard_map/ppermute | solution.py:138
  56.4 7.7 %collective-permute-start.27 = (bf16[256,256]{1,0:T(8,128)(2,1)S(1)}, bf16[256,256]{1,0:T(8,128)(2,1)S(1)}, u32[]{:S(2)}, u32[]{:S(2)}) collective-permute-start(bf16[256,256]{1,0:T(8,128)(2,1)S(1)} %get-tuple-element.22), channel_id=1, source_target_pairs={{0,24},{4,28},{8,16},{12,20},{16,8},{20,12},{24,0},{28,4},{1,25},{... | collective-permute-start | bytes 393224 | tf_op jit(solution)/shard_map/ppermute | solution.py:138
  57.9 7.6 %collective-permute-start.26 = (bf16[256,256]{1,0:T(8,128)(2,1)S(1)}, bf16[256,256]{1,0:T(8,128)(2,1)S(1)}, u32[]{:S(2)}, u32[]{:S(2)}) collective-permute-start(bf16[256,256]{1,0:T(8,128)(2,1)S(1)} %get-tuple-element.23), channel_id=1, source_target_pairs={{0,16},{4,20},{8,24},{12,28},{16,0},{20,4},{24,8},{28,12},{1,17},{... | collective-permute-start | bytes 393224 | tf_op jit(solution)/shard_map/ppermute | solution.py:138
  61.0 7.0 %collective-permute-start.20 = (bf16[256,256]{1,0:T(8,128)(2,1)S(1)}, bf16[256,256]{1,0:T(8,128)(2,1)S(1)}, u32[]{:S(2)}, u32[]{:S(2)}) collective-permute-start(bf16[256,256]{1,0:T(8,128)(2,1)S(1)} %add_convert_fusion), channel_id=1, source_target_pairs={{0,3},{1,2},{2,1},{3,0},{4,7},{5,6},{6,5},{7,4},{8,11},{9,10},{10,... | collective-permute-start | bytes 393224 | tf_op jit(solution)/shard_map/ppermute | solution.py:138

commit v4 on v3

--- a/solution.py
+++ b/solution.py
@@ -149,7 +149,7 @@
 def apply_dense(panel, matrix, matrix_t):
     n_rows = lax.axis_size("row")
     n_cols = lax.axis_size("col")
-    rows, width = panel.shape
+    rows, _ = panel.shape
     half = n_rows // 2
     by_hops = sorted(range(1, n_cols), key=lambda j: (len(hops(j)), -j))
 
@@ -162,8 +162,8 @@
     (begun,) = product(matrix, near, [(0, n_cols * rows)], dtype=jnp.float32)
     upper = [None] * n_cols
     early = [j for j in by_hops if len(hops(j)) == len(hops(by_hops[-1]))]
-    late = [j for j in range(n_cols) if j not in early]
-    for units in (early, late):
+    late = [j for j in by_hops if j not in early]
+    for units in (early, late, [0]):
         pieces = [(j * rows, rows) for j in units]
         done = product(matrix, [far], pieces, half * rows, begun)
         for j, unit in zip(units, done):
@@ -174,12 +174,13 @@
         upper[j ^ last] = upper[j ^ last].astype(jnp.float32) + part.astype(jnp.float32)
     own = upper[0].astype(jnp.float32)
     (give,) = product(matrix_t, range_panels, [(half * rows, half * rows)])
-    (keep,) = product(matrix_t, range_panels, [(0, half * rows)])
-    paired = keep.astype(jnp.float32) + swap(give, "row", 1).astype(jnp.float32)
-    paired = paired.reshape(half, rows, width)
-    own += paired[0]
+    (keep,) = product(matrix_t, range_panels, [(rows, (half - 1) * rows)])
+    (mine,) = product(matrix_t, range_panels, [(0, rows)])
+    given = swap(give, "row", 1).astype(jnp.float32)
+    paired = keep.astype(jnp.float32) + given[rows:]
+    own += mine.astype(jnp.float32) + given[:rows]
     for k in range(1, half):
-        share = paired[k].astype(jnp.bfloat16)
+        share = paired[(k - 1) * rows : k * rows].astype(jnp.bfloat16)
         own += swap(share, "row", 2 * k).astype(jnp.float32)
     return own
 

time: 69 us -> 68.5 us (level)
  waiting for transfers between devices: 19.7 us -> 18.3 us
  Pallas kernels: 9.49 us -> 10.2 us
    ppermute x28, waiting for transfers between devices: 19.7 us -> 18.3 us  [swap(): lax.ppermute(x, axis, [(i, i ^ j) for i in range(lax.axis_size(axis))])]
    pallas_call x10 -> x14, Pallas kernels: 5.98 us -> 6.65 us  [product(): pl.pallas_call(functools.partial(product_kernel, len(panels), [first for...]
  transfers between devices with their start and end apart: 28 -> 28, of which waited for: 12 -> 12; matrix products, arithmetic and copies ran while one was open for 2% -> 2% of each run, Pallas kernels for 14% -> 15%
where the time goes in v4:
time: 68.5 us; the launch traced here: 68.3 us
  starting transfers between devices  34.6 us (51%)
  waiting for transfers between devices  18.3 us (27%)
  Pallas kernels  10.2 us (15%)
  other arithmetic  2.24 us (3%)
  local copies, waits for them, and re-layouts  1.95 us (3%)
  between operations  1 us (1%)
    ppermute x28, starting transfers between devices, swap(): lax.ppermute(x, axis, [(i, i ^ j) for i in range(lax.axis_size(axis))])  34.6 us
    ppermute x28, waiting for transfers between devices, swap(): lax.ppermute(x, axis, [(i, i ^ j) for i in range(lax.axis_size(axis))])  18.3 us
    pallas_call x14, Pallas kernels, product(): pl.pallas_call(functools.partial(product_kernel, len(panels), [first for...  6.65 us
    unnamed x4, local copies, waits for them, and re-layouts  1.89 us
    pallas_call x1, Pallas kernels, densify(): pl.pallas_call(densify_kernel, out_shape=jax.ShapeDtypeStruct((height, br...  1.81 us
    pallas_call x1, Pallas kernels, transpose(): pl.pallas_call(transpose_kernel, out_shape=jax.ShapeDtypeStruct((breadth,...  1.71 us
  transfers between devices with their start and end apart: 28, of which 12 were waited for; matrix products, arithmetic and copies ran while one was open for 2% of the time, Pallas kernels for 15%

profile of v4, /device:TPU:0, one launch (start us, length us, event | category | flops | bytes accessed | tf_op | source)
XLA Modules:
  0.0 68.3 jit_solution(2898671258747488820)
XLA Ops:
  0.0 5.1 %collective-permute-start.8 = (bf16[256,256]{1,0:T(8,128)(2,1)}, bf16[256,256]{1,0:T(8,128)(2,1)S(1)}, u32[]{:S(2)}, u32[]{:S(2)}) collective-permute-start(bf16[256,256]{1,0:T(8,128)(2,1)} %refs_0_.7), channel_id=1, source_target_pairs={{0,3},{1,2},{2,1},{3,0},{4,7},{5,6},{6,5},{7,4},{8,11},{9,10},{10,... | collective-permute-start | bytes 393224 | tf_op jit(solution)/shard_map/ppermute | solution.py:138
  5.1 2.4 %collective-permute-start.2 = (bf16[256,256]{1,0:T(8,128)(2,1)}, bf16[256,256]{1,0:T(8,128)(2,1)S(1)}, u32[]{:S(2)}, u32[]{:S(2)}) collective-permute-start(bf16[256,256]{1,0:T(8,128)(2,1)} %refs_0_.7), channel_id=1, source_target_pairs={{0,24},{4,28},{8,16},{12,20},{16,8},{20,12},{24,0},{28,4},{1,25},{... | collective-permute-start | bytes 393224 | tf_op jit(solution)/shard_map/ppermute | solution.py:138
  7.5 0.5 collective-permute-start.1
  8.0 0.5 collective-permute-start
  9.2 0.7 %compare_select_fusion = s32[96]{0:T(128)S(1)} fusion(s32[96]{0:T(128)} %param.8, s32[96]{0:T(128)} %param.7, s32[]{:T(128)S(6)} %axis_index.23, s32[]{:T(128)S(6)} %axis_index.25, s32[]{:T(128)S(6)} %mul.29, s32[]{:T(128)} %bitcast.1), kind=kLoop, calls=%fused_computation.34 | loop fusion | flops 7104 | bytes 1168 | tf_op jit(solution)/shard_map/jit(_where)/select_n | solution.py:35
  9.9 2.1 %collective-permute-start.9 = (bf16[256,256]{1,0:T(8,128)(2,1)S(1)}, bf16[256,256]{1,0:T(8,128)(2,1)S(1)}, u32[]{:S(2)}, u32[]{:S(2)}) collective-permute-start(bf16[256,256]{1,0:T(8,128)(2,1)S(1)} %collective-permute-done.8.refs_3_), channel_id=1, source_target_pairs={{0,1},{1,0},{2,3},{3,2},{4,5},{5,4},{6,7},{7,6},{8,9},{9,8},{10,11... | collective-permute-start | bytes 393224 | tf_op jit(solution)/shard_map/ppermute | solution.py:138
  12.0 0.1 select_reduce_fusion.table
  12.1 1.9 %copy-done.1 = bf16[96,128,128]{2,1,0:T(8,128)(2,1)S(1)} copy-done((bf16[96,128,128]{2,1,0:T(8,128)(2,1)S(1)}, bf16[96,128,128]{2,1,0:T(8,128)(2,1)}, u32[]{:S(2)}) %copy-start.1) | copy-done | bytes 3145752
  14.0 1.8 %densify.1.m_ref.a_ref = bf16[1024,2048]{1,0:T(8,128)(2,1)S(1)} custom-call(s32[128]{0:T(128)S(1)} %select_reduce_fusion.table, bf16[96,128,128]{2,1,0:T(8,128)(2,1)S(1)} %copy-done.1), custom_call_target="tpu_custom_call" | custom-call | bytes 7340032 | tf_op jit(solution)/shard_map/densify/pallas_call | solution.py:57
  15.8 1.7 %mirror.1.m_ref = bf16[2048,1024]{1,0:T(8,128)(2,1)S(1)} custom-call(bf16[1024,2048]{1,0:T(8,128)(2,1)S(1)} %densify.1.m_ref.a_ref), custom_call_target="tpu_custom_call" | custom-call | bytes 8388608 | tf_op jit(solution)/shard_map/mirror/pallas_call | solution.py:83
  17.6 0.1 collective-permute-start.3
  17.7 0.7 %shard_map.60 = bf16[1024,256]{1,0:T(8,128)(2,1)S(1)} custom-call(bf16[2048,1024]{1,0:T(8,128)(2,1)S(1)} %mirror.1.m_ref, bf16[256,256]{1,0:T(8,128)(2,1)S(1)} %copy-done, bf16[256,256]{1,0:T(8,128)(2,1)S(1)} %collective-permute-done.7.refs_1_, bf16[256,256]{1,0:T(8,128)(2,1)S(1)} %collective-permute-done.9.refs_2_, ...), custom_call_target="tpu_custom_call" | custom-call | flops 536870912 | bytes 3145728 | tf_op jit(solution)/shard_map/pallas_call | solution.py:121
  18.5 0.5 collective-permute-start.10
  19.0 0.7 %shard_map.55.refs_1_ = f32[1024,256]{1,0:T(8,128)S(1)} custom-call(bf16[1024,2048]{1,0:T(8,128)(2,1)S(1)} %densify.1.m_ref.a_ref, bf16[256,256]{1,0:T(8,128)(2,1)S(1)} %copy-done, bf16[256,256]{1,0:T(8,128)(2,1)S(1)} %collective-permute-done.refs_1_, bf16[256,256]{1,0:T(8,128)(2,1)S(1)} %collective-permute-done.1.refs_2_, ...), custom_call_target="tpu_custom_call" | custom-call | flops 536870912 | bytes 3145728 | tf_op jit(solution)/shard_map/pallas_call | solution.py:121
  19.7 0.6 shard_map.61
  20.3 0.4 shard_map.57
  20.7 0.1 collective-permute-start.4
  20.8 0.3 shard_map.58
  21.1 2.1 %collective-permute-start.5 = (bf16[256,256]{1,0:T(8,128)(2,1)S(1)}, bf16[256,256]{1,0:T(8,128)(2,1)S(1)}, u32[]{:S(2)}, u32[]{:S(2)}) collective-permute-start(bf16[256,256]{1,0:T(8,128)(2,1)S(1)} %shard_map.58), channel_id=1, source_target_pairs={{0,1},{1,0},{2,3},{3,2},{4,5},{5,4},{6,7},{7,6},{8,9},{9,8},{10,11... | collective-permute-start | bytes 393224 | tf_op jit(solution)/shard_map/ppermute | solution.py:138
  23.2 0.1 convert_element_type.97
  23.3 0.1 fusion.1
  23.4 1.6 %collective-permute-start.11 = (bf16[256,256]{1,0:T(8,128)(2,1)S(1)}, bf16[256,256]{1,0:T(8,128)(2,1)S(1)}, u32[]{:S(2)}, u32[]{:S(2)}) collective-permute-start(bf16[256,256]{1,0:T(8,128)(2,1)S(1)} %get-tuple-element.16), channel_id=1, source_target_pairs={{0,8},{4,12},{8,0},{12,4},{16,24},{20,28},{24,16},{28,20},{1,9},{5... | collective-permute-start | bytes 393224 | tf_op jit(solution)/shard_map/ppermute | solution.py:138
  25.0 1.5 %collective-permute-start.13 = (bf16[256,256]{1,0:T(8,128)(2,1)S(1)}, bf16[256,256]{1,0:T(8,128)(2,1)S(1)}, u32[]{:S(2)}, u32[]{:S(2)}) collective-permute-start(bf16[256,256]{1,0:T(8,128)(2,1)S(1)} %get-tuple-element.17), channel_id=1, source_target_pairs={{0,24},{4,28},{8,16},{12,20},{16,8},{20,12},{24,0},{28,4},{1,25},{... | collective-permute-start | bytes 393224 | tf_op jit(solution)/shard_map/ppermute | solution.py:138
  26.5 0.5 collective-permute-start.12
  27.0 2.1 %collective-permute-done.5 = bf16[256,256]{1,0:T(8,128)(2,1)S(1)} collective-permute-done((bf16[256,256]{1,0:T(8,128)(2,1)S(1)}, bf16[256,256]{1,0:T(8,128)(2,1)S(1)}, u32[]{:S(2)}, u32[]{:S(2)}) %collective-permute-start.5) | collective-permute-done | bytes 131104 | tf_op jit(solution)/shard_map/ppermute | solution.py:138
  29.1 1.8 %collective-permute-start.6 = (bf16[256,256]{1,0:T(8,128)(2,1)S(1)}, bf16[256,256]{1,0:T(8,128)(2,1)S(1)}, u32[]{:S(2)}, u32[]{:S(2)}) collective-permute-start(bf16[256,256]{1,0:T(8,128)(2,1)S(1)} %add_convert_fusion.1), channel_id=1, source_target_pairs={{0,3},{1,2},{2,1},{3,0},{4,7},{5,6},{6,5},{7,4},{8,11},{9,10},{10,... | collective-permute-start | bytes 393224 | tf_op jit(solution)/shard_map/ppermute | solution.py:138
  30.9 0.3 shard_map.59
  31.2 0.3 shard_map.56
  31.5 0.6 collective-permute-done.13
  32.1 1.4 %collective-permute-done.12 = bf16[256,256]{1,0:T(8,128)(2,1)S(1)} collective-permute-done((bf16[256,256]{1,0:T(8,128)(2,1)S(1)}, bf16[256,256]{1,0:T(8,128)(2,1)S(1)}, u32[]{:S(2)}, u32[]{:S(2)}) %collective-permute-start.12) | collective-permute-done | bytes 131104 | tf_op jit(solution)/shard_map/ppermute | solution.py:138
  33.5 2.4 %collective-permute-done.6 = bf16[256,256]{1,0:T(8,128)(2,1)S(1)} collective-permute-done((bf16[256,256]{1,0:T(8,128)(2,1)S(1)}, bf16[256,256]{1,0:T(8,128)(2,1)S(1)}, u32[]{:S(2)}, u32[]{:S(2)}) %collective-permute-start.6) | collective-permute-done | bytes 131104 | tf_op jit(solution)/shard_map/ppermute | solution.py:138
  35.9 0.2 fusion.4.refs_0_
  36.1 1.8 %collective-permute-start.22 = (bf16[256,256]{1,0:T(8,128)(2,1)S(1)}, bf16[256,256]{1,0:T(8,128)(2,1)S(1)}, u32[]{:S(2)}, u32[]{:S(2)}) collective-permute-start(bf16[256,256]{1,0:T(8,128)(2,1)S(1)} %fusion.4.refs_0_), channel_id=1, source_target_pairs={{0,3},{1,2},{2,1},{3,0},{4,7},{5,6},{6,5},{7,4},{8,11},{9,10},{10,... | collective-permute-start | bytes 393224 | tf_op jit(solution)/shard_map/ppermute | solution.py:138
  37.9 2.4 %collective-permute-start.16 = (bf16[256,256]{1,0:T(8,128)(2,1)S(1)}, bf16[256,256]{1,0:T(8,128)(2,1)S(1)}, u32[]{:S(2)}, u32[]{:S(2)}) collective-permute-start(bf16[256,256]{1,0:T(8,128)(2,1)S(1)} %fusion.4.refs_0_), channel_id=1, source_target_pairs={{0,24},{4,28},{8,16},{12,20},{16,8},{20,12},{24,0},{28,4},{1,25},{... | collective-permute-start | bytes 393224 | tf_op jit(solution)/shard_map/ppermute | solution.py:138
  40.3 0.5 collective-permute-start.15
  40.8 0.5 collective-permute-start.14
  41.4 1.5 %collective-permute-start.21 = (bf16[256,256]{1,0:T(8,128)(2,1)S(1)}, bf16[256,256]{1,0:T(8,128)(2,1)S(1)}, u32[]{:S(2)}, u32[]{:S(2)}) collective-permute-start(bf16[256,256]{1,0:T(8,128)(2,1)S(1)} %fusion.4.refs_0_), channel_id=1, source_target_pairs={{0,1},{1,0},{2,3},{3,2},{4,5},{5,4},{6,7},{7,6},{8,9},{9,8},{10,11... | collective-permute-start | bytes 393224 | tf_op jit(solution)/shard_map/ppermute | solution.py:138
  42.8 0.4 collective-permute-done.22.refs_3_
  43.2 1.6 %collective-permute-start.23 = (bf16[256,256]{1,0:T(8,128)(2,1)S(1)}, bf16[256,256]{1,0:T(8,128)(2,1)S(1)}, u32[]{:S(2)}, u32[]{:S(2)}) collective-permute-start(bf16[256,256]{1,0:T(8,128)(2,1)S(1)} %collective-permute-done.22.refs_3_), channel_id=1, source_target_pairs={{0,1},{1,0},{2,3},{3,2},{4,5},{5,4},{6,7},{7,6},{8,9},{9,8},{10,11... | collective-permute-start | bytes 393224 | tf_op jit(solution)/shard_map/ppermute | solution.py:138
  44.8 1.1 %collective-permute-done.15.refs_2_ = bf16[256,256]{1,0:T(8,128)(2,1)S(1)} collective-permute-done((bf16[256,256]{1,0:T(8,128)(2,1)S(1)}, bf16[256,256]{1,0:T(8,128)(2,1)S(1)}, u32[]{:S(2)}, u32[]{:S(2)}) %collective-permute-start.15) | collective-permute-done | bytes 131104 | tf_op jit(solution)/shard_map/ppermute | solution.py:138
  46.0 0.1 collective-permute-start.17
  46.0 1.4 %collective-permute-done.21.refs_1_ = bf16[256,256]{1,0:T(8,128)(2,1)S(1)} collective-permute-done((bf16[256,256]{1,0:T(8,128)(2,1)S(1)}, bf16[256,256]{1,0:T(8,128)(2,1)S(1)}, u32[]{:S(2)}, u32[]{:S(2)}) %collective-permute-start.21) | collective-permute-done | bytes 131104 | tf_op jit(solution)/shard_map/ppermute | solution.py:138
  47.5 1.7 %collective-permute-done.23.refs_2_ = bf16[256,256]{1,0:T(8,128)(2,1)S(1)} collective-permute-done((bf16[256,256]{1,0:T(8,128)(2,1)S(1)}, bf16[256,256]{1,0:T(8,128)(2,1)S(1)}, u32[]{:S(2)}, u32[]{:S(2)}) %collective-permute-start.23) | collective-permute-done | bytes 131104 | tf_op jit(solution)/shard_map/ppermute | solution.py:138
  49.1 0.7 %shard_map.67 = bf16[1024,256]{1,0:T(8,128)(2,1)S(1)} custom-call(bf16[2048,1024]{1,0:T(8,128)(2,1)S(1)} %mirror.1.m_ref, bf16[256,256]{1,0:T(8,128)(2,1)S(1)} %fusion.4.refs_0_, bf16[256,256]{1,0:T(8,128)(2,1)S(1)} %collective-permute-done.21.refs_1_, bf16[256,256]{1,0:T(8,128)(2,1)S(1)} %collective-permute-done.23.refs_2_, ...), custom_call_target="tpu_custom_call" | custom-call | flops 536870912 | bytes 3145728 | tf_op jit(solution)/shard_map/pallas_call | solution.py:121
  49.9 0.1 collective-permute-start.24
  49.9 0.7 %shard_map.62.refs_1_ = f32[1024,256]{1,0:T(8,128)S(1)} custom-call(bf16[1024,2048]{1,0:T(8,128)(2,1)S(1)} %densify.1.m_ref.a_ref, bf16[256,256]{1,0:T(8,128)(2,1)S(1)} %fusion.4.refs_0_, bf16[256,256]{1,0:T(8,128)(2,1)S(1)} %collective-permute-done.14.refs_1_, bf16[256,256]{1,0:T(8,128)(2,1)S(1)} %collective-permute-done.15.refs_2_, ...), custom_call_target="tpu_custom_call" | custom-call | flops 536870912 | bytes 3145728 | tf_op jit(solution)/shard_map/pallas_call | solution.py:121
  50.6 0.6 shard_map.68
  51.2 0.4 shard_map.64
  51.7 1.5 %collective-permute-start.18 = (bf16[256,256]{1,0:T(8,128)(2,1)S(1)}, bf16[256,256]{1,0:T(8,128)(2,1)S(1)}, u32[]{:S(2)}, u32[]{:S(2)}) collective-permute-start(bf16[256,256]{1,0:T(8,128)(2,1)S(1)} %get-tuple-element.11), channel_id=1, source_target_pairs={{0,1},{1,0},{2,3},{3,2},{4,5},{5,4},{6,7},{7,6},{8,9},{9,8},{10,11... | collective-permute-start | bytes 393224 | tf_op jit(solution)/shard_map/ppermute | solution.py:138
  53.2 0.3 shard_map.65
  53.5 0.6 collective-permute-start.19
  54.1 0.1 convert_element_type.111
  54.2 0.1 fusion
  54.4 1.6 %collective-permute-start.25 = (bf16[256,256]{1,0:T(8,128)(2,1)S(1)}, bf16[256,256]{1,0:T(8,128)(2,1)S(1)}, u32[]{:S(2)}, u32[]{:S(2)}) collective-permute-start(bf16[256,256]{1,0:T(8,128)(2,1)S(1)} %get-tuple-element.13), channel_id=1, source_target_pairs={{0,8},{4,12},{8,0},{12,4},{16,24},{20,28},{24,16},{28,20},{1,9},{5... | collective-permute-start | bytes 393224 | tf_op jit(solution)/shard_map/ppermute | solution.py:138
  55.9 1.5 %collective-permute-start.27 = (bf16[256,256]{1,0:T(8,128)(2,1)S(1)}, bf16[256,256]{1,0:T(8,128)(2,1)S(1)}, u32[]{:S(2)}, u32[]{:S(2)}) collective-permute-start(bf16[256,256]{1,0:T(8,128)(2,1)S(1)} %get-tuple-element.14), channel_id=1, source_target_pairs={{0,24},{4,28},{8,16},{12,20},{16,8},{20,12},{24,0},{28,4},{1,25},{... | collective-permute-start | bytes 393224 | tf_op jit(solution)/shard_map/ppermute | solution.py:138
  57.4 0.5 collective-permute-start.26
  57.9 2.5 %collective-permute-done.19 = bf16[256,256]{1,0:T(8,128)(2,1)S(1)} collective-permute-done((bf16[256,256]{1,0:T(8,128)(2,1)S(1)}, bf16[256,256]{1,0:T(8,128)(2,1)S(1)}, u32[]{:S(2)}, u32[]{:S(2)}) %collective-permute-start.19) | collective-permute-done | bytes 131104 | tf_op jit(solution)/shard_map/ppermute | solution.py:138
  60.5 1.6 %collective-permute-start.20 = (bf16[256,256]{1,0:T(8,128)(2,1)S(1)}, bf16[256,256]{1,0:T(8,128)(2,1)S(1)}, u32[]{:S(2)}, u32[]{:S(2)}) collective-permute-start(bf16[256,256]{1,0:T(8,128)(2,1)S(1)} %add_convert_fusion), channel_id=1, source_target_pairs={{0,3},{1,2},{2,1},{3,0},{4,7},{5,6},{6,5},{7,4},{8,11},{9,10},{10,... | collective-permute-start | bytes 393224 | tf_op jit(solution)/shard_map/ppermute | solution.py:138
  62.1 0.3 shard_map.66
  62.4 0.3 shard_map.63
  62.8 0.9 %collective-permute-done.27 = bf16[256,256]{1,0:T(8,128)(2,1)S(1)} collective-permute-done((bf16[256,256]{1,0:T(8,128)(2,1)S(1)}, bf16[256,256]{1,0:T(8,128)(2,1)S(1)}, u32[]{:S(2)}, u32[]{:S(2)}) %collective-permute-start.27) | collective-permute-done | bytes 131104 | tf_op jit(solution)/shard_map/ppermute | solution.py:138
  63.6 1.4 %collective-permute-done.26 = bf16[256,256]{1,0:T(8,128)(2,1)S(1)} collective-permute-done((bf16[256,256]{1,0:T(8,128)(2,1)S(1)}, bf16[256,256]{1,0:T(8,128)(2,1)S(1)}, u32[]{:S(2)}, u32[]{:S(2)}) %collective-permute-start.26) | collective-permute-done | bytes 131104 | tf_op jit(solution)/shard_map/ppermute | solution.py:138
  65.0 2.5 %collective-permute-done.20 = bf16[256,256]{1,0:T(8,128)(2,1)S(1)} collective-permute-done((bf16[256,256]{1,0:T(8,128)(2,1)S(1)}, bf16[256,256]{1,0:T(8,128)(2,1)S(1)}, u32[]{:S(2)}, u32[]{:S(2)}) %collective-permute-start.20) | collective-permute-done | bytes 131104 | tf_op jit(solution)/shard_map/ppermute | solution.py:138
  67.5 0.8 %fusion.5 = bf16[256,256]{1,0:T(8,128)(2,1)} fusion(bf16[256,256]{1,0:T(8,128)(2,1)S(1)} %copy-done, f32[1024,256]{1,0:T(8,128)S(1)} %convert_element_type.111, bf16[256,256]{1,0:T(8,128)(2,1)S(1)} %fusion.4.refs_0_, bf16[256,256]{1,0:T(8,128)(2,1)S(1)} %collective-permute-done.27, bf16[256,256]{1,0:T(8,128)(2,1)S(1)} %collective-permute-done.26, ...), kind=kLoop, calls=%fused_computation.11 | loop fusion | flops 1376256 | bytes 1572864 | tf_op jit(solution)/shard_map/convert_element_type | solution.py:276
  (26 shorter events, 0.3 us)
Async XLA Ops:
  0.0 9.9 %collective-permute-start.8 = (bf16[256,256]{1,0:T(8,128)(2,1)}, bf16[256,256]{1,0:T(8,128)(2,1)S(1)}, u32[]{:S(2)}, u32[]{:S(2)}) collective-permute-start(bf16[256,256]{1,0:T(8,128)(2,1)} %refs_0_.7), channel_id=1, source_target_pairs={{0,3},{1,2},{2,1},{3,0},{4,7},{5,6},{6,5},{7,4},{8,11},{9,10},{10,... | collective-permute-start | bytes 393224 | tf_op jit(solution)/shard_map/ppermute | solution.py:138
  5.1 12.6 %collective-permute-start.7 = (bf16[256,256]{1,0:T(8,128)(2,1)}, bf16[256,256]{1,0:T(8,128)(2,1)S(1)}, u32[]{:S(2)}, u32[]{:S(2)}) collective-permute-start(bf16[256,256]{1,0:T(8,128)(2,1)} %refs_0_.7), channel_id=1, source_target_pairs={{0,1},{1,0},{2,3},{3,2},{4,5},{5,4},{6,7},{7,6},{8,9},{9,8},{10,11... | collective-permute-start | bytes 393224 | tf_op jit(solution)/shard_map/ppermute | solution.py:138
  5.1 12.5 %collective-permute-start.2 = (bf16[256,256]{1,0:T(8,128)(2,1)}, bf16[256,256]{1,0:T(8,128)(2,1)S(1)}, u32[]{:S(2)}, u32[]{:S(2)}) collective-permute-start(bf16[256,256]{1,0:T(8,128)(2,1)} %refs_0_.7), channel_id=1, source_target_pairs={{0,24},{4,28},{8,16},{12,20},{16,8},{20,12},{24,0},{28,4},{1,25},{... | collective-permute-start | bytes 393224 | tf_op jit(solution)/shard_map/ppermute | solution.py:138
  7.5 10.0 %collective-permute-start.1 = (bf16[256,256]{1,0:T(8,128)(2,1)}, bf16[256,256]{1,0:T(8,128)(2,1)S(1)}, u32[]{:S(2)}, u32[]{:S(2)}) collective-permute-start(bf16[256,256]{1,0:T(8,128)(2,1)} %refs_0_.7), channel_id=1, source_target_pairs={{0,16},{4,20},{8,24},{12,28},{16,0},{20,4},{24,8},{28,12},{1,17},{... | collective-permute-start | bytes 393224 | tf_op jit(solution)/shard_map/ppermute | solution.py:138
  8.0 9.5 %collective-permute-start = (bf16[256,256]{1,0:T(8,128)(2,1)}, bf16[256,256]{1,0:T(8,128)(2,1)S(1)}, u32[]{:S(2)}, u32[]{:S(2)}) collective-permute-start(bf16[256,256]{1,0:T(8,128)(2,1)} %refs_0_.7), channel_id=1, source_target_pairs={{0,8},{4,12},{8,0},{12,4},{16,24},{20,28},{24,16},{28,20},{1,9},{5... | collective-permute-start | bytes 393224 | tf_op jit(solution)/shard_map/ppermute | solution.py:138
  9.9 7.8 %collective-permute-start.9 = (bf16[256,256]{1,0:T(8,128)(2,1)S(1)}, bf16[256,256]{1,0:T(8,128)(2,1)S(1)}, u32[]{:S(2)}, u32[]{:S(2)}) collective-permute-start(bf16[256,256]{1,0:T(8,128)(2,1)S(1)} %collective-permute-done.8.refs_3_), channel_id=1, source_target_pairs={{0,1},{1,0},{2,3},{3,2},{4,5},{5,4},{6,7},{7,6},{8,9},{9,8},{10,11... | collective-permute-start | bytes 393224 | tf_op jit(solution)/shard_map/ppermute | solution.py:138
  12.1 1.9 %copy-start.1 = (bf16[96,128,128]{2,1,0:T(8,128)(2,1)S(1)}, bf16[96,128,128]{2,1,0:T(8,128)(2,1)}, u32[]{:S(2)}) copy-start(bf16[96,128,128]{2,1,0:T(8,128)(2,1)} %tiles_ref.1) | copy-start | bytes 9437188
  15.8 1.8 %copy-start = (bf16[256,256]{1,0:T(8,128)(2,1)S(1)}, bf16[256,256]{1,0:T(8,128)(2,1)}, u32[]{:S(2)}) copy-start(bf16[256,256]{1,0:T(8,128)(2,1)} %refs_0_.7) | copy-start | bytes 393220
  17.6 2.7 %collective-permute-start.3 = (bf16[1024,256]{1,0:T(8,128)(2,1)S(1)}, bf16[1024,256]{1,0:T(8,128)(2,1)S(1)}, u32[]{:S(2)}, u32[]{:S(2)}) collective-permute-start(bf16[1024,256]{1,0:T(8,128)(2,1)S(1)} %pad_maximum_fusion), channel_id=1, source_target_pairs={{0,4},{4,0},{8,12},{12,8},{16,20},{20,16},{24,28},{28,24},{1,5},{5... | collective-permute-start | bytes 1572872 | tf_op jit(solution)/shard_map/ppermute | solution.py:138
  18.5 4.8 %collective-permute-start.10 = (bf16[1024,256]{1,0:T(8,128)(2,1)S(1)}, bf16[1024,256]{1,0:T(8,128)(2,1)S(1)}, u32[]{:S(2)}, u32[]{:S(2)}) collective-permute-start(bf16[1024,256]{1,0:T(8,128)(2,1)S(1)} %shard_map.60), channel_id=1, source_target_pairs={{0,4},{4,0},{8,12},{12,8},{16,20},{20,16},{24,28},{28,24},{1,5},{5... | collective-permute-start | bytes 1572872 | tf_op jit(solution)/shard_map/ppermute | solution.py:138
  20.7 10.8 %collective-permute-start.4 = (bf16[256,256]{1,0:T(8,128)(2,1)S(1)}, bf16[256,256]{1,0:T(8,128)(2,1)S(1)}, u32[]{:S(2)}, u32[]{:S(2)}) collective-permute-start(bf16[256,256]{1,0:T(8,128)(2,1)S(1)} %get-tuple-element.9), channel_id=1, source_target_pairs={{0,1},{1,0},{2,3},{3,2},{4,5},{5,4},{6,7},{7,6},{8,9},{9,8},{10,11... | collective-permute-start | bytes 393224 | tf_op jit(solution)/shard_map/ppermute | solution.py:138
  21.1 7.9 %collective-permute-start.5 = (bf16[256,256]{1,0:T(8,128)(2,1)S(1)}, bf16[256,256]{1,0:T(8,128)(2,1)S(1)}, u32[]{:S(2)}, u32[]{:S(2)}) collective-permute-start(bf16[256,256]{1,0:T(8,128)(2,1)S(1)} %shard_map.58), channel_id=1, source_target_pairs={{0,1},{1,0},{2,3},{3,2},{4,5},{5,4},{6,7},{7,6},{8,9},{9,8},{10,11... | collective-permute-start | bytes 393224 | tf_op jit(solution)/shard_map/ppermute | solution.py:138
  23.4 8.1 %collective-permute-start.11 = (bf16[256,256]{1,0:T(8,128)(2,1)S(1)}, bf16[256,256]{1,0:T(8,128)(2,1)S(1)}, u32[]{:S(2)}, u32[]{:S(2)}) collective-permute-start(bf16[256,256]{1,0:T(8,128)(2,1)S(1)} %get-tuple-element.16), channel_id=1, source_target_pairs={{0,8},{4,12},{8,0},{12,4},{16,24},{20,28},{24,16},{28,20},{1,9},{5... | collective-permute-start | bytes 393224 | tf_op jit(solution)/shard_map/ppermute | solution.py:138
  25.0 7.1 %collective-permute-start.13 = (bf16[256,256]{1,0:T(8,128)(2,1)S(1)}, bf16[256,256]{1,0:T(8,128)(2,1)S(1)}, u32[]{:S(2)}, u32[]{:S(2)}) collective-permute-start(bf16[256,256]{1,0:T(8,128)(2,1)S(1)} %get-tuple-element.17), channel_id=1, source_target_pairs={{0,24},{4,28},{8,16},{12,20},{16,8},{20,12},{24,0},{28,4},{1,25},{... | collective-permute-start | bytes 393224 | tf_op jit(solution)/shard_map/ppermute | solution.py:138
  26.5 7.1 %collective-permute-start.12 = (bf16[256,256]{1,0:T(8,128)(2,1)S(1)}, bf16[256,256]{1,0:T(8,128)(2,1)S(1)}, u32[]{:S(2)}, u32[]{:S(2)}) collective-permute-start(bf16[256,256]{1,0:T(8,128)(2,1)S(1)} %get-tuple-element.18), channel_id=1, source_target_pairs={{0,16},{4,20},{8,24},{12,28},{16,0},{20,4},{24,8},{28,12},{1,17},{... | collective-permute-start | bytes 393224 | tf_op jit(solution)/shard_map/ppermute | solution.py:138
  29.1 6.8 %collective-permute-start.6 = (bf16[256,256]{1,0:T(8,128)(2,1)S(1)}, bf16[256,256]{1,0:T(8,128)(2,1)S(1)}, u32[]{:S(2)}, u32[]{:S(2)}) collective-permute-start(bf16[256,256]{1,0:T(8,128)(2,1)S(1)} %add_convert_fusion.1), channel_id=1, source_target_pairs={{0,3},{1,2},{2,1},{3,0},{4,7},{5,6},{6,5},{7,4},{8,11},{9,10},{10,... | collective-permute-start | bytes 393224 | tf_op jit(solution)/shard_map/ppermute | solution.py:138
  36.1 7.1 %collective-permute-start.22 = (bf16[256,256]{1,0:T(8,128)(2,1)S(1)}, bf16[256,256]{1,0:T(8,128)(2,1)S(1)}, u32[]{:S(2)}, u32[]{:S(2)}) collective-permute-start(bf16[256,256]{1,0:T(8,128)(2,1)S(1)} %fusion.4.refs_0_), channel_id=1, source_target_pairs={{0,3},{1,2},{2,1},{3,0},{4,7},{5,6},{6,5},{7,4},{8,11},{9,10},{10,... | collective-permute-start | bytes 393224 | tf_op jit(solution)/shard_map/ppermute | solution.py:138
  37.9 7.0 %collective-permute-start.16 = (bf16[256,256]{1,0:T(8,128)(2,1)S(1)}, bf16[256,256]{1,0:T(8,128)(2,1)S(1)}, u32[]{:S(2)}, u32[]{:S(2)}) collective-permute-start(bf16[256,256]{1,0:T(8,128)(2,1)S(1)} %fusion.4.refs_0_), channel_id=1, source_target_pairs={{0,24},{4,28},{8,16},{12,20},{16,8},{20,12},{24,0},{28,4},{1,25},{... | collective-permute-start | bytes 393224 | tf_op jit(solution)/shard_map/ppermute | solution.py:138
  40.3 5.6 %collective-permute-start.15 = (bf16[256,256]{1,0:T(8,128)(2,1)S(1)}, bf16[256,256]{1,0:T(8,128)(2,1)S(1)}, u32[]{:S(2)}, u32[]{:S(2)}) collective-permute-start(bf16[256,256]{1,0:T(8,128)(2,1)S(1)} %fusion.4.refs_0_), channel_id=1, source_target_pairs={{0,16},{4,20},{8,24},{12,28},{16,0},{20,4},{24,8},{28,12},{1,17},{... | collective-permute-start | bytes 393224 | tf_op jit(solution)/shard_map/ppermute | solution.py:138
  40.8 5.1 %collective-permute-start.14 = (bf16[256,256]{1,0:T(8,128)(2,1)S(1)}, bf16[256,256]{1,0:T(8,128)(2,1)S(1)}, u32[]{:S(2)}, u32[]{:S(2)}) collective-permute-start(bf16[256,256]{1,0:T(8,128)(2,1)S(1)} %fusion.4.refs_0_), channel_id=1, source_target_pairs={{0,8},{4,12},{8,0},{12,4},{16,24},{20,28},{24,16},{28,20},{1,9},{5... | collective-permute-start | bytes 393224 | tf_op jit(solution)/shard_map/ppermute | solution.py:138
  41.4 6.1 %collective-permute-start.21 = (bf16[256,256]{1,0:T(8,128)(2,1)S(1)}, bf16[256,256]{1,0:T(8,128)(2,1)S(1)}, u32[]{:S(2)}, u32[]{:S(2)}) collective-permute-start(bf16[256,256]{1,0:T(8,128)(2,1)S(1)} %fusion.4.refs_0_), channel_id=1, source_target_pairs={{0,1},{1,0},{2,3},{3,2},{4,5},{5,4},{6,7},{7,6},{8,9},{9,8},{10,11... | collective-permute-start | bytes 393224 | tf_op jit(solution)/shard_map/ppermute | solution.py:138
  43.2 5.9 %collective-permute-start.23 = (bf16[256,256]{1,0:T(8,128)(2,1)S(1)}, bf16[256,256]{1,0:T(8,128)(2,1)S(1)}, u32[]{:S(2)}, u32[]{:S(2)}) collective-permute-start(bf16[256,256]{1,0:T(8,128)(2,1)S(1)} %collective-permute-done.22.refs_3_), channel_id=1, source_target_pairs={{0,1},{1,0},{2,3},{3,2},{4,5},{5,4},{6,7},{7,6},{8,9},{9,8},{10,11... | collective-permute-start | bytes 393224 | tf_op jit(solution)/shard_map/ppermute | solution.py:138
  46.0 5.3 %collective-permute-start.17 = (bf16[1024,256]{1,0:T(8,128)(2,1)S(1)}, bf16[1024,256]{1,0:T(8,128)(2,1)S(1)}, u32[]{:S(2)}, u32[]{:S(2)}) collective-permute-start(bf16[1024,256]{1,0:T(8,128)(2,1)S(1)} %pad_maximum_fusion.1), channel_id=1, source_target_pairs={{0,4},{4,0},{8,12},{12,8},{16,20},{20,16},{24,28},{28,24},{1,5},{5... | collective-permute-start | bytes 1572872 | tf_op jit(solution)/shard_map/ppermute | solution.py:138
  49.9 4.3 %collective-permute-start.24 = (bf16[1024,256]{1,0:T(8,128)(2,1)S(1)}, bf16[1024,256]{1,0:T(8,128)(2,1)S(1)}, u32[]{:S(2)}, u32[]{:S(2)}) collective-permute-start(bf16[1024,256]{1,0:T(8,128)(2,1)S(1)} %shard_map.67), channel_id=1, source_target_pairs={{0,4},{4,0},{8,12},{12,8},{16,20},{20,16},{24,28},{28,24},{1,5},{5... | collective-permute-start | bytes 1572872 | tf_op jit(solution)/shard_map/ppermute | solution.py:138
  51.7 11.1 %collective-permute-start.18 = (bf16[256,256]{1,0:T(8,128)(2,1)S(1)}, bf16[256,256]{1,0:T(8,128)(2,1)S(1)}, u32[]{:S(2)}, u32[]{:S(2)}) collective-permute-start(bf16[256,256]{1,0:T(8,128)(2,1)S(1)} %get-tuple-element.11), channel_id=1, source_target_pairs={{0,1},{1,0},{2,3},{3,2},{4,5},{5,4},{6,7},{7,6},{8,9},{9,8},{10,11... | collective-permute-start | bytes 393224 | tf_op jit(solution)/shard_map/ppermute | solution.py:138
  53.5 6.9 %collective-permute-start.19 = (bf16[256,256]{1,0:T(8,128)(2,1)S(1)}, bf16[256,256]{1,0:T(8,128)(2,1)S(1)}, u32[]{:S(2)}, u32[]{:S(2)}) collective-permute-start(bf16[256,256]{1,0:T(8,128)(2,1)S(1)} %shard_map.65), channel_id=1, source_target_pairs={{0,1},{1,0},{2,3},{3,2},{4,5},{5,4},{6,7},{7,6},{8,9},{9,8},{10,11... | collective-permute-start | bytes 393224 | tf_op jit(solution)/shard_map/ppermute | solution.py:138
  54.4 8.4 %collective-permute-start.25 = (bf16[256,256]{1,0:T(8,128)(2,1)S(1)}, bf16[256,256]{1,0:T(8,128)(2,1)S(1)}, u32[]{:S(2)}, u32[]{:S(2)}) collective-permute-start(bf16[256,256]{1,0:T(8,128)(2,1)S(1)} %get-tuple-element.13), channel_id=1, source_target_pairs={{0,8},{4,12},{8,0},{12,4},{16,24},{20,28},{24,16},{28,20},{1,9},{5... | collective-permute-start | bytes 393224 | tf_op jit(solution)/shard_map/ppermute | solution.py:138
  55.9 7.7 %collective-permute-start.27 = (bf16[256,256]{1,0:T(8,128)(2,1)S(1)}, bf16[256,256]{1,0:T(8,128)(2,1)S(1)}, u32[]{:S(2)}, u32[]{:S(2)}) collective-permute-start(bf16[256,256]{1,0:T(8,128)(2,1)S(1)} %get-tuple-element.14), channel_id=1, source_target_pairs={{0,24},{4,28},{8,16},{12,20},{16,8},{20,12},{24,0},{28,4},{1,25},{... | collective-permute-start | bytes 393224 | tf_op jit(solution)/shard_map/ppermute | solution.py:138
  57.4 7.6 %collective-permute-start.26 = (bf16[256,256]{1,0:T(8,128)(2,1)S(1)}, bf16[256,256]{1,0:T(8,128)(2,1)S(1)}, u32[]{:S(2)}, u32[]{:S(2)}) collective-permute-start(bf16[256,256]{1,0:T(8,128)(2,1)S(1)} %get-tuple-element.15), channel_id=1, source_target_pairs={{0,16},{4,20},{8,24},{12,28},{16,0},{20,4},{24,8},{28,12},{1,17},{... | collective-permute-start | bytes 393224 | tf_op jit(solution)/shard_map/ppermute | solution.py:138
  60.5 7.0 %collective-permute-start.20 = (bf16[256,256]{1,0:T(8,128)(2,1)S(1)}, bf16[256,256]{1,0:T(8,128)(2,1)S(1)}, u32[]{:S(2)}, u32[]{:S(2)}) collective-permute-start(bf16[256,256]{1,0:T(8,128)(2,1)S(1)} %add_convert_fusion), channel_id=1, source_target_pairs={{0,3},{1,2},{2,1},{3,0},{4,7},{5,6},{6,5},{7,4},{8,11},{9,10},{10,... | collective-permute-start | bytes 393224 | tf_op jit(solution)/shard_map/ppermute | solution.py:138
